TPU v7x, 512 devices: a whole 4x4x16 slice. The times are simulated.
512 devices in a mesh: wide: 64 (over x, z), narrow: 8 (over y, core).
Axes of the slice: x: 4, y: 4, z: 16, core: 2. Of those that a mesh axis runs over, the one named last changes fastest.
Arguments:
- frames: bfloat16 [16384, 1024], P('wide'), may hold values from -6 to 6
- expert_ids: int32 [16384, 2], P('wide'), may hold values from 0 to 63, all different within a row; in each aligned block of 256 rows (0 to 255, 256 to 511, ...) at most 16 rows name the same one
- gate_values: float32 [16384, 2], P('wide'), may hold values from 0.1 to 1
- w_gate: bfloat16 [64, 1024, 4096], P('wide', None, 'narrow'), may hold values from -0.1875 to 0.1875
- w_up: bfloat16 [64, 1024, 4096], P('wide', None, 'narrow'), may hold values from -0.1875 to 0.1875
- w_down: bfloat16 [64, 4096, 1024], P('wide', 'narrow'), may hold values from -0.09375 to 0.09375
- norm_gain: float32 [1024], replicated, may hold values from 0.1 to 1.9
- norm_bias: float32 [1024], replicated, may hold values from -2 to 2
- point_in: bfloat16 [1024, 2, 1024], P(None, None, 'narrow'), may hold values from -0.1875 to 0.1875
- depth_kernel: bfloat16 [31, 1024], P(None, 'narrow'), may hold values from -1 to 1
- point_out: bfloat16 [1024, 1024], P('narrow'), may hold values from -0.1875 to 0.1875
Outputs:
- block_out: bfloat16 [16384, 1024], P(('wide', 'narrow'))
Inputs may be any that keep to these rules, and one draw needn't show every extreme that they name: `expert_ids`: each frame names 2 different experts; in each aligned block of 256 frames no expert is named by more than 16 frames, and every expert is named somewhere.
All inputs are finite; a program needn't handle non-finite values.
Results may differ from a plain program's by a relative error of at most 0.015.
Values may be sent and summed in bfloat16 or wider, within the bound.
No kernel may reach another device: no remote copies, remote signals or barrier semaphores. Data moves between devices by JAX's collectives and lax.ppermute only.
A program may use at most 64 MiB of HBM per device.

v0:
```python
import jax
import jax.numpy as jnp
from jax import lax
from jax.sharding import PartitionSpec as P


def padded_2(cells, sides, width):
    for axis, dim in sides:
        count = lax.axis_size(axis)
        ends = count - 1
        head = lax.slice_in_dim(cells, 0, width, axis=dim)
        tail = lax.slice_in_dim(cells, cells.shape[dim] - width, cells.shape[dim], axis=dim)
        cells = jnp.concatenate(
            [
                lax.ppermute(tail, axis, [(i, (i + 1) % count) for i in range(ends)]),
                cells,
                lax.ppermute(head, axis, [((i + 1) % count, i) for i in range(ends)]),
            ],
            axis=dim,
        )
    return cells


def shards(
    frames,
    expert_ids,
    gate_values,
    w_gate,
    w_up,
    w_down,
    norm_gain,
    norm_bias,
    point_in,
    depth_kernel,
    point_out,
):
    frame_count = frames.shape[0]
    model_width = frames.shape[1]
    top_count = expert_ids.shape[1]
    wide_count = lax.axis_size("wide")
    narrow_count = lax.axis_size("narrow")
    local_experts = w_gate.shape[0]
    expert_count = local_experts * wide_count
    capacity = 2 * top_count * frame_count // expert_count
    flat_ids = expert_ids.reshape(-1)
    one_hot = (flat_ids[:, None] == jnp.arange(expert_count, dtype=jnp.int32)[None, :]).astype(
        jnp.int32
    )
    running = jnp.cumsum(one_hot, axis=0)
    slot_index = jnp.sum((running - 1) * one_hot, axis=1)
    target_row = flat_ids * capacity + slot_index
    repeated = jnp.repeat(frames, top_count, axis=0)
    outgoing = (
        jnp.zeros((expert_count * capacity, model_width), jnp.bfloat16).at[target_row].set(repeated)
    )
    outgoing = outgoing.reshape(expert_count, capacity, model_width)
    arrived = lax.all_to_all(outgoing, "wide", split_axis=0, concat_axis=0, tiled=True)
    arrived = arrived.reshape(wide_count, local_experts, capacity, model_width)
    gate_h = jnp.einsum("sjcd,jdf->sjcf", arrived, w_gate, preferred_element_type=jnp.float32)
    up_h = jnp.einsum("sjcd,jdf->sjcf", arrived, w_up, preferred_element_type=jnp.float32)
    hidden = (jax.nn.silu(gate_h) * up_h).astype(jnp.bfloat16)
    partial_value = jnp.einsum(
        "sjcf,jfd->sjcd", hidden, w_down, preferred_element_type=jnp.float32
    ).astype(jnp.bfloat16)
    partial_value = partial_value.reshape(wide_count * local_experts, capacity, model_width)
    returned = lax.all_to_all(partial_value, "wide", split_axis=0, concat_axis=0, tiled=True)
    picked = jnp.take(returned.reshape(expert_count * capacity, model_width), target_row, axis=0)
    picked = picked.reshape(frame_count, top_count, model_width)
    mixture = jnp.sum(gate_values[:, :, None] * picked.astype(jnp.float32), axis=1)
    moe_sum = lax.psum(mixture.astype(jnp.bfloat16), "narrow").astype(jnp.float32)
    residual = frames.astype(jnp.float32) + moe_sum
    row_mean = jnp.mean(residual, axis=1, keepdims=True)
    centered = residual - row_mean
    row_var = jnp.mean(centered * centered, axis=1, keepdims=True)
    normed = (
        centered / jnp.sqrt(row_var + 1e-05) * norm_gain[None, :] + norm_bias[None, :]
    ).astype(jnp.bfloat16)
    channels = point_in.shape[2]
    projected = jnp.dot(
        normed, point_in.reshape(model_width, 2 * channels), preferred_element_type=jnp.float32
    )
    value_half = projected[:, :channels]
    gate_half = projected[:, channels:]
    glu_out = (value_half * jax.nn.sigmoid(gate_half)).astype(jnp.bfloat16)
    taps_count = depth_kernel.shape[0]
    half_width = (taps_count - 1) // 2
    padded = padded_2(glu_out, (("wide", 0),), half_width)
    depthwise = jnp.zeros((frame_count, channels), jnp.float32)
    for tap_index in range(taps_count):
        depthwise = (
            depthwise
            + padded[tap_index : tap_index + frame_count].astype(jnp.float32)
            * depth_kernel[tap_index].astype(jnp.float32)[None, :]
        )
    activated = (depthwise * jax.nn.sigmoid(depthwise)).astype(jnp.bfloat16)
    share_rows = frame_count // narrow_count
    summed = lax.psum_scatter(
        jnp.dot(activated, point_out, preferred_element_type=jnp.float32).astype(jnp.bfloat16),
        "narrow",
        scatter_dimension=0,
        tiled=True,
    ).astype(jnp.float32)
    own_rows = lax.dynamic_slice_in_dim(
        residual, lax.axis_index("narrow") * share_rows, share_rows, 0
    )
    return (own_rows + summed).astype(jnp.bfloat16)


def solution(mesh):
    return jax.shard_map(
        shards,
        mesh=mesh,
        in_specs=(
            P("wide", None),
            P("wide", None),
            P("wide", None),
            P("wide", None, "narrow"),
            P("wide", None, "narrow"),
            P("wide", "narrow", None),
            P(),
            P(),
            P(None, None, "narrow"),
            P(None, "narrow"),
            P("narrow", None),
        ),
        out_specs=P(("wide", "narrow"), None),
        check_vma=False,
    )
```

profile of v0, /device:TPU:6, one launch (start us, length us, event | category | flops | bytes accessed | tf_op | source)
XLA Modules:
  0.0 387.4 jit_solution(1770547481121458651)
XLA Ops:
  6.5 0.0 copy-start
  6.5 0.9 copy.20
  7.4 0.1 eq.26
  7.6 0.1 reshape.113
  7.7 0.7 broadcast_multiply_fusion
  8.4 1.2 reduce-window.6
  9.6 0.2 slice_reduce_fusion
  9.9 0.1 copy.25
  10.1 0.1 mul.464
  10.2 1.6 broadcast_in_dim.16
  11.8 1.2 reshape.166
  13.0 0.1 fusion.17
  13.2 3.9 %scatter_custom_fusion = bf16[1024,1024]{1,0:T(8,128)(2,1)S(1)} fusion(s32[512]{0:T(512)S(1)} %bitcast.172, bf16[512,1024]{1,0:T(8,128)(2,1)} %reshape.166, bf16[]{:T(256)} %constant.21.clone.1), kind=kCustom, calls=%fused_computation.22 | custom fusion | bytes 2097664 | tf_op jit(solution)/shard_map/scatter | solution.py:54
  17.1 0.0 copy-start.7
  17.1 116.3 %all_to_all.10 = bf16[64,16,1024]{2,1,0:T(8,128)(2,1)S(1)} all-to-all(bf16[64,16,1024]{2,1,0:T(8,128)(2,1)S(1)} %bitcast.170), channel_id=1, replica_groups=mesh['wide'=64,'narrow'=8] {'wide'}, dimensions={0} | all-to-all | bytes 4194304 | tf_op jit(solution)/shard_map/all_to_all | solution.py:57
  133.4 1.3 copy-done.2
  134.8 0.0 copy-done.7
  134.8 2.5 fusion.8
  137.3 6.0 %convolution_convert_fusion = bf16[64,16,1024]{2,1,0:T(8,128)(2,1)} fusion(bf16[64,16,1024]{2,1,0:T(8,128)(2,1)} %copy-done.2, f32[64,16,512]{2,1,0:T(8,128)} %fusion.8, bf16[1,512,1024]{2,1,0:T(8,128)(2,1)S(1)} %copy-done, bf16[1,1024,512]{2,1,0:T(8,128)(2,1)S(1)} %copy-done.8), kind=kOutput, calls=%fused_computation.11 | convolution fusion | flops 2151677952 | bytes 8388608 | tf_op jit(solution)/shard_map/sjcf,jfd->sjcd/dot_general | solution.py:62
  143.3 8.1 %all-to-all-start.1 = ((bf16[64,16,1024]{2,1,0:T(8,128)(2,1)}), bf16[64,16,1024]{2,1,0:T(8,128)(2,1)S(1)}, u32[]{:S(2)}, u32[]{:S(2)}) async-start(bf16[64,16,1024]{2,1,0:T(8,128)(2,1)} %convolution_convert_fusion), calls=%async_computation.1 | async-start | bytes 4194304 | tf_op jit(solution)/shard_map/all_to_all | solution.py:66
  151.4 0.2 all-reduce.2.cloned.1.call-start
  151.7 0.1 reduce_sum.41
  151.8 0.1 copy.23
  151.9 0.2 copy.24
  152.1 0.0 copy-done.6
  152.1 0.1 copy.19
  152.3 96.2 %all-to-all-done.1 = bf16[64,16,1024]{2,1,0:T(8,128)(2,1)S(1)} async-done(((bf16[64,16,1024]{2,1,0:T(8,128)(2,1)}), bf16[64,16,1024]{2,1,0:T(8,128)(2,1)S(1)}, u32[]{:S(2)}, u32[]{:S(2)}) %all-to-all-start.1) | async-done | bytes 2097184 | tf_op jit(solution)/shard_map/all_to_all | solution.py:66
  248.5 2.8 gather_fusion
  251.3 1.5 gather.7
  252.8 5.0 %multiply_reduce_fusion = bf16[256,1024]{1,0:T(8,128)(2,1)} fusion(bf16[256,2,1024]{2,1,0:T(2,128)(2,1)S(1)} %gather.7, pred[256,2]{1,0:T(8,128)(4,1)S(1)} %copy.24, f32[256,2]{1,0:T(8,128)S(1)} %copy.19), kind=kLoop, calls=%fused_computation.9 | loop fusion | flops 1835008 | bytes 1575424 | tf_op jit(solution)/shard_map/reduce_sum | solution.py:69
  257.8 0.0 all-reduce.2.cloned.1.call-update
  257.9 0.0 reduce-scatter.2.cloned.1.call-start
  258.0 70.5 %all-reduce.2.cloned.1.call-done = bf16[256,1024]{1,0:T(8,128)(2,1)} async-done(((bf16[256,1024]{1,0:T(8,128)(2,1)}), bf16[256,1024]{1,0:T(8,128)(2,1)}) %all-reduce.2.cloned.1.call-update) | async-done | bytes 524304 | tf_op jit(solution)/shard_map/psum | solution.py:70
  328.4 1.3 convert_add_fusion
  329.8 0.3 multiply_reduce_fusion.1
  330.1 0.0 copy-done.9
  330.1 0.0 copy-done.11
  330.1 0.0 copy-done.12
  330.1 0.0 copy-start.10
  330.1 0.5 fusion.13
  330.6 3.5 collective-permute-start
  334.1 4.7 %collective-permute-start.1 = (bf16[15,128]{1,0:T(8,128)(2,1)S(1)}, bf16[15,128]{1,0:T(8,128)(2,1)S(1)}, u32[]{:S(2)}, u32[]{:S(2)}) collective-permute-start(bf16[15,128]{1,0:T(8,128)(2,1)S(1)} %get-tuple-element.8), channel_id=1, source_target_pairs={{8,0},{16,8},{24,16},{32,24},{40,32},{48,40},{56,48},{64,56},{72,6... | collective-permute-start | bytes 11528 | tf_op jit(solution)/shard_map/ppermute | solution.py:17
  338.8 0.0 collective-permute-done
  338.9 1.3 collective-permute-done.1
  340.1 1.5 convolution_convert_fusion.1
  341.6 0.0 reduce-scatter.2.cloned.1.call-update
  341.7 37.4 %reduce-scatter.2.cloned.1.call-done = bf16[32,1024]{1,0:T(8,128)(2,1)} async-done(((bf16[256,1024]{1,0:T(8,128)(2,1)}), bf16[32,1024]{1,0:T(8,128)(2,1)}) %reduce-scatter.2.cloned.1.call-update) | async-done | bytes 65552 | tf_op jit(solution)/shard_map/reduce_scatter | solution.py:97
  379.1 1.5 add_convert_fusion.2
  (29 shorter events, 0.2 us)
Async XLA Ops:
  6.5 130.8 %copy-start = (bf16[1,512,1024]{2,1,0:T(8,128)(2,1)S(1)}, bf16[1,512,1024]{2,1,0:T(8,128)(2,1)}, u32[]{:S(2)}) copy-start(bf16[1,512,1024]{2,1,0:T(8,128)(2,1)} %param.16) | copy-start | bytes 3145732
  17.1 117.7 %copy-start.7 = (bf16[1,1024,512]{2,1,0:T(8,128)(2,1)S(1)}, bf16[1,1024,512]{2,1,0:T(8,128)(2,1)}, u32[]{:S(2)}) copy-start(bf16[1,1024,512]{2,1,0:T(8,128)(2,1)} %param.14) | copy-start | bytes 3145732
  133.4 1.4 copy-start.2
  134.8 2.5 copy-start.8
  143.3 8.6 %copy-start.5 = (s32[256,2]{0,1:T(2,128)S(1)}, s32[256,2]{0,1:T(2,128)}, u32[]{:S(2)}) copy-start(s32[256,2]{0,1:T(2,128)} %param.12) | copy-start | bytes 6148
  143.3 8.8 %copy-start.6 = (f32[256,2]{0,1:T(2,128)S(1)}, f32[256,2]{0,1:T(2,128)}, u32[]{:S(2)}) copy-start(f32[256,2]{0,1:T(2,128)} %param.13) | copy-start | bytes 6148
  143.3 105.2 %all-to-all-start.1 = ((bf16[64,16,1024]{2,1,0:T(8,128)(2,1)}), bf16[64,16,1024]{2,1,0:T(8,128)(2,1)S(1)}, u32[]{:S(2)}, u32[]{:S(2)}) async-start(bf16[64,16,1024]{2,1,0:T(8,128)(2,1)} %convolution_convert_fusion), calls=%async_computation.1 | async-start | bytes 4194304 | tf_op jit(solution)/shard_map/all_to_all | solution.py:66
  151.4 177.0 %all-reduce.2.cloned.1.call-start = ((), (), s32[]{:S(2)}) async-start(), calls=%async_computation.3 | async-start | bytes 1048576 | tf_op jit(solution)/shard_map/psum | solution.py:70
  251.3 6.7 %copy-start.4 = (bf16[31,128]{1,0:T(8,128)(2,1)S(1)}, bf16[31,128]{1,0:T(8,128)(2,1)}, u32[]{:S(2)}) copy-start(bf16[31,128]{1,0:T(8,128)(2,1)} %param.20) | copy-start | bytes 23812
  251.3 77.2 %copy-start.1 = (bf16[256,1024]{1,0:T(8,128)(2,1)S(1)}, bf16[256,1024]{1,0:T(8,128)(2,1)}, u32[]{:S(2)}) copy-start(bf16[256,1024]{1,0:T(8,128)(2,1)} %param.11) | copy-start | bytes 1572868
  257.8 72.2 %copy-start.9 = (bf16[1024,2,128]{2,1,0:T(2,128)(2,1)S(1)}, bf16[1024,2,128]{2,1,0:T(2,128)(2,1)}, u32[]{:S(2)}) copy-start(bf16[1024,2,128]{2,1,0:T(2,128)(2,1)} %param.19) | copy-start | bytes 1572868
  257.8 72.2 %copy-start.11 = (f32[1024]{0:T(1024)S(1)}, f32[1024]{0:T(1024)}, u32[]{:S(2)}) copy-start(f32[1024]{0:T(1024)} %param.18) | copy-start | bytes 12292
  257.8 72.2 %copy-start.12 = (f32[1024]{0:T(1024)S(1)}, f32[1024]{0:T(1024)}, u32[]{:S(2)}) copy-start(f32[1024]{0:T(1024)} %param.17) | copy-start | bytes 12292
  257.9 121.2 %reduce-scatter.2.cloned.1.call-start = ((), (), s32[]{:S(2)}) async-start(), calls=%async_computation.4 | async-start | bytes 589824 | tf_op jit(solution)/shard_map/reduce_scatter | solution.py:97
  328.4 1.3 copy-start.3
  330.1 10.0 %copy-start.10 = (bf16[128,1024]{1,0:T(8,128)(2,1)S(1)}, bf16[128,1024]{1,0:T(8,128)(2,1)}, u32[]{:S(2)}) copy-start(bf16[128,1024]{1,0:T(8,128)(2,1)} %param.21) | copy-start | bytes 786436
  330.6 8.2 %collective-permute-start = (bf16[15,128]{1,0:T(8,128)(2,1)S(1)}, bf16[15,128]{1,0:T(8,128)(2,1)S(1)}, u32[]{:S(2)}, u32[]{:S(2)}) collective-permute-start(bf16[15,128]{1,0:T(8,128)(2,1)S(1)} %get-tuple-element.7), channel_id=1, source_target_pairs={{0,8},{8,16},{16,24},{24,32},{32,40},{40,48},{48,56},{56,64},{64,7... | collective-permute-start | bytes 11528 | tf_op jit(solution)/shard_map/ppermute | solution.py:15
  334.1 6.0 %collective-permute-start.1 = (bf16[15,128]{1,0:T(8,128)(2,1)S(1)}, bf16[15,128]{1,0:T(8,128)(2,1)S(1)}, u32[]{:S(2)}, u32[]{:S(2)}) collective-permute-start(bf16[15,128]{1,0:T(8,128)(2,1)S(1)} %get-tuple-element.8), channel_id=1, source_target_pairs={{8,0},{16,8},{24,16},{32,24},{40,32},{48,40},{56,48},{64,56},{72,6... | collective-permute-start | bytes 11528 | tf_op jit(solution)/shard_map/ppermute | solution.py:17
Sparse Core Ops, SparseCore 0:
  258.0 70.3 all-reduce.1
  341.8 37.2 reduce-scatter.1
where the time goes:
time: 388 us; the launch traced here: 387 us
  waiting for transfers between devices  205 us (53%)
  blocking collectives  116 us (30%)
  starting transfers between devices  16.6 us (4%)
  local copies, waits for them, and re-layouts  14.7 us (4%)
  between operations  13.6 us (4%)
  matrix products  10.5 us (3%)
  other arithmetic  10.3 us (3%)
    all_to_all x1, blocking collectives, shards(): lax.all_to_all(outgoing, 'wide', split_axis=0, concat_axis=0, tiled=True)  116 us
    all_to_all x1, waiting for transfers between devices, shards(): lax.all_to_all(partial_value, 'wide', split_axis=0, concat_axis=0, tiled=...  96.2 us
    psum x1, waiting for transfers between devices, shards(): lax.psum(mixture.astype(jnp.bfloat16), 'narrow').astype(jnp.float32)  70.5 us
    reduce_scatter x1, waiting for transfers between devices, shards(): lax.psum_scatter(jnp.dot(activated, point_out, preferred_element_type=jnp...  37.4 us
    all_to_all x1, starting transfers between devices, shards(): lax.all_to_all(partial_value, 'wide', split_axis=0, concat_axis=0, tiled=...  8.15 us
  transfers between devices with their start and end apart: 5, of which 4 were waited for; matrix products, arithmetic and copies ran while one was open for 0% of the time, Pallas kernels for 0%

commit v1 on v0

v1 whole, which is shorter than its diff:
```python
import jax
import jax.numpy as jnp
from jax import lax
from jax.experimental import pallas as pl
from jax.experimental.pallas import tpu as pltpu
from jax.sharding import Mesh
from jax.sharding import PartitionSpec as P

WIDE = ("x", "z")
NARROW = ("y", "c")
EVERY = ("x", "z", "y", "c")
VMEM_BYTES = 48 << 20


def in_vmem(count):
    return [pl.BlockSpec(memory_space=pltpu.VMEM)] * count


def mm(a, b):
    return jnp.dot(a, b, preferred_element_type=jnp.float32)


def route_kernel(experts, slots, pos_ref, ids_ref, frames_ref, out_ref, target_ref):
    count = ids_ref.shape[1]
    first = pos_ref[1] * slots
    expert = lax.broadcasted_iota(jnp.int32, (experts, count), 0)
    named = [jnp.where(expert == ids_ref[k : k + 1, :], 1.0, 0.0) for k in range(2)]
    before = lax.broadcasted_iota(jnp.int32, (count, count), 0) < lax.broadcasted_iota(
        jnp.int32, (count, count), 1
    )
    rank = mm(
        jnp.concatenate(named, axis=0).astype(jnp.bfloat16),
        jnp.where(before, 1.0, 0.0).astype(jnp.bfloat16),
    )
    held = jnp.sum(named[0], axis=1, keepdims=True)
    place = [
        jnp.sum(named[0] * rank[:experts], axis=0, keepdims=True),
        jnp.sum(named[1] * (rank[experts:] + held), axis=0, keepdims=True),
    ]
    row = lax.broadcasted_iota(jnp.int32, (experts * slots, count), 0)
    chosen = None
    for k in range(2):
        local = place[k].astype(jnp.int32) - first
        target = jnp.where(
            (local >= 0) & (local < slots), ids_ref[k : k + 1, :] * slots + local, -1
        )
        target_ref[k : k + 1, :] = target.astype(jnp.float32)
        hit = row == target
        chosen = hit if chosen is None else chosen | hit
    out_ref[...] = mm(
        jnp.where(chosen, 1.0, 0.0).astype(jnp.bfloat16), frames_ref[...]
    ).astype(jnp.bfloat16)


def expert_kernel(x_ref, *refs):
    out_ref = refs[-1]
    chunks, _, width = x_ref.shape
    total = None
    for pair in range(2):
        gate_ref, up_ref, down_ref = refs[3 * pair : 3 * pair + 3]
        gate = up = None
        for q in range(chunks):
            rows = slice(q * width, (q + 1) * width)
            g, u = mm(x_ref[q], gate_ref[rows, :]), mm(x_ref[q], up_ref[rows, :])
            gate, up = (g, u) if gate is None else (gate + g, up + u)
        hidden = (gate * jax.nn.sigmoid(gate) * up).astype(jnp.bfloat16)
        part = mm(hidden, down_ref[...])
        total = part if total is None else total + part
    for q in range(chunks):
        out_ref[q] = total[:, q * width : (q + 1) * width].astype(jnp.bfloat16)


def combine_kernel(target_ref, gate_ref, rows_ref, out_ref):
    count = target_ref.shape[1]
    table = jnp.concatenate(
        [target_ref[...], gate_ref[...], jnp.zeros((4, count), jnp.float32)], axis=0
    ).T
    slot = lax.broadcasted_iota(jnp.int32, (count, rows_ref.shape[0]), 1)
    total = None
    for k in range(2):
        hit = slot == table[:, k : k + 1].astype(jnp.int32)
        picked = mm(jnp.where(hit, 1.0, 0.0).astype(jnp.bfloat16), rows_ref[...])
        picked = picked * table[:, 2 + k : 3 + k]
        total = picked if total is None else total + picked
    out_ref[...] = total.astype(jnp.bfloat16)


def norm_kernel(pos_ref, frames_ref, parts_ref, gain_ref, bias_ref, in_ref, res_ref, lo_ref, hi_ref):
    width = frames_ref.shape[1]
    moe = jnp.concatenate(
        [
            parts_ref[2 * q].astype(jnp.float32) + parts_ref[2 * q + 1].astype(jnp.float32)
            for q in range(parts_ref.shape[0] // 2)
        ],
        axis=1,
    )
    residual = frames_ref[...].astype(jnp.float32) + moe
    res_ref[...] = residual
    centered = residual - jnp.mean(residual, axis=1, keepdims=True)
    variance = jnp.mean(centered * centered, axis=1, keepdims=True)
    normed = (centered / jnp.sqrt(variance + 1e-05) * gain_ref[...] + bias_ref[...]).astype(
        jnp.bfloat16
    )
    channels = in_ref.shape[2]
    half = lo_ref.shape[0]
    for n in range(in_ref.shape[0]):
        both = jnp.concatenate([in_ref[n, :width, :], in_ref[n, width : 2 * width, :]], axis=1)
        projected = mm(normed, both)
        glu = projected[:, :channels] * jax.nn.sigmoid(projected[:, channels:])
        glu = glu.astype(jnp.bfloat16)
        cols = slice(n * channels, (n + 1) * channels)
        lo_ref[:, cols] = glu[:half]
        hi_ref[:, cols] = glu[half:]


def conv_kernel(taps, left_ref, lo_ref, hi_ref, right_ref, in_ref, point_ref, res_ref, out_ref, pad_ref):
    half = lo_ref.shape[0]
    count = 2 * half
    for i, ref in enumerate((left_ref, lo_ref, hi_ref, right_ref)):
        pad_ref[i * half : (i + 1) * half, :] = ref[...].astype(jnp.float32)
    base = half - (taps - 1) // 2
    channels = in_ref.shape[2]
    at = 2 * lo_ref.shape[1]
    acts = []
    for n in range(in_ref.shape[0]):
        cols = slice(n * channels, (n + 1) * channels)
        kernel = in_ref[n, at : at + taps + 1, :].astype(jnp.float32)
        total = None
        for j in range(taps):
            term = pad_ref[base + j : base + j + count, cols] * kernel[j : j + 1, :]
            total = term if total is None else total + term
        acts.append((total * jax.nn.sigmoid(total)).astype(jnp.bfloat16))
    act = jnp.concatenate(acts, axis=1)
    out_ref[...] = (res_ref[...] + mm(act, point_ref[...])).astype(jnp.bfloat16)


def shards(
    frames,
    expert_ids,
    gate_values,
    w_gate,
    w_up,
    w_down,
    norm_gain,
    norm_bias,
    point_in,
    depth_kernel,
    point_out,
):
    count, width = frames.shape
    wide = lax.axis_size("x") * lax.axis_size("z")
    quarters, cores = lax.axis_size("y"), lax.axis_size("c")
    narrow = quarters * cores
    experts = w_gate.shape[0] * wide
    slots = 2 * expert_ids.shape[1] * count // experts // cores
    share = width // quarters
    own = count // narrow
    taps, channels = depth_kernel.shape
    params = pltpu.CompilerParams(vmem_limit_bytes=VMEM_BYTES)

    y, c = lax.axis_index("y"), lax.axis_index("c")
    pos = jnp.stack([y, c, y * cores + c]).astype(jnp.int32)

    packed = jnp.concatenate(
        [
            point_in.transpose(1, 0, 2).reshape(2 * width, channels),
            depth_kernel,
            jnp.zeros((1, channels), jnp.bfloat16),
        ],
        axis=0,
    )
    packed = lax.all_gather(packed, NARROW, axis=0)
    point = lax.all_gather(point_out, NARROW, axis=0, tiled=True)

    mine = [w_gate[0], w_up[0], w_down[0]]
    swap = [(i, cores - 1 - i) for i in range(cores)]
    theirs = [lax.ppermute(w, "c", swap) for w in mine]

    rows = experts * slots
    outgoing, target = pl.pallas_call(
        lambda *refs: route_kernel(experts, slots, *refs),
        grid_spec=pltpu.PrefetchScalarGridSpec(
            num_scalar_prefetch=1,
            grid=(1,),
            in_specs=[
                pl.BlockSpec((2, count), lambda i, pos: (0, 0)),
                pl.BlockSpec((count, share), lambda i, pos: (0, pos[0])),
            ],
            out_specs=[
                pl.BlockSpec((rows, share), lambda i, pos: (0, 0)),
                pl.BlockSpec((2, count), lambda i, pos: (0, 0)),
            ],
        ),
        out_shape=[
            jax.ShapeDtypeStruct((rows, share), jnp.bfloat16),
            jax.ShapeDtypeStruct((2, count), jnp.float32),
        ],
        compiler_params=params,
        name="route",
    )(pos, expert_ids.T, frames)

    arrived = lax.all_to_all(
        outgoing.reshape(experts, slots, share), WIDE, split_axis=0, concat_axis=0, tiled=True
    ).reshape(1, rows, share)
    x = lax.all_to_all(
        jnp.broadcast_to(arrived, (quarters, rows, share)), "y", split_axis=0, concat_axis=0, tiled=True
    )
    partial = pl.pallas_call(
        expert_kernel,
        in_specs=in_vmem(7),
        out_specs=pl.BlockSpec(memory_space=pltpu.VMEM),
        out_shape=jax.ShapeDtypeStruct((quarters, rows, share), jnp.bfloat16),
        compiler_params=params,
        name="experts",
    )(x, *mine, *theirs)
    partial = lax.all_to_all(partial, "y", split_axis=0, concat_axis=0, tiled=True)
    summed = jnp.sum(partial.astype(jnp.float32), axis=0).astype(jnp.bfloat16)
    returned = lax.all_to_all(
        summed.reshape(experts, slots, share), WIDE, split_axis=0, concat_axis=0, tiled=True
    ).reshape(rows, share)
    mixed = pl.pallas_call(
        combine_kernel,
        in_specs=in_vmem(3),
        out_specs=pl.BlockSpec(memory_space=pltpu.VMEM),
        out_shape=jax.ShapeDtypeStruct((count, share), jnp.bfloat16),
        compiler_params=params,
        name="combine",
    )(target, gate_values.T, returned)
    parts = lax.all_to_all(
        mixed.reshape(narrow, own, share), NARROW, split_axis=0, concat_axis=0, tiled=True
    )

    half = own // 2
    whole = lambda *shape: pl.BlockSpec(shape, lambda i, pos: (0,) * len(shape))
    residual, lo, hi = pl.pallas_call(
        norm_kernel,
        grid_spec=pltpu.PrefetchScalarGridSpec(
            num_scalar_prefetch=1,
            grid=(1,),
            in_specs=[
                pl.BlockSpec((own, width), lambda i, pos: (pos[2], 0)),
                whole(narrow, own, share),
                whole(1, width),
                whole(1, width),
                whole(*packed.shape),
            ],
            out_specs=[whole(own, width), whole(half, width), whole(half, width)],
        ),
        out_shape=[
            jax.ShapeDtypeStruct((own, width), jnp.float32),
            jax.ShapeDtypeStruct((half, width), jnp.bfloat16),
            jax.ShapeDtypeStruct((half, width), jnp.bfloat16),
        ],
        compiler_params=params,
        name="norm_glu",
    )(pos, frames, parts, norm_gain[None, :], norm_bias[None, :], packed)

    ends = wide * narrow - 1
    left = lax.ppermute(hi, EVERY, [(i, i + 1) for i in range(ends)])
    right = lax.ppermute(lo, EVERY, [(i + 1, i) for i in range(ends)])
    return pl.pallas_call(
        lambda *refs: conv_kernel(taps, *refs),
        in_specs=in_vmem(7),
        out_specs=pl.BlockSpec(memory_space=pltpu.VMEM),
        out_shape=jax.ShapeDtypeStruct((own, width), jnp.bfloat16),
        scratch_shapes=[pltpu.VMEM((4 * half, width), jnp.float32)],
        compiler_params=params,
        name="conv",
    )(left, lo, hi, right, packed, point, residual)


def solution(mesh):
    chips = Mesh(mesh.devices.reshape(4, 16, 4, 2), EVERY)
    return jax.shard_map(
        shards,
        mesh=chips,
        in_specs=(
            P(WIDE, None),
            P(WIDE, None),
            P(WIDE, None),
            P(WIDE, None, NARROW),
            P(WIDE, None, NARROW),
            P(WIDE, NARROW, None),
            P(),
            P(),
            P(None, None, NARROW),
            P(None, NARROW),
            P(NARROW, None),
        ),
        out_specs=P(EVERY, None),
        check_vma=False,
    )
```

time: 388 us -> 170 us (0.44)
  waiting for transfers between devices: 205 us -> 28.9 us
  blocking collectives: 116 us -> 61.3 us
  starting transfers between devices: 16.6 us -> 39.5 us
  Pallas kernels: 0 us -> 13 us
  matrix products: 10.5 us -> 0 us
  other arithmetic: 10.3 us -> 0.33 us
    psum x1 -> x0, waiting for transfers between devices: 70.5 us -> none  [shards(): lax.psum(mixture.astype(jnp.bfloat16), 'narrow').astype(jnp.float32)]
    all_to_all x1 -> x2, waiting for transfers between devices: 96.2 us -> 26.6 us  [the longest x1 13.8 us: shards(): lax.all_to_all(outgoing.reshape(experts, slots, share), WIDE, split_axis=...]
    all_to_all x1 -> x3, blocking collectives: 116 us -> 61.3 us  [the longest x1 32.4 us: shards(): lax.all_to_all(summed.reshape(experts, slots, share), WIDE, split_axis=0,...]
    reduce_scatter x1 -> x0, waiting for transfers between devices: 37.4 us -> none  [shards(): lax.psum_scatter(jnp.dot(activated, point_out, preferred_element_type=jnp...]
    all_to_all x1 -> x2, starting transfers between devices: 8.15 us -> 23.4 us  [the longest x1 18.8 us: shards(): lax.all_to_all(outgoing.reshape(experts, slots, share), WIDE, split_axis=...]
    pallas_call x0 -> x5, Pallas kernels: none -> 13 us  [the longest x1 5.37 us: shards(): pl.pallas_call(expert_kernel, in_specs=in_vmem(7), out_specs=pl.BlockSpec...]
    dot_general x4 -> x0, matrix products: 10.5 us -> none  [the longest x1 5.97 us: shards(): jnp.einsum('sjcf,jfd->sjcd', hidden, w_down, preferred_element_type=jnp.f...]
    ppermute x2 -> x5, starting transfers between devices: 8.16 us -> 16 us  [the longest x1 7.86 us: shards(): right = lax.ppermute(lo, EVERY, [(i + 1, i) for i in range(ends)])]
  transfers between devices with their start and end apart: 5 -> 9, of which waited for: 4 -> 3; matrix products, arithmetic and copies ran while one was open for 0% -> 1% of each run, Pallas kernels for 0% -> 5%
where the time goes in v1:
time: 170 us
  blocking collectives  61.3 us (36%)
  starting transfers between devices  39.5 us (23%)
  waiting for transfers between devices  28.9 us (17%)
  between operations  13.6 us (8%)
  local copies, waits for them, and re-layouts  13.1 us (8%)
  Pallas kernels  13 us (8%)
    all_to_all x1, blocking collectives, shards(): lax.all_to_all(summed.reshape(experts, slots, share), WIDE, split_axis=0,...  32.4 us
    all_to_all x1, blocking collectives, shards(): lax.all_to_all(partial, 'y', split_axis=0, concat_axis=0, tiled=True)  20.4 us
    all_to_all x1, starting transfers between devices, shards(): lax.all_to_all(outgoing.reshape(experts, slots, share), WIDE, split_axis=...  18.8 us
    all_to_all x1, waiting for transfers between devices, shards(): lax.all_to_all(outgoing.reshape(experts, slots, share), WIDE, split_axis=...  13.8 us
    all_to_all x1, waiting for transfers between devices, shards(): lax.all_to_all(jnp.broadcast_to(arrived, (quarters, rows, share)), 'y', s...  12.8 us
    all_to_all x1, blocking collectives, shards(): lax.all_to_all(mixed.reshape(narrow, own, share), NARROW, split_axis=0, c...  8.52 us
    unnamed x23, local copies, waits for them, and re-layouts  8.03 us
    ppermute x1, starting transfers between devices, shards(): right = lax.ppermute(lo, EVERY, [(i + 1, i) for i in range(ends)])  7.86 us
  transfers between devices with their start and end apart: 9, of which 3 were waited for; matrix products, arithmetic and copies ran while one was open for 1% of the time, Pallas kernels for 5%

profile of v1, /device:TPU:6, one launch (start us, length us, event | category | flops | bytes accessed | tf_op | source)
XLA Modules:
  0.0 169.7 jit_solution(3914294624602721686)
XLA Ops:
  6.5 0.0 copy-start.5
  6.5 0.0 all-gather.6.cloned.1.call-start
  6.5 1.3 copy.12
  7.8 4.0 %concatenate.3 = bf16[2080,128]{1,0:T(8,128)(2,1)} concatenate(bf16[2048,128]{1,0:T(8,128)(2,1)S(1)} %bitcast.33, bf16[31,128]{1,0:T(8,128)(2,1)} %param.20, bf16[1,128]{1,0:T(2,128)(2,1)S(1)} %broadcast_in_dim.20), dimensions={0} | concatenate | bytes 1064960 | tf_op jit(solution)/shard_map/concatenate | solution.py:164
  11.8 0.0 all-gather.6.cloned.1.call-update
  11.8 0.1 pad_add_fusion.refs_0_.pos_ref
  11.9 1.0 copy-done.2
  12.9 0.7 copy-done.9
  13.6 1.7 route.1
  15.3 18.8 %all-to-all-start = ((bf16[64,8,256]{2,1,0:T(8,128)(2,1)}), bf16[64,8,256]{2,1,0:T(8,128)(2,1)S(1)}, u32[]{:S(2)}, u32[]{:S(2)}) async-start(bf16[64,8,256]{2,1,0:T(8,128)(2,1)} %bitcast.5), calls=%async_computation | async-start | bytes 524288 | tf_op jit(solution)/shard_map/all_to_all | solution.py:202
  34.1 0.0 all-gather.4.cloned.1.call-start
  34.2 0.7 all-gather.4.cloned.1.call-update
  34.9 1.9 %collective-permute-start = (bf16[1024,512]{1,0:T(8,128)(2,1)}, bf16[1024,512]{1,0:T(8,128)(2,1)}, u32[]{:S(2)}, u32[]{:S(2)}) collective-permute-start(bf16[1024,512]{1,0:T(8,128)(2,1)} %bitcast.22), channel_id=1, source_target_pairs={{0,1},{1,0},{2,3},{3,2},{4,5},{5,4},{6,7},{7,6},{8,9},{9,8},{10,11... | collective-permute-start | bytes 3145736 | tf_op jit(solution)/shard_map/ppermute | solution.py:177
  36.8 2.4 %collective-permute-start.1 = (bf16[1024,512]{1,0:T(8,128)(2,1)}, bf16[1024,512]{1,0:T(8,128)(2,1)}, u32[]{:S(2)}, u32[]{:S(2)}) collective-permute-start(bf16[1024,512]{1,0:T(8,128)(2,1)} %bitcast.24), channel_id=1, source_target_pairs={{0,1},{1,0},{2,3},{3,2},{4,5},{5,4},{6,7},{7,6},{8,9},{9,8},{10,11... | collective-permute-start | bytes 3145736 | tf_op jit(solution)/shard_map/ppermute | solution.py:177
  39.2 1.9 %collective-permute-start.2 = (bf16[512,1024]{1,0:T(8,128)(2,1)}, bf16[512,1024]{1,0:T(8,128)(2,1)}, u32[]{:S(2)}, u32[]{:S(2)}) collective-permute-start(bf16[512,1024]{1,0:T(8,128)(2,1)} %bitcast.26), channel_id=1, source_target_pairs={{0,1},{1,0},{2,3},{3,2},{4,5},{5,4},{6,7},{7,6},{8,9},{9,8},{10,11... | collective-permute-start | bytes 3145736 | tf_op jit(solution)/shard_map/ppermute | solution.py:177
  41.1 13.8 %all-to-all-done = bf16[64,8,256]{2,1,0:T(8,128)(2,1)S(1)} async-done(((bf16[64,8,256]{2,1,0:T(8,128)(2,1)}), bf16[64,8,256]{2,1,0:T(8,128)(2,1)S(1)}, u32[]{:S(2)}, u32[]{:S(2)}) %all-to-all-start) | async-done | bytes 262176 | tf_op jit(solution)/shard_map/all_to_all | solution.py:202
  54.9 1.1 broadcast_in_dim.17
  56.0 4.6 %all-to-all-start.1 = ((bf16[4,512,256]{2,1,0:T(8,128)(2,1)}), bf16[4,512,256]{2,1,0:T(8,128)(2,1)S(1)}, u32[]{:S(2)}, u32[]{:S(2)}) async-start(bf16[4,512,256]{2,1,0:T(8,128)(2,1)} %broadcast_in_dim.17), calls=%async_computation.1 | async-start | bytes 2097152 | tf_op jit(solution)/shard_map/all_to_all | solution.py:205
  60.6 0.0 collective-permute-done.refs_3_
  60.6 0.0 collective-permute-done.1.refs_4_
  60.6 0.0 collective-permute-done.2.refs_5_
  60.6 12.8 %all-to-all-done.1.x_ref = bf16[4,512,256]{2,1,0:T(8,128)(2,1)S(1)} async-done(((bf16[4,512,256]{2,1,0:T(8,128)(2,1)}), bf16[4,512,256]{2,1,0:T(8,128)(2,1)S(1)}, u32[]{:S(2)}, u32[]{:S(2)}) %all-to-all-start.1) | async-done | bytes 1048608 | tf_op jit(solution)/shard_map/all_to_all | solution.py:205
  73.4 0.0 copy-done.4
  73.4 0.0 copy-done.5
  73.4 1.2 copy-done.6
  74.7 5.4 %experts.1 = bf16[4,512,256]{2,1,0:T(8,128)(2,1)S(1)} custom-call(bf16[4,512,256]{2,1,0:T(8,128)(2,1)S(1)} %all-to-all-done.1.x_ref, bf16[1024,512]{1,0:T(8,128)(2,1)S(1)} %bitcast.23, bf16[1024,512]{1,0:T(8,128)(2,1)S(1)} %bitcast.25, bf16[512,1024]{1,0:T(8,128)(2,1)S(1)} %bitcast.27, bf16[1024,512]{1,0:T(8,128)(2,1)} %collective-permute-done.refs_3_, ...), custom_call_target="tpu_custom_call" | custom-call | tf_op jit(solution)/shard_map/experts/pallas_call | solution.py:208
  80.1 0.0 copy-start.3
  80.1 0.0 copy-start.7
  80.1 0.0 copy-start.8
  80.1 20.4 %all_to_all.25 = bf16[4,512,256]{2,1,0:T(8,128)(2,1)S(1)} all-to-all(bf16[4,512,256]{2,1,0:T(8,128)(2,1)S(1)} %experts.1), channel_id=1, replica_groups=mesh['x'=4,'z'=16,'y'=4,'c'=2] {'y'}, dimensions={0} | all-to-all | bytes 2097152 | tf_op jit(solution)/shard_map/all_to_all | solution.py:216
  100.5 0.3 reduce_sum.12
  100.7 32.4 %all_to_all.26 = bf16[64,8,256]{2,1,0:T(8,128)(2,1)S(1)} all-to-all(bf16[64,8,256]{2,1,0:T(8,128)(2,1)S(1)} %bitcast.35), channel_id=1, replica_groups=mesh['x'=4,'z'=16,'y'=4,'c'=2] {'x','z'}, dimensions={0} | all-to-all | bytes 524288 | tf_op jit(solution)/shard_map/all_to_all | solution.py:218
  133.2 0.0 copy-done.10
  133.2 0.5 combine.1
  133.7 8.5 %all_to_all.27.parts_ref = bf16[8,32,256]{2,1,0:T(8,128)(2,1)S(1)} all-to-all(bf16[8,32,256]{2,1,0:T(8,128)(2,1)S(1)} %bitcast.28), channel_id=1, replica_groups=mesh['x'=4,'z'=16,'y'=4,'c'=2] {'y','c'}, dimensions={0} | all-to-all | bytes 262144 | tf_op jit(solution)/shard_map/all_to_all | solution.py:229
  142.2 0.0 copy-done.3
  142.2 0.0 copy-done.7
  142.2 0.0 copy-done.8
  142.2 0.0 copy-start
  142.2 2.2 %copy-done = bf16[16640,128]{1,0:T(8,128)(2,1)S(1)} copy-done((bf16[16640,128]{1,0:T(8,128)(2,1)S(1)}, bf16[16640,128]{1,0:T(8,128)(2,1)}, u32[]{:S(2)}) %copy-start) | copy-done | bytes 4259864
  144.4 1.5 norm_glu.1
  146.0 1.9 %collective-permute-start.3 = (bf16[16,1024]{1,0:T(8,128)(2,1)S(1)}, bf16[16,1024]{1,0:T(8,128)(2,1)S(1)}, u32[]{:S(2)}, u32[]{:S(2)}) collective-permute-start(bf16[16,1024]{1,0:T(8,128)(2,1)S(1)} %get-tuple-element.12.refs_2_), channel_id=1, source_target_pairs={{0,1},{1,2},{2,3},{3,4},{4,5},{5,6},{6,7},{7,8},{8,9},{9,10},{10,1... | collective-permute-start | bytes 98312 | tf_op jit(solution)/shard_map/ppermute | solution.py:259
  147.9 7.9 %collective-permute-start.4 = (bf16[16,1024]{1,0:T(8,128)(2,1)S(1)}, bf16[16,1024]{1,0:T(8,128)(2,1)S(1)}, u32[]{:S(2)}, u32[]{:S(2)}) collective-permute-start(bf16[16,1024]{1,0:T(8,128)(2,1)S(1)} %get-tuple-element.13.refs_1_), channel_id=1, source_target_pairs={{1,0},{2,1},{3,2},{4,3},{5,4},{6,5},{7,6},{8,7},{9,8},{10,9},{11,1... | collective-permute-start | bytes 98312 | tf_op jit(solution)/shard_map/ppermute | solution.py:260
  155.8 0.0 all-gather.4.cloned.1.call-done.refs_5_
  155.8 0.0 collective-permute-done.3.refs_0_
  155.8 1.5 collective-permute-done.4.refs_3_
  157.3 1.6 copy-done.1
  158.9 3.9 %conv.1 = bf16[32,1024]{1,0:T(8,128)(2,1)} custom-call(bf16[16,1024]{1,0:T(8,128)(2,1)S(1)} %collective-permute-done.3.refs_0_, bf16[16,1024]{1,0:T(8,128)(2,1)S(1)} %get-tuple-element.13.refs_1_, bf16[16,1024]{1,0:T(8,128)(2,1)S(1)} %get-tuple-element.12.refs_2_, bf16[16,1024]{1,0:T(8,128)(2,1)S(1)} %collective-permute-done.4.refs_3_, ...), custom_call_target="tpu_custom_call" | custom-call | tf_op jit(solution)/shard_map/conv/pallas_call | solution.py:261
  (8 shorter events, 0.0 us)
Async XLA Ops:
  6.5 66.9 %copy-start.4 = (bf16[1,1024,512]{2,1,0:T(8,128)(2,1)S(1)}, bf16[1,1024,512]{2,1,0:T(8,128)(2,1)}, u32[]{:S(2)}) copy-start(bf16[1,1024,512]{2,1,0:T(8,128)(2,1)} %param.14) | copy-start | bytes 3145732
  6.5 66.9 %copy-start.5 = (bf16[1,1024,512]{2,1,0:T(8,128)(2,1)S(1)}, bf16[1,1024,512]{2,1,0:T(8,128)(2,1)}, u32[]{:S(2)}) copy-start(bf16[1,1024,512]{2,1,0:T(8,128)(2,1)} %param.15) | copy-start | bytes 3145732
  6.5 135.6 %all-gather.6.cloned.1.call-start = ((), (), s32[]{:S(2)}) async-start(), calls=%async_computation.6 | async-start | bytes 4792320 | tf_op jit(solution)/shard_map/all_gather | solution.py:172
  11.9 1.0 copy-start.2
  12.9 0.7 copy-start.9
  15.3 39.6 %all-to-all-start = ((bf16[64,8,256]{2,1,0:T(8,128)(2,1)}), bf16[64,8,256]{2,1,0:T(8,128)(2,1)S(1)}, u32[]{:S(2)}, u32[]{:S(2)}) async-start(bf16[64,8,256]{2,1,0:T(8,128)(2,1)} %bitcast.5), calls=%async_computation | async-start | bytes 524288 | tf_op jit(solution)/shard_map/all_to_all | solution.py:202
  34.1 121.7 %all-gather.4.cloned.1.call-start = ((), (), s32[]{:S(2)}) async-start(), calls=%async_computation.5 | async-start | bytes 2359296 | tf_op jit(solution)/shard_map/all_gather | solution.py:173
  34.9 25.7 %collective-permute-start = (bf16[1024,512]{1,0:T(8,128)(2,1)}, bf16[1024,512]{1,0:T(8,128)(2,1)}, u32[]{:S(2)}, u32[]{:S(2)}) collective-permute-start(bf16[1024,512]{1,0:T(8,128)(2,1)} %bitcast.22), channel_id=1, source_target_pairs={{0,1},{1,0},{2,3},{3,2},{4,5},{5,4},{6,7},{7,6},{8,9},{9,8},{10,11... | collective-permute-start | bytes 3145736 | tf_op jit(solution)/shard_map/ppermute | solution.py:177
  36.8 23.8 %collective-permute-start.1 = (bf16[1024,512]{1,0:T(8,128)(2,1)}, bf16[1024,512]{1,0:T(8,128)(2,1)}, u32[]{:S(2)}, u32[]{:S(2)}) collective-permute-start(bf16[1024,512]{1,0:T(8,128)(2,1)} %bitcast.24), channel_id=1, source_target_pairs={{0,1},{1,0},{2,3},{3,2},{4,5},{5,4},{6,7},{7,6},{8,9},{9,8},{10,11... | collective-permute-start | bytes 3145736 | tf_op jit(solution)/shard_map/ppermute | solution.py:177
  39.2 21.4 %collective-permute-start.2 = (bf16[512,1024]{1,0:T(8,128)(2,1)}, bf16[512,1024]{1,0:T(8,128)(2,1)}, u32[]{:S(2)}, u32[]{:S(2)}) collective-permute-start(bf16[512,1024]{1,0:T(8,128)(2,1)} %bitcast.26), channel_id=1, source_target_pairs={{0,1},{1,0},{2,3},{3,2},{4,5},{5,4},{6,7},{7,6},{8,9},{9,8},{10,11... | collective-permute-start | bytes 3145736 | tf_op jit(solution)/shard_map/ppermute | solution.py:177
  56.0 77.2 %copy-start.10 = (f32[256,2]{0,1:T(2,128)S(1)}, f32[256,2]{0,1:T(2,128)}, u32[]{:S(2)}) copy-start(f32[256,2]{0,1:T(2,128)} %param.13) | copy-start | bytes 6148
  56.0 17.4 %all-to-all-start.1 = ((bf16[4,512,256]{2,1,0:T(8,128)(2,1)}), bf16[4,512,256]{2,1,0:T(8,128)(2,1)S(1)}, u32[]{:S(2)}, u32[]{:S(2)}) async-start(bf16[4,512,256]{2,1,0:T(8,128)(2,1)} %broadcast_in_dim.17), calls=%async_computation.1 | async-start | bytes 2097152 | tf_op jit(solution)/shard_map/all_to_all | solution.py:205
  73.4 1.2 copy-start.6
  80.1 62.1 %copy-start.3 = (bf16[256,1024]{1,0:T(8,128)(2,1)S(1)}, bf16[256,1024]{1,0:T(8,128)(2,1)}, u32[]{:S(2)}) copy-start(bf16[256,1024]{1,0:T(8,128)(2,1)} %frames_ref.1) | copy-start | bytes 1572868
  80.1 62.1 %copy-start.7 = (f32[1024]{0:T(1024)S(1)}, f32[1024]{0:T(1024)}, u32[]{:S(2)}) copy-start(f32[1024]{0:T(1024)} %param.17) | copy-start | bytes 12292
  80.1 62.1 %copy-start.8 = (f32[1024]{0:T(1024)S(1)}, f32[1024]{0:T(1024)}, u32[]{:S(2)}) copy-start(f32[1024]{0:T(1024)} %param.18) | copy-start | bytes 12292
  142.2 2.2 %copy-start = (bf16[16640,128]{1,0:T(8,128)(2,1)S(1)}, bf16[16640,128]{1,0:T(8,128)(2,1)}, u32[]{:S(2)}) copy-start(bf16[16640,128]{1,0:T(8,128)(2,1)} %all-gather.6.cloned.1.call-done) | copy-start | bytes 12779524
  146.0 9.8 %collective-permute-start.3 = (bf16[16,1024]{1,0:T(8,128)(2,1)S(1)}, bf16[16,1024]{1,0:T(8,128)(2,1)S(1)}, u32[]{:S(2)}, u32[]{:S(2)}) collective-permute-start(bf16[16,1024]{1,0:T(8,128)(2,1)S(1)} %get-tuple-element.12.refs_2_), channel_id=1, source_target_pairs={{0,1},{1,2},{2,3},{3,4},{4,5},{5,6},{6,7},{7,8},{8,9},{9,10},{10,1... | collective-permute-start | bytes 98312 | tf_op jit(solution)/shard_map/ppermute | solution.py:259
  147.9 9.4 %collective-permute-start.4 = (bf16[16,1024]{1,0:T(8,128)(2,1)S(1)}, bf16[16,1024]{1,0:T(8,128)(2,1)S(1)}, u32[]{:S(2)}, u32[]{:S(2)}) collective-permute-start(bf16[16,1024]{1,0:T(8,128)(2,1)S(1)} %get-tuple-element.13.refs_1_), channel_id=1, source_target_pairs={{1,0},{2,1},{3,2},{4,3},{5,4},{6,5},{7,6},{8,7},{9,8},{10,9},{11,1... | collective-permute-start | bytes 98312 | tf_op jit(solution)/shard_map/ppermute | solution.py:260
  157.3 1.6 copy-start.1
Sparse Core Ops, SparseCore 0:
  11.9 44.4 all-gather.5
  58.6 40.6 all-gather.3

commit v2 on v1

v2 whole, which is shorter than its diff:
```python
import jax
import jax.numpy as jnp
from jax import lax
from jax.experimental import pallas as pl
from jax.experimental.pallas import tpu as pltpu
from jax.sharding import Mesh
from jax.sharding import PartitionSpec as P

WIDE = ("x", "z")
NARROW = ("y", "c")
EVERY = ("x", "z", "y", "c")
VMEM_BYTES = 48 << 20


def in_vmem(count):
    return [pl.BlockSpec(memory_space=pltpu.VMEM)] * count


def mm(a, b):
    return jnp.dot(a, b, preferred_element_type=jnp.float32)


def fetched(copies):
    for copy in copies:
        copy.start()
    return copies


def pack_kernel(in_ref, taps_ref, packed_ref, in_vmem_ref, taps_vmem, wide_ref, sem):
    copies = fetched(
        [
            pltpu.make_async_copy(in_ref, in_vmem_ref, sem.at[0]),
            pltpu.make_async_copy(taps_ref, taps_vmem, sem.at[1]),
        ]
    )
    both, lanes = in_ref.shape
    half = both // 2
    taps = taps_ref.shape[0]
    copies[0].wait()
    wide_ref[...] = in_vmem_ref[...].astype(jnp.float32)
    packed_ref[:half, :] = wide_ref[pl.ds(0, half, 2), :].astype(jnp.bfloat16)
    packed_ref[half:both, :] = wide_ref[pl.ds(1, half, 2), :].astype(jnp.bfloat16)
    copies[1].wait()
    packed_ref[both : both + taps + 1, :] = jnp.concatenate(
        [taps_vmem[...].astype(jnp.float32), jnp.zeros((1, lanes), jnp.float32)], axis=0
    ).astype(jnp.bfloat16)


def route_kernel(experts, slots, ids_ref, frames_ref, out_ref, target_ref, held_ref, ids_vmem, sem):
    count, share = held_ref.shape
    column = pl.multiple_of(lax.axis_index("y") * share, share)
    names, held = fetched(
        [
            pltpu.make_async_copy(ids_ref, ids_vmem, sem.at[0]),
            pltpu.make_async_copy(frames_ref.at[:, pl.ds(column, share)], held_ref, sem.at[1]),
        ]
    )
    names.wait()
    ids = ids_vmem[...]
    first = lax.axis_index("c") * slots
    expert = lax.broadcasted_iota(jnp.int32, (experts, count), 0)
    named = [jnp.where(expert == ids[k : k + 1, :], 1.0, 0.0) for k in range(2)]
    before = lax.broadcasted_iota(jnp.int32, (count, count), 0) < lax.broadcasted_iota(
        jnp.int32, (count, count), 1
    )
    rank = mm(
        jnp.concatenate(named, axis=0).astype(jnp.bfloat16),
        jnp.where(before, 1.0, 0.0).astype(jnp.bfloat16),
    )
    total = jnp.sum(named[0], axis=1, keepdims=True)
    place = [
        jnp.sum(named[0] * rank[:experts], axis=0, keepdims=True),
        jnp.sum(named[1] * (rank[experts:] + total), axis=0, keepdims=True),
    ]
    row = lax.broadcasted_iota(jnp.int32, (experts * slots, count), 0)
    chosen = None
    for k in range(2):
        local = place[k].astype(jnp.int32) - first
        target = jnp.where(
            (local >= 0) & (local < slots), ids[k : k + 1, :] * slots + local, -1
        )
        target_ref[k : k + 1, :] = target.astype(jnp.float32)
        hit = row == target
        chosen = hit if chosen is None else chosen | hit
    pick = jnp.where(chosen, 1.0, 0.0).astype(jnp.bfloat16)
    held.wait()
    out_ref[...] = mm(pick, held_ref[...]).astype(jnp.bfloat16)


def expert_kernel(x_ref, *refs):
    sources, out_ref, held, sem = refs[:6], refs[6], refs[7:13], refs[13]
    order = (0, 1, 3, 4, 2, 5)
    copies = [pltpu.make_async_copy(s, h, sem.at[i]) for i, (s, h) in enumerate(zip(sources, held))]
    for i in order:
        copies[i].start()
    chunks, _, width = x_ref.shape
    hidden = []
    for pair in range(2):
        gate_ref, up_ref = held[3 * pair : 3 * pair + 2]
        x = jnp.concatenate([x_ref[q] for q in range(chunks)], axis=1)
        copies[3 * pair].wait()
        gate = mm(x, gate_ref[...])
        copies[3 * pair + 1].wait()
        up = mm(x, up_ref[...])
        hidden.append((gate * jax.nn.sigmoid(gate) * up).astype(jnp.bfloat16))
    copies[2].wait()
    copies[5].wait()
    for q in range(chunks):
        cols = slice(q * width, (q + 1) * width)
        out_ref[q] = (mm(hidden[0], held[2][:, cols]) + mm(hidden[1], held[5][:, cols])).astype(
            jnp.bfloat16
        )


def combine_kernel(target_ref, gate_ref, rows_ref, out_ref):
    count = target_ref.shape[1]
    table = jnp.concatenate(
        [target_ref[...], gate_ref[...], jnp.zeros((4, count), jnp.float32)], axis=0
    ).T
    slot = lax.broadcasted_iota(jnp.int32, (count, rows_ref.shape[0]), 1)
    total = None
    for k in range(2):
        hit = slot == table[:, k : k + 1].astype(jnp.int32)
        picked = mm(jnp.where(hit, 1.0, 0.0).astype(jnp.bfloat16), rows_ref[...])
        picked = picked * table[:, 2 + k : 3 + k]
        total = picked if total is None else total + picked
    out_ref[...] = total.astype(jnp.bfloat16)


def norm_kernel(
    cores, frames_ref, in_ref, parts_ref, gain_ref, bias_ref, res_ref, lo_ref, hi_ref, taps_ref, own_ref, held_ref, sem
):
    own, width = own_ref.shape
    blocks = in_ref.shape[0]
    index = lax.axis_index("y") * cores + lax.axis_index("c")
    copies = fetched(
        [
            pltpu.make_async_copy(
                frames_ref.at[pl.ds(pl.multiple_of(index * own, own), own), :],
                own_ref,
                sem.at[blocks],
            )
        ]
        + [pltpu.make_async_copy(in_ref.at[n], held_ref.at[n], sem.at[n]) for n in range(blocks)]
    )
    moe = jnp.concatenate(
        [
            parts_ref[2 * q].astype(jnp.float32) + parts_ref[2 * q + 1].astype(jnp.float32)
            for q in range(parts_ref.shape[0] // 2)
        ],
        axis=1,
    )
    copies[0].wait()
    residual = own_ref[...].astype(jnp.float32) + moe
    res_ref[...] = residual
    centered = residual - jnp.mean(residual, axis=1, keepdims=True)
    variance = jnp.mean(centered * centered, axis=1, keepdims=True)
    normed = (centered / jnp.sqrt(variance + 1e-05) * gain_ref[...] + bias_ref[...]).astype(
        jnp.bfloat16
    )
    channels = in_ref.shape[2]
    half = lo_ref.shape[0]
    for n in range(blocks):
        copies[n + 1].wait()
        both = jnp.concatenate(
            [held_ref[n, :width, :], held_ref[n, width : 2 * width, :]], axis=1
        )
        projected = mm(normed, both)
        glu = projected[:, :channels] * jax.nn.sigmoid(projected[:, channels:])
        glu = glu.astype(jnp.bfloat16)
        cols = slice(n * channels, (n + 1) * channels)
        lo_ref[:, cols] = glu[:half]
        hi_ref[:, cols] = glu[half:]
        taps_ref[:, cols] = held_ref[n, 2 * width :, :].astype(jnp.float32)


def conv_kernel(taps, point_ref, left_ref, lo_ref, hi_ref, right_ref, taps_ref, res_ref, out_ref, held_ref, sem):
    half, width = lo_ref.shape
    count = 2 * half
    reach = (taps - 1) // 2
    step = width // sem.shape[0]
    copies = fetched(
        [
            pltpu.make_async_copy(
                point_ref.at[i * step : (i + 1) * step, :],
                held_ref.at[i * step : (i + 1) * step, :],
                sem.at[i],
            )
            for i in range(sem.shape[0])
        ]
    )
    total = res_ref[...]
    for i, copy in enumerate(copies):
        cols = slice(i * step, (i + 1) * step)
        window = jnp.concatenate(
            [ref[:, cols] for ref in (left_ref, lo_ref, hi_ref, right_ref)], axis=0
        ).astype(jnp.float32)
        depth = None
        for turn in range(8):
            moved = pltpu.roll(window, 2 * count - turn, 0) if turn else window
            for j in range(taps):
                start = half - reach + j
                if start % 8 == turn:
                    term = moved[start - turn : start - turn + count] * taps_ref[j : j + 1, cols]
                    depth = term if depth is None else depth + term
        act = (depth * jax.nn.sigmoid(depth)).astype(jnp.bfloat16)
        copy.wait()
        total = total + mm(act, held_ref[cols, :])
    out_ref[...] = total.astype(jnp.bfloat16)


def shards(
    frames,
    expert_ids,
    gate_values,
    w_gate,
    w_up,
    w_down,
    norm_gain,
    norm_bias,
    point_in,
    depth_kernel,
    point_out,
):
    count, width = frames.shape
    wide = lax.axis_size("x") * lax.axis_size("z")
    quarters, cores = lax.axis_size("y"), lax.axis_size("c")
    narrow = quarters * cores
    experts = w_gate.shape[0] * wide
    slots = 2 * expert_ids.shape[1] * count // experts // cores
    share = width // quarters
    own = count // narrow
    taps, channels = depth_kernel.shape
    params = pltpu.CompilerParams(vmem_limit_bytes=VMEM_BYTES)

    in_hbm = lambda n: [pl.BlockSpec(memory_space=pltpu.HBM)] * n
    far = lambda array: pltpu.with_memory_space_constraint(array, pltpu.HBM)
    frames = far(frames)

    packed_rows = 2 * width + taps + 1
    packed = pl.pallas_call(
        pack_kernel,
        in_specs=in_hbm(2),
        out_specs=pl.BlockSpec(memory_space=pltpu.VMEM),
        out_shape=jax.ShapeDtypeStruct((packed_rows, channels), jnp.bfloat16),
        scratch_shapes=[
            pltpu.VMEM((2 * width, channels), jnp.bfloat16),
            pltpu.VMEM((taps, channels), jnp.bfloat16),
            pltpu.VMEM((2 * width, channels), jnp.float32),
            pltpu.SemaphoreType.DMA((2,)),
        ],
        compiler_params=params,
        name="pack",
    )(far(point_in.reshape(2 * width, channels)), far(depth_kernel))
    packed = lax.all_gather(packed, NARROW, axis=0)

    mine = [w_gate[0], w_up[0], w_down[0]]
    swap = [(i, cores - 1 - i) for i in range(cores)]
    theirs = [lax.ppermute(w, "c", swap) for w in mine]

    rows = experts * slots
    outgoing, target = pl.pallas_call(
        lambda *refs: route_kernel(experts, slots, *refs),
        in_specs=in_hbm(2),
        out_specs=in_vmem(2),
        out_shape=[
            jax.ShapeDtypeStruct((rows, share), jnp.bfloat16),
            jax.ShapeDtypeStruct((2, count), jnp.float32),
        ],
        scratch_shapes=[
            pltpu.VMEM((count, share), jnp.bfloat16),
            pltpu.VMEM((2, count), jnp.int32),
            pltpu.SemaphoreType.DMA((2,)),
        ],
        compiler_params=params,
        name="route",
    )(far(expert_ids.T), frames)

    def over(axis, cells):
        return lax.all_to_all(cells, axis, split_axis=0, concat_axis=0, tiled=True)

    arrived = over(WIDE, outgoing.reshape(experts, slots, share)).reshape(1, rows, share)
    x = over("y", jnp.broadcast_to(arrived, (quarters, rows, share)))
    weights = mine + theirs
    partial = pl.pallas_call(
        expert_kernel,
        in_specs=in_vmem(1) + in_hbm(6),
        out_specs=pl.BlockSpec(memory_space=pltpu.VMEM),
        out_shape=jax.ShapeDtypeStruct((quarters, rows, share), jnp.bfloat16),
        scratch_shapes=[pltpu.VMEM(w.shape, w.dtype) for w in weights]
        + [pltpu.SemaphoreType.DMA((6,))],
        compiler_params=params,
        name="experts",
    )(x, *[far(w) for w in weights])
    partial = over("y", partial)
    summed = jnp.sum(partial.astype(jnp.float32), axis=0).astype(jnp.bfloat16)
    summed, point_out = lax.optimization_barrier((summed, point_out))
    point = lax.all_gather(point_out, NARROW, axis=0, tiled=True)
    returned = over(WIDE, summed.reshape(experts, slots, share)).reshape(rows, share)
    mixed = pl.pallas_call(
        combine_kernel,
        in_specs=in_vmem(3),
        out_specs=pl.BlockSpec(memory_space=pltpu.VMEM),
        out_shape=jax.ShapeDtypeStruct((count, share), jnp.bfloat16),
        compiler_params=params,
        name="combine",
    )(target, gate_values.T, returned)
    parts = over(NARROW, mixed.reshape(narrow, own, share))

    half = own // 2
    residual, lo, hi, kernel = pl.pallas_call(
        lambda *refs: norm_kernel(cores, *refs),
        in_specs=in_hbm(2) + in_vmem(3),
        out_specs=in_vmem(4),
        out_shape=[
            jax.ShapeDtypeStruct((own, width), jnp.float32),
            jax.ShapeDtypeStruct((half, width), jnp.bfloat16),
            jax.ShapeDtypeStruct((half, width), jnp.bfloat16),
            jax.ShapeDtypeStruct((taps + 1, width), jnp.float32),
        ],
        scratch_shapes=[
            pltpu.VMEM((own, width), jnp.bfloat16),
            pltpu.VMEM(packed.shape, jnp.bfloat16),
            pltpu.SemaphoreType.DMA((narrow + 1,)),
        ],
        compiler_params=params,
        name="norm_glu",
    )(frames, far(packed), parts, norm_gain[None, :], norm_bias[None, :])

    ends = wide * narrow - 1
    left = lax.ppermute(hi, EVERY, [(i, i + 1) for i in range(ends)])
    right = lax.ppermute(lo, EVERY, [(i + 1, i) for i in range(ends)])
    return pl.pallas_call(
        lambda *refs: conv_kernel(taps, *refs),
        in_specs=in_hbm(1) + in_vmem(6),
        out_specs=pl.BlockSpec(memory_space=pltpu.VMEM),
        out_shape=jax.ShapeDtypeStruct((own, width), jnp.bfloat16),
        scratch_shapes=[
            pltpu.VMEM((width, width), jnp.bfloat16),
            pltpu.SemaphoreType.DMA((quarters,)),
        ],
        compiler_params=params,
        name="conv",
    )(far(point), left, lo, hi, right, kernel, residual)


def solution(mesh):
    chips = Mesh(mesh.devices.reshape(4, 16, 4, 2), EVERY)
    return jax.shard_map(
        shards,
        mesh=chips,
        in_specs=(
            P(WIDE, None),
            P(WIDE, None),
            P(WIDE, None),
            P(WIDE, None, NARROW),
            P(WIDE, None, NARROW),
            P(WIDE, NARROW, None),
            P(),
            P(),
            P(None, None, NARROW),
            P(None, NARROW),
            P(NARROW, None),
        ),
        out_specs=P(EVERY, None),
        check_vma=False,
    )
```

time: 170 us -> 155 us (0.912)
  local copies, waits for them, and re-layouts: 13.1 us -> 1.15 us
  blocking collectives: 61.3 us -> 55.7 us
  Pallas kernels: 13 us -> 15.7 us
    unnamed x23 -> x10, local copies, waits for them, and re-layouts: 8.03 us -> 0.02 us
    all_to_all x3, blocking collectives: 61.3 us -> 55.7 us  [over(): return lax.all_to_all(cells, axis, split_axis=0, concat_axis=0, tiled=True)]
    concatenate x1 -> x0, local copies, waits for them, and re-layouts: 3.98 us -> none  [shards(): jnp.concatenate([point_in.transpose(1, 0, 2).reshape(2 * width, channels)...]
    pallas_call x4 -> x5, Pallas kernels: 12.5 us -> 15.2 us  [the longest x1 5.43 us: shards(): pl.pallas_call(expert_kernel, in_specs=in_vmem(1) + in_hbm(6), out_specs=...]
  transfers between devices with their start and end apart: 9 -> 9, of which waited for: 3 -> 3; matrix products, arithmetic and copies ran while one was open for 1% -> 1% of each run, Pallas kernels for 5% -> 7%
where the time goes in v2:
time: 155 us
  blocking collectives  55.7 us (36%)
  starting transfers between devices  39.3 us (25%)
  waiting for transfers between devices  28.9 us (19%)
  Pallas kernels  15.7 us (10%)
  between operations  13.6 us (9%)
    all_to_all x3, blocking collectives, over(): return lax.all_to_all(cells, axis, split_axis=0, concat_axis=0, tiled=True)  55.7 us
    all_to_all x2, waiting for transfers between devices, over(): return lax.all_to_all(cells, axis, split_axis=0, concat_axis=0, tiled=True)  27.3 us
    all_to_all x2, starting transfers between devices, over(): return lax.all_to_all(cells, axis, split_axis=0, concat_axis=0, tiled=True)  23.3 us
    ppermute x1, starting transfers between devices, shards(): right = lax.ppermute(lo, EVERY, [(i + 1, i) for i in range(ends)])  7.86 us
    ppermute x3, starting transfers between devices, shards(): theirs = [lax.ppermute(w, 'c', swap) for w in mine]  6.25 us
    pallas_call x1, Pallas kernels, shards(): pl.pallas_call(expert_kernel, in_specs=in_vmem(1) + in_hbm(6), out_specs=...  5.43 us
    pallas_call x1, Pallas kernels, shards(): pl.pallas_call(lambda *refs: norm_kernel(cores, *refs), in_specs=in_hbm(2...  3.3 us
  transfers between devices with their start and end apart: 9, of which 3 were waited for; matrix products, arithmetic and copies ran while one was open for 1% of the time, Pallas kernels for 7%

profile of v2, /device:TPU:6, one launch (start us, length us, event | category | flops | bytes accessed | tf_op | source)
XLA Modules:
  0.0 154.6 jit_solution(17578730754494234971)
XLA Ops:
  6.5 0.0 all-gather.6.cloned.1.call-start
  6.5 2.1 %pack.1 = bf16[2080,128]{1,0:T(8,128)(2,1)} custom-call(bf16[2048,128]{1,0:T(8,128)(2,1)} %bitcast.28, bf16[31,128]{1,0:T(8,128)(2,1)} %taps_ref.1), custom_call_target="tpu_custom_call" | custom-call | tf_op jit(solution)/shard_map/pack/pallas_call | solution.py:241
  8.6 0.0 all-gather.6.cloned.1.call-update
  8.6 2.0 %route.1 = (bf16[512,256]{1,0:T(8,128)(2,1)}, f32[2,256]{1,0:T(2,128)S(1)}) custom-call(s32[2,256]{1,0:T(2,128)} %bitcast.29, bf16[256,1024]{1,0:T(8,128)(2,1)} %refs_0_.1), custom_call_target="tpu_custom_call" | custom-call | tf_op jit(solution)/shard_map/route/pallas_call | solution.py:262
  10.6 18.8 %all-to-all-start = ((bf16[64,8,256]{2,1,0:T(8,128)(2,1)}), bf16[64,8,256]{2,1,0:T(8,128)(2,1)S(1)}, u32[]{:S(2)}, u32[]{:S(2)}) async-start(bf16[64,8,256]{2,1,0:T(8,128)(2,1)} %bitcast.1), calls=%async_computation | async-start | bytes 524288 | tf_op jit(solution)/shard_map/all_to_all | solution.py:280
  29.4 1.9 %collective-permute-start = (bf16[1024,512]{1,0:T(8,128)(2,1)}, bf16[1024,512]{1,0:T(8,128)(2,1)S(1)}, u32[]{:S(2)}, u32[]{:S(2)}) collective-permute-start(bf16[1024,512]{1,0:T(8,128)(2,1)} %bitcast.22), channel_id=1, source_target_pairs={{0,1},{1,0},{2,3},{3,2},{4,5},{5,4},{6,7},{7,6},{8,9},{9,8},{10,11... | collective-permute-start | bytes 3145736 | tf_op jit(solution)/shard_map/ppermute | solution.py:259
  31.3 2.4 %collective-permute-start.1 = (bf16[1024,512]{1,0:T(8,128)(2,1)}, bf16[1024,512]{1,0:T(8,128)(2,1)S(1)}, u32[]{:S(2)}, u32[]{:S(2)}) collective-permute-start(bf16[1024,512]{1,0:T(8,128)(2,1)} %bitcast.24), channel_id=1, source_target_pairs={{0,1},{1,0},{2,3},{3,2},{4,5},{5,4},{6,7},{7,6},{8,9},{9,8},{10,11... | collective-permute-start | bytes 3145736 | tf_op jit(solution)/shard_map/ppermute | solution.py:259
  33.8 1.9 %collective-permute-start.2 = (bf16[512,1024]{1,0:T(8,128)(2,1)}, bf16[512,1024]{1,0:T(8,128)(2,1)}, u32[]{:S(2)}, u32[]{:S(2)}) collective-permute-start(bf16[512,1024]{1,0:T(8,128)(2,1)} %bitcast.26), channel_id=1, source_target_pairs={{0,1},{1,0},{2,3},{3,2},{4,5},{5,4},{6,7},{7,6},{8,9},{9,8},{10,11... | collective-permute-start | bytes 3145736 | tf_op jit(solution)/shard_map/ppermute | solution.py:259
  35.7 14.5 %all-to-all-done = bf16[64,8,256]{2,1,0:T(8,128)(2,1)S(1)} async-done(((bf16[64,8,256]{2,1,0:T(8,128)(2,1)}), bf16[64,8,256]{2,1,0:T(8,128)(2,1)S(1)}, u32[]{:S(2)}, u32[]{:S(2)}) %all-to-all-start) | async-done | bytes 262176 | tf_op jit(solution)/shard_map/all_to_all | solution.py:280
  50.2 1.1 broadcast_in_dim.14
  51.4 4.5 %all-to-all-start.1 = ((bf16[4,512,256]{2,1,0:T(8,128)(2,1)}), bf16[4,512,256]{2,1,0:T(8,128)(2,1)S(1)}, u32[]{:S(2)}, u32[]{:S(2)}) async-start(bf16[4,512,256]{2,1,0:T(8,128)(2,1)} %broadcast_in_dim.14), calls=%async_computation.1 | async-start | bytes 2097152 | tf_op jit(solution)/shard_map/all_to_all | solution.py:280
  55.8 0.0 copy-start.2
  55.8 0.0 all-gather.4.cloned.1.call-start
  55.8 0.0 collective-permute-done.refs_3_
  55.8 0.0 copy-start.3
  55.8 0.0 collective-permute-done.1.refs_4_
  55.9 0.0 copy-start.4
  55.9 0.0 collective-permute-done.2.refs_5_
  55.9 12.8 %all-to-all-done.1.x_ref = bf16[4,512,256]{2,1,0:T(8,128)(2,1)S(1)} async-done(((bf16[4,512,256]{2,1,0:T(8,128)(2,1)}), bf16[4,512,256]{2,1,0:T(8,128)(2,1)S(1)}, u32[]{:S(2)}, u32[]{:S(2)}) %all-to-all-start.1) | async-done | bytes 1048608 | tf_op jit(solution)/shard_map/all_to_all | solution.py:280
  68.7 0.0 copy-done.3
  68.7 0.0 copy-done.4
  68.7 5.4 %experts.1 = bf16[4,512,256]{2,1,0:T(8,128)(2,1)S(1)} custom-call(bf16[4,512,256]{2,1,0:T(8,128)(2,1)S(1)} %all-to-all-done.1.x_ref, bf16[1024,512]{1,0:T(8,128)(2,1)} %bitcast.23, bf16[1024,512]{1,0:T(8,128)(2,1)} %bitcast.25, bf16[512,1024]{1,0:T(8,128)(2,1)} %bitcast.27, bf16[1024,512]{1,0:T(8,128)(2,1)} %copy-done.3, bf16[1024,512]{1,0:T(8,128)(2,1)} %copy-done.4, ...), custom_call_target="tpu_custom_call" | custom-call | tf_op jit(solution)/shard_map/experts/pallas_call | solution.py:285
  74.1 0.0 copy-start
  74.1 0.0 copy-start.1
  74.1 14.1 %all_to_all.25 = bf16[4,512,256]{2,1,0:T(8,128)(2,1)S(1)} all-to-all(bf16[4,512,256]{2,1,0:T(8,128)(2,1)S(1)} %experts.1), channel_id=1, replica_groups=mesh['x'=4,'z'=16,'y'=4,'c'=2] {'y'}, dimensions={0} | all-to-all | bytes 2097152 | tf_op jit(solution)/shard_map/all_to_all | solution.py:280
  88.2 0.3 reduce_sum.12
  88.5 0.0 all-gather.4.cloned.1.call-update
  88.5 33.1 %all_to_all.26 = bf16[64,8,256]{2,1,0:T(8,128)(2,1)S(1)} all-to-all(bf16[64,8,256]{2,1,0:T(8,128)(2,1)S(1)} %bitcast.21), channel_id=1, replica_groups=mesh['x'=4,'z'=16,'y'=4,'c'=2] {'x','z'}, dimensions={0} | all-to-all | bytes 524288 | tf_op jit(solution)/shard_map/all_to_all | solution.py:280
  121.6 0.0 copy-done.2
  121.6 0.5 combine.1
  122.1 8.5 %all_to_all.27.refs_2_ = bf16[8,32,256]{2,1,0:T(8,128)(2,1)S(1)} all-to-all(bf16[8,32,256]{2,1,0:T(8,128)(2,1)S(1)} %bitcast.15), channel_id=1, replica_groups=mesh['x'=4,'z'=16,'y'=4,'c'=2] {'y','c'}, dimensions={0} | all-to-all | bytes 262144 | tf_op jit(solution)/shard_map/all_to_all | solution.py:280
  130.6 0.0 all-gather.6.cloned.1.call-done
  130.6 0.0 copy-done
  130.6 0.0 copy-done.1
  130.6 3.3 %norm_glu.1 = (f32[32,1024]{1,0:T(8,128)S(1)}, bf16[16,1024]{1,0:T(8,128)(2,1)S(1)}, bf16[16,1024]{1,0:T(8,128)(2,1)S(1)}, f32[32,1024]{1,0:T(8,128)S(1)}) custom-call(bf16[256,1024]{1,0:T(8,128)(2,1)} %refs_0_.1, bf16[8,2080,128]{2,1,0:T(8,128)(2,1)} %bitcast.19, bf16[8,32,256]{2,1,0:T(8,128)(2,1)S(1)} %all_to_all.27.refs_2_, f32[1,1024]{1,0:T(1,128)S(1)} %bitcast.16, ...), custom_call_target="tpu_custom_call" | custom-call | tf_op jit(solution)/shard_map/norm_glu/pallas_call | solution.py:311
  133.9 1.9 %collective-permute-start.3 = (bf16[16,1024]{1,0:T(8,128)(2,1)S(1)}, bf16[16,1024]{1,0:T(8,128)(2,1)S(1)}, u32[]{:S(2)}, u32[]{:S(2)}) collective-permute-start(bf16[16,1024]{1,0:T(8,128)(2,1)S(1)} %get-tuple-element.17.refs_3_), channel_id=1, source_target_pairs={{0,1},{1,2},{2,3},{3,4},{4,5},{5,6},{6,7},{7,8},{8,9},{9,10},{10,1... | collective-permute-start | bytes 98312 | tf_op jit(solution)/shard_map/ppermute | solution.py:331
  135.9 7.9 %collective-permute-start.4 = (bf16[16,1024]{1,0:T(8,128)(2,1)S(1)}, bf16[16,1024]{1,0:T(8,128)(2,1)S(1)}, u32[]{:S(2)}, u32[]{:S(2)}) collective-permute-start(bf16[16,1024]{1,0:T(8,128)(2,1)S(1)} %get-tuple-element.18.refs_2_), channel_id=1, source_target_pairs={{1,0},{2,1},{3,2},{4,3},{5,4},{6,5},{7,6},{8,7},{9,8},{10,9},{11,1... | collective-permute-start | bytes 98312 | tf_op jit(solution)/shard_map/ppermute | solution.py:332
  143.7 0.0 all-gather.4.cloned.1.call-done.refs_0_
  143.8 0.0 collective-permute-done.3.refs_1_
  143.8 1.5 collective-permute-done.4.refs_4_
  145.3 2.5 %conv.1 = bf16[32,1024]{1,0:T(8,128)(2,1)} custom-call(bf16[1024,1024]{1,0:T(8,128)(2,1)} %all-gather.4.cloned.1.call-done.refs_0_, bf16[16,1024]{1,0:T(8,128)(2,1)S(1)} %collective-permute-done.3.refs_1_, bf16[16,1024]{1,0:T(8,128)(2,1)S(1)} %get-tuple-element.18.refs_2_, bf16[16,1024]{1,0:T(8,128)(2,1)S(1)} %get-tuple-element.17.refs_3_, ...), custom_call_target="tpu_custom_call" | custom-call | tf_op jit(solution)/shard_map/conv/pallas_call | solution.py:333
Async XLA Ops:
  6.5 124.1 %all-gather.6.cloned.1.call-start = ((), (), s32[]{:S(2)}) async-start(), calls=%async_computation.6 | async-start | bytes 4792320 | tf_op jit(solution)/shard_map/all_gather | solution.py:255
  10.6 39.6 %all-to-all-start = ((bf16[64,8,256]{2,1,0:T(8,128)(2,1)}), bf16[64,8,256]{2,1,0:T(8,128)(2,1)S(1)}, u32[]{:S(2)}, u32[]{:S(2)}) async-start(bf16[64,8,256]{2,1,0:T(8,128)(2,1)} %bitcast.1), calls=%async_computation | async-start | bytes 524288 | tf_op jit(solution)/shard_map/all_to_all | solution.py:280
  29.4 26.4 %collective-permute-start = (bf16[1024,512]{1,0:T(8,128)(2,1)}, bf16[1024,512]{1,0:T(8,128)(2,1)S(1)}, u32[]{:S(2)}, u32[]{:S(2)}) collective-permute-start(bf16[1024,512]{1,0:T(8,128)(2,1)} %bitcast.22), channel_id=1, source_target_pairs={{0,1},{1,0},{2,3},{3,2},{4,5},{5,4},{6,7},{7,6},{8,9},{9,8},{10,11... | collective-permute-start | bytes 3145736 | tf_op jit(solution)/shard_map/ppermute | solution.py:259
  31.3 24.5 %collective-permute-start.1 = (bf16[1024,512]{1,0:T(8,128)(2,1)}, bf16[1024,512]{1,0:T(8,128)(2,1)S(1)}, u32[]{:S(2)}, u32[]{:S(2)}) collective-permute-start(bf16[1024,512]{1,0:T(8,128)(2,1)} %bitcast.24), channel_id=1, source_target_pairs={{0,1},{1,0},{2,3},{3,2},{4,5},{5,4},{6,7},{7,6},{8,9},{9,8},{10,11... | collective-permute-start | bytes 3145736 | tf_op jit(solution)/shard_map/ppermute | solution.py:259
  33.8 22.1 %collective-permute-start.2 = (bf16[512,1024]{1,0:T(8,128)(2,1)}, bf16[512,1024]{1,0:T(8,128)(2,1)}, u32[]{:S(2)}, u32[]{:S(2)}) collective-permute-start(bf16[512,1024]{1,0:T(8,128)(2,1)} %bitcast.26), channel_id=1, source_target_pairs={{0,1},{1,0},{2,3},{3,2},{4,5},{5,4},{6,7},{7,6},{8,9},{9,8},{10,11... | collective-permute-start | bytes 3145736 | tf_op jit(solution)/shard_map/ppermute | solution.py:259
  51.4 17.3 %all-to-all-start.1 = ((bf16[4,512,256]{2,1,0:T(8,128)(2,1)}), bf16[4,512,256]{2,1,0:T(8,128)(2,1)S(1)}, u32[]{:S(2)}, u32[]{:S(2)}) async-start(bf16[4,512,256]{2,1,0:T(8,128)(2,1)} %broadcast_in_dim.14), calls=%async_computation.1 | async-start | bytes 2097152 | tf_op jit(solution)/shard_map/all_to_all | solution.py:280
  55.8 65.8 %copy-start.2 = (f32[256,2]{0,1:T(2,128)S(1)}, f32[256,2]{0,1:T(2,128)}, u32[]{:S(2)}) copy-start(f32[256,2]{0,1:T(2,128)} %param.13) | copy-start | bytes 6148
  55.8 87.9 %all-gather.4.cloned.1.call-start = ((), (), s32[]{:S(2)}) async-start(), calls=%async_computation.5 | async-start | bytes 2359296 | tf_op jit(solution)/shard_map/all_gather | solution.py:298
  55.8 12.8 %copy-start.3 = (bf16[1024,512]{1,0:T(8,128)(2,1)}, bf16[1024,512]{1,0:T(8,128)(2,1)S(1)}, u32[]{:S(2)}) copy-start(bf16[1024,512]{1,0:T(8,128)(2,1)S(1)} %collective-permute-done.refs_3_) | copy-start | bytes 3145732
  55.9 12.8 %copy-start.4 = (bf16[1024,512]{1,0:T(8,128)(2,1)}, bf16[1024,512]{1,0:T(8,128)(2,1)S(1)}, u32[]{:S(2)}) copy-start(bf16[1024,512]{1,0:T(8,128)(2,1)S(1)} %collective-permute-done.1.refs_4_) | copy-start | bytes 3145732
  74.1 56.5 %copy-start = (f32[1024]{0:T(1024)S(1)}, f32[1024]{0:T(1024)}, u32[]{:S(2)}) copy-start(f32[1024]{0:T(1024)} %param.17) | copy-start | bytes 12292
  74.1 56.5 %copy-start.1 = (f32[1024]{0:T(1024)S(1)}, f32[1024]{0:T(1024)}, u32[]{:S(2)}) copy-start(f32[1024]{0:T(1024)} %param.18) | copy-start | bytes 12292
  133.9 9.8 %collective-permute-start.3 = (bf16[16,1024]{1,0:T(8,128)(2,1)S(1)}, bf16[16,1024]{1,0:T(8,128)(2,1)S(1)}, u32[]{:S(2)}, u32[]{:S(2)}) collective-permute-start(bf16[16,1024]{1,0:T(8,128)(2,1)S(1)} %get-tuple-element.17.refs_3_), channel_id=1, source_target_pairs={{0,1},{1,2},{2,3},{3,4},{4,5},{5,6},{6,7},{7,8},{8,9},{9,10},{10,1... | collective-permute-start | bytes 98312 | tf_op jit(solution)/shard_map/ppermute | solution.py:331
  135.9 9.4 %collective-permute-start.4 = (bf16[16,1024]{1,0:T(8,128)(2,1)S(1)}, bf16[16,1024]{1,0:T(8,128)(2,1)S(1)}, u32[]{:S(2)}, u32[]{:S(2)}) collective-permute-start(bf16[16,1024]{1,0:T(8,128)(2,1)S(1)} %get-tuple-element.18.refs_2_), channel_id=1, source_target_pairs={{1,0},{2,1},{3,2},{4,3},{5,4},{6,5},{7,6},{8,7},{9,8},{10,9},{11,1... | collective-permute-start | bytes 98312 | tf_op jit(solution)/shard_map/ppermute | solution.py:332
Sparse Core Ops, SparseCore 0:
  9.5 44.4 all-gather.5
  88.6 30.7 all-gather.3

commit v3 on v2

v3 whole, which is shorter than its diff:
```python
import jax
import jax.numpy as jnp
from jax import lax
from jax.experimental import pallas as pl
from jax.experimental.pallas import tpu as pltpu
from jax.sharding import Mesh
from jax.sharding import PartitionSpec as P

WIDE = ("x", "z")
NARROW = ("y", "c")
EVERY = ("x", "z", "y", "c")
VMEM_BYTES = 32 << 20


def in_vmem(count):
    return [pl.BlockSpec(memory_space=pltpu.VMEM)] * count


def mm(a, b):
    return jnp.dot(a, b, preferred_element_type=jnp.float32)


def fetched(copies):
    for copy in copies:
        copy.start()
    return copies


def prepare_kernel(
    experts,
    slots,
    ids_ref,
    frames_ref,
    in_ref,
    taps_ref,
    point_ref,
    gates_ref,
    out_ref,
    table_ref,
    packed_ref,
    held_ref,
    ids_vmem,
    gates_vmem,
    in_vmem_ref,
    taps_vmem,
    wide_ref,
    sem,
):
    both, lanes = in_ref.shape
    half = both // 2
    taps = taps_ref.shape[0]
    at = both + taps + 1
    count, share = held_ref.shape
    column = pl.multiple_of(lax.axis_index("y") * share, share)
    names, held, halves, kernel, gates, *points = fetched(
        [
            pltpu.make_async_copy(ids_ref, ids_vmem, sem.at[0]),
            pltpu.make_async_copy(frames_ref.at[:, pl.ds(column, share)], held_ref, sem.at[1]),
            pltpu.make_async_copy(in_ref, in_vmem_ref, sem.at[2]),
            pltpu.make_async_copy(taps_ref, taps_vmem, sem.at[3]),
            pltpu.make_async_copy(gates_ref, gates_vmem, sem.at[4]),
        ]
        + [
            pltpu.make_async_copy(
                point_ref.at[:, b * lanes : (b + 1) * lanes],
                packed_ref.at[at + b * lanes : at + (b + 1) * lanes, :],
                sem.at[5 + b],
            )
            for b in range(point_ref.shape[1] // lanes)
        ]
    )
    names.wait()
    ids = ids_vmem[...]
    first = lax.axis_index("c") * slots
    expert = lax.broadcasted_iota(jnp.int32, (experts, count), 0)
    named = [jnp.where(expert == ids[k : k + 1, :], 1.0, 0.0) for k in range(2)]
    before = lax.broadcasted_iota(jnp.int32, (count, count), 0) < lax.broadcasted_iota(
        jnp.int32, (count, count), 1
    )
    rank = mm(
        jnp.concatenate(named, axis=0).astype(jnp.bfloat16),
        jnp.where(before, 1.0, 0.0).astype(jnp.bfloat16),
    )
    total = jnp.sum(named[0], axis=1, keepdims=True)
    place = [
        jnp.sum(named[0] * rank[:experts], axis=0, keepdims=True),
        jnp.sum(named[1] * (rank[experts:] + total), axis=0, keepdims=True),
    ]
    row = lax.broadcasted_iota(jnp.int32, (experts * slots, count), 0)
    chosen = None
    targets = []
    for k in range(2):
        local = place[k].astype(jnp.int32) - first
        target = jnp.where(
            (local >= 0) & (local < slots), ids[k : k + 1, :] * slots + local, -1
        )
        targets.append(target.astype(jnp.float32))
        hit = row == target
        chosen = hit if chosen is None else chosen | hit
    pick = jnp.where(chosen, 1.0, 0.0).astype(jnp.bfloat16)
    held.wait()
    out_ref[...] = mm(pick, held_ref[...]).astype(jnp.bfloat16)
    halves.wait()
    wide_ref[...] = in_vmem_ref[...].astype(jnp.float32)
    packed_ref[:half, :] = wide_ref[pl.ds(0, half, 2), :].astype(jnp.bfloat16)
    packed_ref[half:both, :] = wide_ref[pl.ds(1, half, 2), :].astype(jnp.bfloat16)
    kernel.wait()
    packed_ref[both:at, :] = jnp.concatenate(
        [taps_vmem[...].astype(jnp.float32), jnp.zeros((1, lanes), jnp.float32)], axis=0
    ).astype(jnp.bfloat16)
    gates.wait()
    table_ref[...] = jnp.concatenate(
        targets + [gates_vmem[...], jnp.zeros((4, count), jnp.float32)], axis=0
    )
    for copy in points:
        copy.wait()


def expert_kernel(x_ref, *refs):
    sources, out_ref, held, sem = refs[:6], refs[6], refs[7:13], refs[13]
    chunks, _, width = x_ref.shape
    units = held[0].shape[1]
    parts = [slice(i * width, (i + 1) * width) for i in range(units // width)]
    loads = {}
    for pair in range(2):
        for i, cols in enumerate(parts):
            for which in (3 * pair, 3 * pair + 1):
                at = sem.at[len(loads)]
                loads[which, i] = pltpu.make_async_copy(
                    sources[which].at[:, cols], held[which].at[:, cols], at
                )
    for which in (2, 5):
        loads[which, 0] = pltpu.make_async_copy(sources[which], held[which], sem.at[len(loads)])
    for copy in loads.values():
        copy.start()
    x = jnp.concatenate([x_ref[q] for q in range(chunks)], axis=1)
    hidden = []
    for pair in range(2):
        for i, cols in enumerate(parts):
            loads[3 * pair, i].wait()
            gate = mm(x, held[3 * pair][:, cols])
            loads[3 * pair + 1, i].wait()
            up = mm(x, held[3 * pair + 1][:, cols])
            hidden.append((gate * jax.nn.sigmoid(gate) * up).astype(jnp.bfloat16))
    hidden = jnp.concatenate(hidden, axis=1)
    loads[2, 0].wait()
    loads[5, 0].wait()
    for q in range(chunks):
        cols = slice(q * width, (q + 1) * width)
        total = mm(hidden[:, :units], held[2][:, cols]) + mm(hidden[:, units:], held[5][:, cols])
        out_ref[q] = total.astype(jnp.bfloat16)


def gather(quarters, cores, first, last, sources, out_ref, sem):
    y, c = lax.axis_index("y"), lax.axis_index("c")
    rows, cut = sources[0].shape[0], sources[3].shape[0]
    copies, order = {}, []
    for side in range(2):
        core = c if side == 0 else cores - 1 - c
        for i, (shift, start, stop) in enumerate(
            ((0, 0, rows), (quarters - 1, 0, rows), (1, 0, rows), (2, 0, cut), (2, cut, rows))
        ):
            block = 4 * side + min(i, 3)
            if block == len(order):
                order.append(lax.rem(y + shift, quarters) * cores + core)
                copies[block] = []
            low, high = max(first, start), min(last, stop)
            if low < high:
                copies[block].append(
                    pltpu.make_async_copy(
                        sources[5 * side + i].at[low - start : high - start, :],
                        out_ref.at[block, low - first : high - first, :],
                        sem.at[5 * side + i],
                    )
                )
                copies[block][-1].start()
    return copies, order


def combine_kernel(table_ref, rows_ref, out_ref):
    count = table_ref.shape[1]
    table = table_ref[...].T
    slot = lax.broadcasted_iota(jnp.int32, (count, rows_ref.shape[0]), 1)
    total = None
    for k in range(2):
        hit = slot == table[:, k : k + 1].astype(jnp.int32)
        picked = mm(jnp.where(hit, 1.0, 0.0).astype(jnp.bfloat16), rows_ref[...])
        picked = picked * table[:, 2 + k : 3 + k]
        total = picked if total is None else total + picked
    out_ref[...] = total.astype(jnp.bfloat16)


def norm_kernel(quarters, cores, frames_ref, *refs):
    parts_ref, gain_ref, bias_ref, res_ref, lo_ref, hi_ref, taps_ref, own_ref, held_ref, sem = refs[10:]
    own, width = own_ref.shape
    index = lax.axis_index("y") * cores + lax.axis_index("c")
    fetch = pltpu.make_async_copy(
        frames_ref.at[pl.ds(pl.multiple_of(index * own, own), own), :], own_ref, sem.at[10]
    )
    fetch.start()
    copies, order = gather(quarters, cores, 0, held_ref.shape[1], refs[:10], held_ref, sem)
    moe = jnp.concatenate(
        [
            parts_ref[2 * q].astype(jnp.float32) + parts_ref[2 * q + 1].astype(jnp.float32)
            for q in range(parts_ref.shape[0] // 2)
        ],
        axis=1,
    )
    fetch.wait()
    residual = own_ref[...].astype(jnp.float32) + moe
    res_ref[...] = residual
    centered = residual - jnp.mean(residual, axis=1, keepdims=True)
    variance = jnp.mean(centered * centered, axis=1, keepdims=True)
    normed = (centered / jnp.sqrt(variance + 1e-05) * gain_ref[...] + bias_ref[...]).astype(
        jnp.bfloat16
    )
    channels = held_ref.shape[2]
    half = lo_ref.shape[0]
    for block, index in enumerate(order):
        for copy in copies[block]:
            copy.wait()
        both = jnp.concatenate(
            [held_ref[block, :width, :], held_ref[block, width : 2 * width, :]], axis=1
        )
        projected = mm(normed, both)
        glu = projected[:, :channels] * jax.nn.sigmoid(projected[:, channels:])
        glu = glu.astype(jnp.bfloat16)
        cols = pl.ds(pl.multiple_of(index * channels, channels), channels)
        lo_ref[:, cols] = glu[:half]
        hi_ref[:, cols] = glu[half:]
        taps_ref[:, cols] = held_ref[block, 2 * width :, :].astype(jnp.float32)


def conv_kernel(quarters, cores, taps, *refs):
    left_ref, lo_ref, hi_ref, right_ref, taps_ref, res_ref, out_ref, act_ref, held_ref, sem = refs[10:]
    blocks, rows, channels = held_ref.shape
    last = refs[0].shape[0]
    copies, order = gather(quarters, cores, last - rows, last, refs[:10], held_ref, sem)
    half, width = lo_ref.shape
    count = 2 * half
    reach = (taps - 1) // 2
    for n in range(0, blocks, 2):
        cols = slice(n * channels, (n + 2) * channels)
        window = jnp.concatenate(
            [ref[:, cols] for ref in (left_ref, lo_ref, hi_ref, right_ref)], axis=0
        ).astype(jnp.float32)
        depth = None
        for turn in range(8):
            moved = pltpu.roll(window, 2 * count - turn, 0) if turn else window
            for j in range(taps):
                start = half - reach + j
                if start % 8 == turn:
                    term = moved[start - turn : start - turn + count] * taps_ref[j : j + 1, cols]
                    depth = term if depth is None else depth + term
        act_ref[:, cols] = (depth * jax.nn.sigmoid(depth)).astype(jnp.bfloat16)
    acts, points = [], []
    for block, index in enumerate(order):
        for copy in copies[block]:
            copy.wait()
        acts.append(act_ref[:, pl.ds(pl.multiple_of(index * channels, channels), channels)])
        points.append(
            jnp.concatenate(
                [held_ref[block, b * channels : (b + 1) * channels, :] for b in range(blocks)],
                axis=1,
            )
        )
    total = res_ref[...] + mm(jnp.concatenate(acts, axis=1), jnp.concatenate(points, axis=0))
    out_ref[...] = total.astype(jnp.bfloat16)


def shards(
    frames,
    expert_ids,
    gate_values,
    w_gate,
    w_up,
    w_down,
    norm_gain,
    norm_bias,
    point_in,
    depth_kernel,
    point_out,
):
    count, width = frames.shape
    wide = lax.axis_size("x") * lax.axis_size("z")
    quarters, cores = lax.axis_size("y"), lax.axis_size("c")
    narrow = quarters * cores
    experts = w_gate.shape[0] * wide
    slots = 2 * expert_ids.shape[1] * count // experts // cores
    share = width // quarters
    own = count // narrow
    taps, channels = depth_kernel.shape
    params = pltpu.CompilerParams(vmem_limit_bytes=VMEM_BYTES)

    in_hbm = lambda n: [pl.BlockSpec(memory_space=pltpu.HBM)] * n
    far = lambda array: pltpu.with_memory_space_constraint(array, pltpu.HBM)
    frames = far(frames)

    mine = [w_gate[0], w_up[0], w_down[0]]
    swap = [(i, cores - 1 - i) for i in range(cores)]
    theirs = [lax.ppermute(w, "c", swap) for w in mine]

    rows = experts * slots
    packed_rows = 3 * width + taps + 1
    outgoing, table, packed = pl.pallas_call(
        lambda *refs: prepare_kernel(experts, slots, *refs),
        in_specs=in_hbm(6),
        out_specs=in_vmem(3),
        out_shape=[
            jax.ShapeDtypeStruct((rows, share), jnp.bfloat16),
            jax.ShapeDtypeStruct((8, count), jnp.float32),
            jax.ShapeDtypeStruct((packed_rows, channels), jnp.bfloat16),
        ],
        scratch_shapes=[
            pltpu.VMEM((count, share), jnp.bfloat16),
            pltpu.VMEM((2, count), jnp.int32),
            pltpu.VMEM((2, count), jnp.float32),
            pltpu.VMEM((2 * width, channels), jnp.bfloat16),
            pltpu.VMEM((taps, channels), jnp.bfloat16),
            pltpu.VMEM((2 * width, channels), jnp.float32),
            pltpu.SemaphoreType.DMA((5 + narrow,)),
        ],
        compiler_params=params,
        name="prepare",
    )(
        far(expert_ids.T),
        frames,
        far(point_in.reshape(2 * width, channels)),
        far(depth_kernel),
        far(point_out),
        far(gate_values.T),
    )

    ahead = [(i, (i + 1) % quarters) for i in range(quarters)]
    behind = [((i + 1) % quarters, i) for i in range(quarters)]
    before = lax.ppermute(packed, "y", ahead)
    after = lax.ppermute(packed, "y", behind)

    def over(axis, cells):
        return lax.all_to_all(cells, axis, split_axis=0, concat_axis=0, tiled=True)

    arrived = over(WIDE, outgoing.reshape(experts, slots, share)).reshape(1, rows, share)
    x = over("y", jnp.broadcast_to(arrived, (quarters, rows, share)))
    weights = mine + theirs
    partial = pl.pallas_call(
        expert_kernel,
        in_specs=in_vmem(1) + in_hbm(6),
        out_specs=pl.BlockSpec(memory_space=pltpu.VMEM),
        out_shape=jax.ShapeDtypeStruct((quarters, rows, share), jnp.bfloat16),
        scratch_shapes=[pltpu.VMEM(w.shape, w.dtype) for w in weights]
        + [pltpu.SemaphoreType.DMA((4 * w_gate.shape[2] // share + 2,))],
        compiler_params=params,
        name="experts",
    )(x, *[far(w) for w in weights])
    partial = over("y", partial)
    summed = jnp.sum(partial.astype(jnp.float32), axis=0).astype(jnp.bfloat16)
    summed, packed, before, after = lax.optimization_barrier((summed, packed, before, after))
    cut = packed_rows // 2
    held = [
        packed,
        before,
        after,
        lax.ppermute(before[:cut], "y", ahead),
        lax.ppermute(after[cut:], "y", behind),
    ]
    held = held + [lax.ppermute(cells, "c", swap) for cells in held]
    returned = over(WIDE, summed.reshape(experts, slots, share)).reshape(rows, share)
    mixed = pl.pallas_call(
        combine_kernel,
        in_specs=in_vmem(2),
        out_specs=pl.BlockSpec(memory_space=pltpu.VMEM),
        out_shape=jax.ShapeDtypeStruct((count, share), jnp.bfloat16),
        compiler_params=params,
        name="combine",
    )(table, returned)
    held = [far(cells) for cells in held]
    parts = over(NARROW, mixed.reshape(narrow, own, share))

    half = own // 2
    residual, lo, hi, kernel = pl.pallas_call(
        lambda *refs: norm_kernel(quarters, cores, *refs),
        in_specs=in_hbm(11) + in_vmem(3),
        out_specs=in_vmem(4),
        out_shape=[
            jax.ShapeDtypeStruct((own, width), jnp.float32),
            jax.ShapeDtypeStruct((half, width), jnp.bfloat16),
            jax.ShapeDtypeStruct((half, width), jnp.bfloat16),
            jax.ShapeDtypeStruct((taps + 1, width), jnp.float32),
        ],
        scratch_shapes=[
            pltpu.VMEM((own, width), jnp.bfloat16),
            pltpu.VMEM((narrow, packed_rows - width, channels), jnp.bfloat16),
            pltpu.SemaphoreType.DMA((11,)),
        ],
        compiler_params=params,
        name="norm_glu",
    )(frames, *held, parts, norm_gain[None, :], norm_bias[None, :])

    ends = wide * narrow - 1
    left = lax.ppermute(hi, EVERY, [(i, i + 1) for i in range(ends)])
    right = lax.ppermute(lo, EVERY, [(i + 1, i) for i in range(ends)])
    return pl.pallas_call(
        lambda *refs: conv_kernel(quarters, cores, taps, *refs),
        in_specs=in_hbm(10) + in_vmem(6),
        out_specs=pl.BlockSpec(memory_space=pltpu.VMEM),
        out_shape=jax.ShapeDtypeStruct((own, width), jnp.bfloat16),
        scratch_shapes=[
            pltpu.VMEM((own, width), jnp.bfloat16),
            pltpu.VMEM((narrow, width, channels), jnp.bfloat16),
            pltpu.SemaphoreType.DMA((10,)),
        ],
        compiler_params=params,
        name="conv",
    )(*held, left, lo, hi, right, kernel, residual)


def solution(mesh):
    chips = Mesh(mesh.devices.reshape(4, 16, 4, 2), EVERY)
    return jax.shard_map(
        shards,
        mesh=chips,
        in_specs=(
            P(WIDE, None),
            P(WIDE, None),
            P(WIDE, None),
            P(WIDE, None, NARROW),
            P(WIDE, None, NARROW),
            P(WIDE, NARROW, None),
            P(),
            P(),
            P(None, None, NARROW),
            P(None, NARROW),
            P(NARROW, None),
        ),
        out_specs=P(EVERY, None),
        check_vma=False,
    )
```

time: 155 us -> 146 us (0.942)
  blocking collectives: 55.7 us -> 16.6 us
  starting transfers between devices: 39.3 us -> 74.4 us
  between operations: 13.6 us -> 0.31 us
  waiting for transfers between devices: 28.9 us -> 34.3 us
  Pallas kernels: 15.7 us -> 17.3 us
    all_to_all x3 -> x1, blocking collectives: 55.7 us -> 16.6 us  [over(): return lax.all_to_all(cells, axis, split_axis=0, concat_axis=0, tiled=True)]
    ppermute x0 -> x9, starting transfers between devices: none -> 23.5 us  [the longest x5 10.6 us: shards(): held = held + [lax.ppermute(cells, 'c', swap) for cells in held]]
    all_to_all x2 -> x4, starting transfers between devices: 23.3 us -> 34.9 us  [over(): return lax.all_to_all(cells, axis, split_axis=0, concat_axis=0, tiled=True)]
    all_to_all x2 -> x4, waiting for transfers between devices: 27.3 us -> 32.4 us  [over(): return lax.all_to_all(cells, axis, split_axis=0, concat_axis=0, tiled=True)]
    pallas_call x1, Pallas kernels: 5.43 us -> 7.92 us  [shards(): pl.pallas_call(expert_kernel, in_specs=in_vmem(1) + in_hbm(6), out_specs=...]
    pallas_call x5 -> x4, Pallas kernels: 10.3 us -> 9.39 us  [the longest x1 3.32 us: shards(): pl.pallas_call(lambda *refs: norm_kernel(quarters, cores, *refs), in_spec...]
  transfers between devices with their start and end apart: 9 -> 18, of which waited for: 3 -> 6; matrix products, arithmetic and copies ran while one was open for 1% -> 1% of each run, Pallas kernels for 7% -> 6%
where the time goes in v3:
time: 146 us; the launch traced here: 145 us
  starting transfers between devices  74.4 us (51%)
  waiting for transfers between devices  34.3 us (23%)
  Pallas kernels  17.3 us (12%)
  blocking collectives  16.6 us (11%)
    all_to_all x4, starting transfers between devices, over(): return lax.all_to_all(cells, axis, split_axis=0, concat_axis=0, tiled=True)  34.9 us
    all_to_all x4, waiting for transfers between devices, over(): return lax.all_to_all(cells, axis, split_axis=0, concat_axis=0, tiled=True)  32.4 us
    all_to_all x1, blocking collectives, over(): return lax.all_to_all(cells, axis, split_axis=0, concat_axis=0, tiled=True)  16.6 us
    ppermute x5, starting transfers between devices, shards(): held = held + [lax.ppermute(cells, 'c', swap) for cells in held]  10.6 us
    pallas_call x1, Pallas kernels, shards(): pl.pallas_call(expert_kernel, in_specs=in_vmem(1) + in_hbm(6), out_specs=...  7.92 us
    ppermute x1, starting transfers between devices, shards(): right = lax.ppermute(lo, EVERY, [(i + 1, i) for i in range(ends)])  7.86 us
    ppermute x3, starting transfers between devices, shards(): theirs = [lax.ppermute(w, 'c', swap) for w in mine]  6.26 us
    ppermute x1, starting transfers between devices, shards(): after = lax.ppermute(packed, 'y', behind)  5.13 us
  transfers between devices with their start and end apart: 18, of which 6 were waited for; matrix products, arithmetic and copies ran while one was open for 1% of the time, Pallas kernels for 6%

profile of v3, /device:TPU:6, one launch (start us, length us, event | category | flops | bytes accessed | tf_op | source)
XLA Modules:
  0.0 144.9 jit_solution(13527876071513022621)
XLA Ops:
  0.0 2.2 %prepare.1 = (bf16[512,256]{1,0:T(8,128)(2,1)}, f32[8,256]{1,0:T(8,128)S(1)}, bf16[3104,128]{1,0:T(8,128)(2,1)S(1)}) custom-call(s32[2,256]{1,0:T(2,128)} %bitcast.19, bf16[256,1024]{1,0:T(8,128)(2,1)} %refs_0_.1, bf16[2048,128]{1,0:T(8,128)(2,1)} %bitcast.18, bf16[31,128]{1,0:T(8,128)(2,1)} %refs_3_.1, bf16[128,1024]{1,0:T(8,128)(2,1)} %refs_4_.1, ...), custom_call_target="tpu_custom_call" | custom-call | tf_op jit(solution)/shard_map/prepare/pallas_call | solution.py:305
  2.2 0.0 copy-start
  2.2 18.8 %all-to-all-start = ((bf16[64,8,256]{2,1,0:T(8,128)(2,1)}), bf16[64,8,256]{2,1,0:T(8,128)(2,1)S(1)}, u32[]{:S(2)}, u32[]{:S(2)}) async-start(bf16[64,8,256]{2,1,0:T(8,128)(2,1)} %bitcast.3), calls=%async_computation | async-start | bytes 524288 | tf_op jit(solution)/shard_map/all_to_all | solution.py:340
  21.0 1.9 %collective-permute-start = (bf16[1024,512]{1,0:T(8,128)(2,1)}, bf16[1024,512]{1,0:T(8,128)(2,1)}, u32[]{:S(2)}, u32[]{:S(2)}) collective-permute-start(bf16[1024,512]{1,0:T(8,128)(2,1)} %bitcast.5.refs_0_), channel_id=1, source_target_pairs={{0,1},{1,0},{2,3},{3,2},{4,5},{5,4},{6,7},{7,6},{8,9},{9,8},{10,11... | collective-permute-start | bytes 3145736 | tf_op jit(solution)/shard_map/ppermute | solution.py:301
  23.0 2.4 %collective-permute-start.1 = (bf16[1024,512]{1,0:T(8,128)(2,1)}, bf16[1024,512]{1,0:T(8,128)(2,1)}, u32[]{:S(2)}, u32[]{:S(2)}) collective-permute-start(bf16[1024,512]{1,0:T(8,128)(2,1)} %bitcast.6.refs_1_), channel_id=1, source_target_pairs={{0,1},{1,0},{2,3},{3,2},{4,5},{5,4},{6,7},{7,6},{8,9},{9,8},{10,11... | collective-permute-start | bytes 3145736 | tf_op jit(solution)/shard_map/ppermute | solution.py:301
  25.4 1.9 %collective-permute-start.2 = (bf16[512,1024]{1,0:T(8,128)(2,1)}, bf16[512,1024]{1,0:T(8,128)(2,1)}, u32[]{:S(2)}, u32[]{:S(2)}) collective-permute-start(bf16[512,1024]{1,0:T(8,128)(2,1)} %bitcast.7.refs_2_), channel_id=1, source_target_pairs={{0,1},{1,0},{2,3},{3,2},{4,5},{5,4},{6,7},{7,6},{8,9},{9,8},{10,11... | collective-permute-start | bytes 3145736 | tf_op jit(solution)/shard_map/ppermute | solution.py:301
  27.3 14.5 %all-to-all-done = bf16[64,8,256]{2,1,0:T(8,128)(2,1)S(1)} async-done(((bf16[64,8,256]{2,1,0:T(8,128)(2,1)}), bf16[64,8,256]{2,1,0:T(8,128)(2,1)S(1)}, u32[]{:S(2)}, u32[]{:S(2)}) %all-to-all-start) | async-done | bytes 262176 | tf_op jit(solution)/shard_map/all_to_all | solution.py:340
  41.9 1.0 broadcast_in_dim.14
  42.9 4.5 %all-to-all-start.1 = ((bf16[4,512,256]{2,1,0:T(8,128)(2,1)}), bf16[4,512,256]{2,1,0:T(8,128)(2,1)S(1)}, u32[]{:S(2)}, u32[]{:S(2)}) async-start(bf16[4,512,256]{2,1,0:T(8,128)(2,1)} %broadcast_in_dim.14), calls=%async_computation.1 | async-start | bytes 2097152 | tf_op jit(solution)/shard_map/all_to_all | solution.py:340
  47.4 5.1 %collective-permute-start.4 = (bf16[3104,128]{1,0:T(8,128)(2,1)S(1)}, bf16[3104,128]{1,0:T(8,128)(2,1)S(1)}, u32[]{:S(2)}, u32[]{:S(2)}) collective-permute-start(bf16[3104,128]{1,0:T(8,128)(2,1)S(1)} %get-tuple-element.18.refs_1_.refs_0_), channel_id=1, source_target_pairs={{2,0},{4,2},{6,4},{0,6},{3,1},{5,3},{7,5},{1,7},{10,8},{12,10},{14... | collective-permute-start | bytes 2383880 | tf_op jit(solution)/shard_map/ppermute | solution.py:337
  52.5 1.9 %collective-permute-start.3 = (bf16[3104,128]{1,0:T(8,128)(2,1)S(1)}, bf16[3104,128]{1,0:T(8,128)(2,1)S(1)}, u32[]{:S(2)}, u32[]{:S(2)}) collective-permute-start(bf16[3104,128]{1,0:T(8,128)(2,1)S(1)} %get-tuple-element.18.refs_1_.refs_0_), channel_id=1, source_target_pairs={{0,2},{2,4},{4,6},{6,0},{1,3},{3,5},{5,7},{7,1},{8,10},{10,12},{12... | collective-permute-start | bytes 2383880 | tf_op jit(solution)/shard_map/ppermute | solution.py:336
  54.4 0.0 collective-permute-done.refs_3_
  54.4 0.0 collective-permute-done.1.refs_4_
  54.4 0.0 collective-permute-done.2.refs_5_
  54.5 9.5 %all-to-all-done.1.x_ref = bf16[4,512,256]{2,1,0:T(8,128)(2,1)S(1)} async-done(((bf16[4,512,256]{2,1,0:T(8,128)(2,1)}), bf16[4,512,256]{2,1,0:T(8,128)(2,1)S(1)}, u32[]{:S(2)}, u32[]{:S(2)}) %all-to-all-start.1) | async-done | bytes 1048608 | tf_op jit(solution)/shard_map/all_to_all | solution.py:340
  63.9 7.9 %experts.1 = bf16[4,512,256]{2,1,0:T(8,128)(2,1)S(1)} custom-call(bf16[4,512,256]{2,1,0:T(8,128)(2,1)S(1)} %all-to-all-done.1.x_ref, bf16[1024,512]{1,0:T(8,128)(2,1)} %bitcast.5.refs_0_, bf16[1024,512]{1,0:T(8,128)(2,1)} %bitcast.6.refs_1_, bf16[512,1024]{1,0:T(8,128)(2,1)} %bitcast.7.refs_2_, bf16[1024,512]{1,0:T(8,128)(2,1)} %collective-permute-done.refs_3_, ...), custom_call_target="tpu_custom_call" | custom-call | tf_op jit(solution)/shard_map/experts/pallas_call | solution.py:345
  71.9 16.6 %all_to_all.25 = bf16[4,512,256]{2,1,0:T(8,128)(2,1)S(1)} all-to-all(bf16[4,512,256]{2,1,0:T(8,128)(2,1)S(1)} %experts.1), channel_id=1, replica_groups=mesh['x'=4,'z'=16,'y'=4,'c'=2] {'y'}, dimensions={0} | all-to-all | bytes 2097152 | tf_op jit(solution)/shard_map/all_to_all | solution.py:340
  88.5 0.9 reduce_sum.12
  89.4 0.0 collective-permute-done.4.refs_3_.refs_2_
  89.4 0.0 collective-permute-done.3.refs_2_.refs_1_
  89.4 8.1 %all-to-all-start.3 = ((bf16[64,8,256]{2,1,0:T(8,128)(2,1)}), bf16[64,8,256]{2,1,0:T(8,128)(2,1)S(1)}, u32[]{:S(2)}, u32[]{:S(2)}) async-start(bf16[64,8,256]{2,1,0:T(8,128)(2,1)} %bitcast.16), calls=%async_computation.3 | async-start | bytes 524288 | tf_op jit(solution)/shard_map/all_to_all | solution.py:340
  97.6 3.1 %collective-permute-start.6 = (bf16[1552,128]{1,0:T(8,128)(2,1)S(1)}, bf16[1552,128]{1,0:T(8,128)(2,1)S(1)}, u32[]{:S(2)}, u32[]{:S(2)}) collective-permute-start(bf16[1552,128]{1,0:T(8,128)(2,1)S(1)} %slice.7), channel_id=1, source_target_pairs={{2,0},{4,2},{6,4},{0,6},{3,1},{5,3},{7,5},{1,7},{10,8},{12,10},{14... | collective-permute-start | bytes 1191944 | tf_op jit(solution)/shard_map/ppermute | solution.py:364
  100.7 2.8 %collective-permute-start.5 = (bf16[1552,128]{1,0:T(8,128)(2,1)S(1)}, bf16[1552,128]{1,0:T(8,128)(2,1)}, u32[]{:S(2)}, u32[]{:S(2)}) collective-permute-start(bf16[1552,128]{1,0:T(8,128)(2,1)S(1)} %slice.6), channel_id=1, source_target_pairs={{0,2},{2,4},{4,6},{6,0},{1,3},{3,5},{5,7},{7,1},{8,10},{10,12},{12... | collective-permute-start | bytes 1191944 | tf_op jit(solution)/shard_map/ppermute | solution.py:363
  103.5 0.0 copy-done
  103.5 1.9 %collective-permute-start.7 = (bf16[3104,128]{1,0:T(8,128)(2,1)S(1)}, bf16[3104,128]{1,0:T(8,128)(2,1)}, u32[]{:S(2)}, u32[]{:S(2)}) collective-permute-start(bf16[3104,128]{1,0:T(8,128)(2,1)S(1)} %get-tuple-element.18.refs_1_.refs_0_), channel_id=1, source_target_pairs={{0,1},{1,0},{2,3},{3,2},{4,5},{5,4},{6,7},{7,6},{8,9},{9,8},{10,11... | collective-permute-start | bytes 2383880 | tf_op jit(solution)/shard_map/ppermute | solution.py:366
  105.4 0.0 copy-done.4
  105.4 2.4 %collective-permute-start.8 = (bf16[3104,128]{1,0:T(8,128)(2,1)S(1)}, bf16[3104,128]{1,0:T(8,128)(2,1)}, u32[]{:S(2)}, u32[]{:S(2)}) collective-permute-start(bf16[3104,128]{1,0:T(8,128)(2,1)S(1)} %collective-permute-done.3.refs_2_.refs_1_), channel_id=1, source_target_pairs={{0,1},{1,0},{2,3},{3,2},{4,5},{5,4},{6,7},{7,6},{8,9},{9,8},{10,11... | collective-permute-start | bytes 2383880 | tf_op jit(solution)/shard_map/ppermute | solution.py:366
  107.8 0.0 copy-done.3
  107.8 1.9 %collective-permute-start.9 = (bf16[3104,128]{1,0:T(8,128)(2,1)S(1)}, bf16[3104,128]{1,0:T(8,128)(2,1)}, u32[]{:S(2)}, u32[]{:S(2)}) collective-permute-start(bf16[3104,128]{1,0:T(8,128)(2,1)S(1)} %collective-permute-done.4.refs_3_.refs_2_), channel_id=1, source_target_pairs={{0,1},{1,0},{2,3},{3,2},{4,5},{5,4},{6,7},{7,6},{8,9},{9,8},{10,11... | collective-permute-start | bytes 2383880 | tf_op jit(solution)/shard_map/ppermute | solution.py:366
  109.8 0.0 collective-permute-done.6.refs_5_.refs_4_
  109.8 2.4 %collective-permute-start.11 = (bf16[1552,128]{1,0:T(8,128)(2,1)S(1)}, bf16[1552,128]{1,0:T(8,128)(2,1)}, u32[]{:S(2)}, u32[]{:S(2)}) collective-permute-start(bf16[1552,128]{1,0:T(8,128)(2,1)S(1)} %collective-permute-done.6.refs_5_.refs_4_), channel_id=1, source_target_pairs={{0,1},{1,0},{2,3},{3,2},{4,5},{5,4},{6,7},{7,6},{8,9},{9,8},{10,11... | collective-permute-start | bytes 1191944 | tf_op jit(solution)/shard_map/ppermute | solution.py:366
  112.2 0.2 collective-permute-done.5.refs_4_.refs_3_
  112.5 1.9 %collective-permute-start.10 = (bf16[1552,128]{1,0:T(8,128)(2,1)}, bf16[1552,128]{1,0:T(8,128)(2,1)}, u32[]{:S(2)}, u32[]{:S(2)}) collective-permute-start(bf16[1552,128]{1,0:T(8,128)(2,1)} %collective-permute-done.5.refs_4_.refs_3_), channel_id=1, source_target_pairs={{0,1},{1,0},{2,3},{3,2},{4,5},{5,4},{6,7},{7,6},{8,9},{9,8},{10,11... | collective-permute-start | bytes 1191944 | tf_op jit(solution)/shard_map/ppermute | solution.py:366
  114.4 2.4 %all-to-all-done.3 = bf16[64,8,256]{2,1,0:T(8,128)(2,1)S(1)} async-done(((bf16[64,8,256]{2,1,0:T(8,128)(2,1)}), bf16[64,8,256]{2,1,0:T(8,128)(2,1)S(1)}, u32[]{:S(2)}, u32[]{:S(2)}) %all-to-all-start.3) | async-done | bytes 262176 | tf_op jit(solution)/shard_map/all_to_all | solution.py:340
  116.8 1.2 combine.1
  118.0 3.5 %all-to-all-start.4 = ((bf16[8,32,256]{2,1,0:T(8,128)(2,1)}), bf16[8,32,256]{2,1,0:T(8,128)(2,1)S(1)}, u32[]{:S(2)}, u32[]{:S(2)}) async-start(bf16[8,32,256]{2,1,0:T(8,128)(2,1)} %bitcast.10), calls=%async_computation.4 | async-start | bytes 262144 | tf_op jit(solution)/shard_map/all_to_all | solution.py:340
  121.5 0.0 collective-permute-done.11.refs_10_.refs_9_
  121.5 0.0 collective-permute-done.10.refs_9_.refs_8_
  121.5 0.0 collective-permute-done.7.refs_6_.refs_5_
  121.5 0.0 collective-permute-done.8.refs_7_.refs_6_
  121.5 0.0 collective-permute-done.9.refs_8_.refs_7_
  121.5 6.0 %all-to-all-done.4.refs_11_ = bf16[8,32,256]{2,1,0:T(8,128)(2,1)S(1)} async-done(((bf16[8,32,256]{2,1,0:T(8,128)(2,1)}), bf16[8,32,256]{2,1,0:T(8,128)(2,1)S(1)}, u32[]{:S(2)}, u32[]{:S(2)}) %all-to-all-start.4) | async-done | bytes 131104 | tf_op jit(solution)/shard_map/all_to_all | solution.py:340
  127.5 3.3 %norm_glu.1 = (f32[32,1024]{1,0:T(8,128)S(1)}, bf16[16,1024]{1,0:T(8,128)(2,1)S(1)}, bf16[16,1024]{1,0:T(8,128)(2,1)S(1)}, f32[32,1024]{1,0:T(8,128)S(1)}) custom-call(bf16[256,1024]{1,0:T(8,128)(2,1)} %refs_0_.1, bf16[3104,128]{1,0:T(8,128)(2,1)} %copy-done, bf16[3104,128]{1,0:T(8,128)(2,1)} %copy-done.4, bf16[3104,128]{1,0:T(8,128)(2,1)} %copy-done.3, ...), custom_call_target="tpu_custom_call" | custom-call | tf_op jit(solution)/shard_map/norm_glu/pallas_call | solution.py:380
  130.9 1.9 %collective-permute-start.12 = (bf16[16,1024]{1,0:T(8,128)(2,1)S(1)}, bf16[16,1024]{1,0:T(8,128)(2,1)S(1)}, u32[]{:S(2)}, u32[]{:S(2)}) collective-permute-start(bf16[16,1024]{1,0:T(8,128)(2,1)S(1)} %get-tuple-element.23.refs_12_), channel_id=1, source_target_pairs={{0,1},{1,2},{2,3},{3,4},{4,5},{5,6},{6,7},{7,8},{8,9},{9,10},{10,1... | collective-permute-start | bytes 98312 | tf_op jit(solution)/shard_map/ppermute | solution.py:400
  132.8 7.9 %collective-permute-start.13 = (bf16[16,1024]{1,0:T(8,128)(2,1)S(1)}, bf16[16,1024]{1,0:T(8,128)(2,1)S(1)}, u32[]{:S(2)}, u32[]{:S(2)}) collective-permute-start(bf16[16,1024]{1,0:T(8,128)(2,1)S(1)} %get-tuple-element.24.refs_11_), channel_id=1, source_target_pairs={{1,0},{2,1},{3,2},{4,3},{5,4},{6,5},{7,6},{8,7},{9,8},{10,9},{11,1... | collective-permute-start | bytes 98312 | tf_op jit(solution)/shard_map/ppermute | solution.py:401
  140.7 0.0 collective-permute-done.12.refs_10_
  140.7 1.6 %collective-permute-done.13.refs_13_ = bf16[16,1024]{1,0:T(8,128)(2,1)S(1)} collective-permute-done((bf16[16,1024]{1,0:T(8,128)(2,1)S(1)}, bf16[16,1024]{1,0:T(8,128)(2,1)S(1)}, u32[]{:S(2)}, u32[]{:S(2)}) %collective-permute-start.13) | collective-permute-done | bytes 32800 | tf_op jit(solution)/shard_map/ppermute | solution.py:401
  142.2 2.7 %conv.1 = bf16[32,1024]{1,0:T(8,128)(2,1)} custom-call(bf16[3104,128]{1,0:T(8,128)(2,1)} %copy-done, bf16[3104,128]{1,0:T(8,128)(2,1)} %copy-done.4, bf16[3104,128]{1,0:T(8,128)(2,1)} %copy-done.3, bf16[1552,128]{1,0:T(8,128)(2,1)} %collective-permute-done.5.refs_4_.refs_3_, bf16[1552,128]{1,0:T(8,128)(2,1)} %copy-done.5, ...), custom_call_target="tpu_custom_call" | custom-call | tf_op jit(solution)/shard_map/conv/pallas_call | solution.py:402
  (10 shorter events, 0.1 us)
Async XLA Ops:
  2.2 101.3 %copy-start = (bf16[3104,128]{1,0:T(8,128)(2,1)}, bf16[3104,128]{1,0:T(8,128)(2,1)S(1)}, u32[]{:S(2)}) copy-start(bf16[3104,128]{1,0:T(8,128)(2,1)S(1)} %get-tuple-element.18.refs_1_.refs_0_) | copy-start | bytes 2383876
  2.2 39.6 %all-to-all-start = ((bf16[64,8,256]{2,1,0:T(8,128)(2,1)}), bf16[64,8,256]{2,1,0:T(8,128)(2,1)S(1)}, u32[]{:S(2)}, u32[]{:S(2)}) async-start(bf16[64,8,256]{2,1,0:T(8,128)(2,1)} %bitcast.3), calls=%async_computation | async-start | bytes 524288 | tf_op jit(solution)/shard_map/all_to_all | solution.py:340
  21.0 33.4 %collective-permute-start = (bf16[1024,512]{1,0:T(8,128)(2,1)}, bf16[1024,512]{1,0:T(8,128)(2,1)}, u32[]{:S(2)}, u32[]{:S(2)}) collective-permute-start(bf16[1024,512]{1,0:T(8,128)(2,1)} %bitcast.5.refs_0_), channel_id=1, source_target_pairs={{0,1},{1,0},{2,3},{3,2},{4,5},{5,4},{6,7},{7,6},{8,9},{9,8},{10,11... | collective-permute-start | bytes 3145736 | tf_op jit(solution)/shard_map/ppermute | solution.py:301
  23.0 31.5 %collective-permute-start.1 = (bf16[1024,512]{1,0:T(8,128)(2,1)}, bf16[1024,512]{1,0:T(8,128)(2,1)}, u32[]{:S(2)}, u32[]{:S(2)}) collective-permute-start(bf16[1024,512]{1,0:T(8,128)(2,1)} %bitcast.6.refs_1_), channel_id=1, source_target_pairs={{0,1},{1,0},{2,3},{3,2},{4,5},{5,4},{6,7},{7,6},{8,9},{9,8},{10,11... | collective-permute-start | bytes 3145736 | tf_op jit(solution)/shard_map/ppermute | solution.py:301
  25.4 29.1 %collective-permute-start.2 = (bf16[512,1024]{1,0:T(8,128)(2,1)}, bf16[512,1024]{1,0:T(8,128)(2,1)}, u32[]{:S(2)}, u32[]{:S(2)}) collective-permute-start(bf16[512,1024]{1,0:T(8,128)(2,1)} %bitcast.7.refs_2_), channel_id=1, source_target_pairs={{0,1},{1,0},{2,3},{3,2},{4,5},{5,4},{6,7},{7,6},{8,9},{9,8},{10,11... | collective-permute-start | bytes 3145736 | tf_op jit(solution)/shard_map/ppermute | solution.py:301
  42.9 21.0 %all-to-all-start.1 = ((bf16[4,512,256]{2,1,0:T(8,128)(2,1)}), bf16[4,512,256]{2,1,0:T(8,128)(2,1)S(1)}, u32[]{:S(2)}, u32[]{:S(2)}) async-start(bf16[4,512,256]{2,1,0:T(8,128)(2,1)} %broadcast_in_dim.14), calls=%async_computation.1 | async-start | bytes 2097152 | tf_op jit(solution)/shard_map/all_to_all | solution.py:340
  47.4 42.0 %collective-permute-start.4 = (bf16[3104,128]{1,0:T(8,128)(2,1)S(1)}, bf16[3104,128]{1,0:T(8,128)(2,1)S(1)}, u32[]{:S(2)}, u32[]{:S(2)}) collective-permute-start(bf16[3104,128]{1,0:T(8,128)(2,1)S(1)} %get-tuple-element.18.refs_1_.refs_0_), channel_id=1, source_target_pairs={{2,0},{4,2},{6,4},{0,6},{3,1},{5,3},{7,5},{1,7},{10,8},{12,10},{14... | collective-permute-start | bytes 2383880 | tf_op jit(solution)/shard_map/ppermute | solution.py:337
  52.5 36.9 %collective-permute-start.3 = (bf16[3104,128]{1,0:T(8,128)(2,1)S(1)}, bf16[3104,128]{1,0:T(8,128)(2,1)S(1)}, u32[]{:S(2)}, u32[]{:S(2)}) collective-permute-start(bf16[3104,128]{1,0:T(8,128)(2,1)S(1)} %get-tuple-element.18.refs_1_.refs_0_), channel_id=1, source_target_pairs={{0,2},{2,4},{4,6},{6,0},{1,3},{3,5},{5,7},{7,1},{8,10},{10,12},{12... | collective-permute-start | bytes 2383880 | tf_op jit(solution)/shard_map/ppermute | solution.py:336
  89.4 18.5 %copy-start.3 = (bf16[3104,128]{1,0:T(8,128)(2,1)}, bf16[3104,128]{1,0:T(8,128)(2,1)S(1)}, u32[]{:S(2)}) copy-start(bf16[3104,128]{1,0:T(8,128)(2,1)S(1)} %collective-permute-done.4.refs_3_.refs_2_) | copy-start | bytes 2383876
  89.4 16.0 %copy-start.4 = (bf16[3104,128]{1,0:T(8,128)(2,1)}, bf16[3104,128]{1,0:T(8,128)(2,1)S(1)}, u32[]{:S(2)}) copy-start(bf16[3104,128]{1,0:T(8,128)(2,1)S(1)} %collective-permute-done.3.refs_2_.refs_1_) | copy-start | bytes 2383876
  89.4 27.4 %all-to-all-start.3 = ((bf16[64,8,256]{2,1,0:T(8,128)(2,1)}), bf16[64,8,256]{2,1,0:T(8,128)(2,1)S(1)}, u32[]{:S(2)}, u32[]{:S(2)}) async-start(bf16[64,8,256]{2,1,0:T(8,128)(2,1)} %bitcast.16), calls=%async_computation.3 | async-start | bytes 524288 | tf_op jit(solution)/shard_map/all_to_all | solution.py:340
  97.6 12.2 %collective-permute-start.6 = (bf16[1552,128]{1,0:T(8,128)(2,1)S(1)}, bf16[1552,128]{1,0:T(8,128)(2,1)S(1)}, u32[]{:S(2)}, u32[]{:S(2)}) collective-permute-start(bf16[1552,128]{1,0:T(8,128)(2,1)S(1)} %slice.7), channel_id=1, source_target_pairs={{2,0},{4,2},{6,4},{0,6},{3,1},{5,3},{7,5},{1,7},{10,8},{12,10},{14... | collective-permute-start | bytes 1191944 | tf_op jit(solution)/shard_map/ppermute | solution.py:364
  100.7 11.8 %collective-permute-start.5 = (bf16[1552,128]{1,0:T(8,128)(2,1)S(1)}, bf16[1552,128]{1,0:T(8,128)(2,1)}, u32[]{:S(2)}, u32[]{:S(2)}) collective-permute-start(bf16[1552,128]{1,0:T(8,128)(2,1)S(1)} %slice.6), channel_id=1, source_target_pairs={{0,2},{2,4},{4,6},{6,0},{1,3},{3,5},{5,7},{7,1},{8,10},{10,12},{12... | collective-permute-start | bytes 1191944 | tf_op jit(solution)/shard_map/ppermute | solution.py:363
  103.5 18.0 %collective-permute-start.7 = (bf16[3104,128]{1,0:T(8,128)(2,1)S(1)}, bf16[3104,128]{1,0:T(8,128)(2,1)}, u32[]{:S(2)}, u32[]{:S(2)}) collective-permute-start(bf16[3104,128]{1,0:T(8,128)(2,1)S(1)} %get-tuple-element.18.refs_1_.refs_0_), channel_id=1, source_target_pairs={{0,1},{1,0},{2,3},{3,2},{4,5},{5,4},{6,7},{7,6},{8,9},{9,8},{10,11... | collective-permute-start | bytes 2383880 | tf_op jit(solution)/shard_map/ppermute | solution.py:366
  105.4 16.1 %collective-permute-start.8 = (bf16[3104,128]{1,0:T(8,128)(2,1)S(1)}, bf16[3104,128]{1,0:T(8,128)(2,1)}, u32[]{:S(2)}, u32[]{:S(2)}) collective-permute-start(bf16[3104,128]{1,0:T(8,128)(2,1)S(1)} %collective-permute-done.3.refs_2_.refs_1_), channel_id=1, source_target_pairs={{0,1},{1,0},{2,3},{3,2},{4,5},{5,4},{6,7},{7,6},{8,9},{9,8},{10,11... | collective-permute-start | bytes 2383880 | tf_op jit(solution)/shard_map/ppermute | solution.py:366
  107.8 13.7 %collective-permute-start.9 = (bf16[3104,128]{1,0:T(8,128)(2,1)S(1)}, bf16[3104,128]{1,0:T(8,128)(2,1)}, u32[]{:S(2)}, u32[]{:S(2)}) collective-permute-start(bf16[3104,128]{1,0:T(8,128)(2,1)S(1)} %collective-permute-done.4.refs_3_.refs_2_), channel_id=1, source_target_pairs={{0,1},{1,0},{2,3},{3,2},{4,5},{5,4},{6,7},{7,6},{8,9},{9,8},{10,11... | collective-permute-start | bytes 2383880 | tf_op jit(solution)/shard_map/ppermute | solution.py:366
  109.8 17.7 %copy-start.5 = (bf16[1552,128]{1,0:T(8,128)(2,1)}, bf16[1552,128]{1,0:T(8,128)(2,1)S(1)}, u32[]{:S(2)}) copy-start(bf16[1552,128]{1,0:T(8,128)(2,1)S(1)} %collective-permute-done.6.refs_5_.refs_4_) | copy-start | bytes 1191940
  109.8 11.7 %collective-permute-start.11 = (bf16[1552,128]{1,0:T(8,128)(2,1)S(1)}, bf16[1552,128]{1,0:T(8,128)(2,1)}, u32[]{:S(2)}, u32[]{:S(2)}) collective-permute-start(bf16[1552,128]{1,0:T(8,128)(2,1)S(1)} %collective-permute-done.6.refs_5_.refs_4_), channel_id=1, source_target_pairs={{0,1},{1,0},{2,3},{3,2},{4,5},{5,4},{6,7},{7,6},{8,9},{9,8},{10,11... | collective-permute-start | bytes 1191944 | tf_op jit(solution)/shard_map/ppermute | solution.py:366
  112.5 9.0 %collective-permute-start.10 = (bf16[1552,128]{1,0:T(8,128)(2,1)}, bf16[1552,128]{1,0:T(8,128)(2,1)}, u32[]{:S(2)}, u32[]{:S(2)}) collective-permute-start(bf16[1552,128]{1,0:T(8,128)(2,1)} %collective-permute-done.5.refs_4_.refs_3_), channel_id=1, source_target_pairs={{0,1},{1,0},{2,3},{3,2},{4,5},{5,4},{6,7},{7,6},{8,9},{9,8},{10,11... | collective-permute-start | bytes 1191944 | tf_op jit(solution)/shard_map/ppermute | solution.py:366
  118.0 9.6 %copy-start.1 = (f32[1024]{0:T(1024)S(1)}, f32[1024]{0:T(1024)}, u32[]{:S(2)}) copy-start(f32[1024]{0:T(1024)} %param.17) | copy-start | bytes 12292
  118.0 9.6 %copy-start.2 = (f32[1024]{0:T(1024)S(1)}, f32[1024]{0:T(1024)}, u32[]{:S(2)}) copy-start(f32[1024]{0:T(1024)} %param.18) | copy-start | bytes 12292
  118.0 9.6 %all-to-all-start.4 = ((bf16[8,32,256]{2,1,0:T(8,128)(2,1)}), bf16[8,32,256]{2,1,0:T(8,128)(2,1)S(1)}, u32[]{:S(2)}, u32[]{:S(2)}) async-start(bf16[8,32,256]{2,1,0:T(8,128)(2,1)} %bitcast.10), calls=%async_computation.4 | async-start | bytes 262144 | tf_op jit(solution)/shard_map/all_to_all | solution.py:340
  130.9 9.8 %collective-permute-start.12 = (bf16[16,1024]{1,0:T(8,128)(2,1)S(1)}, bf16[16,1024]{1,0:T(8,128)(2,1)S(1)}, u32[]{:S(2)}, u32[]{:S(2)}) collective-permute-start(bf16[16,1024]{1,0:T(8,128)(2,1)S(1)} %get-tuple-element.23.refs_12_), channel_id=1, source_target_pairs={{0,1},{1,2},{2,3},{3,4},{4,5},{5,6},{6,7},{7,8},{8,9},{9,10},{10,1... | collective-permute-start | bytes 98312 | tf_op jit(solution)/shard_map/ppermute | solution.py:400
  132.8 9.4 %collective-permute-start.13 = (bf16[16,1024]{1,0:T(8,128)(2,1)S(1)}, bf16[16,1024]{1,0:T(8,128)(2,1)S(1)}, u32[]{:S(2)}, u32[]{:S(2)}) collective-permute-start(bf16[16,1024]{1,0:T(8,128)(2,1)S(1)} %get-tuple-element.24.refs_11_), channel_id=1, source_target_pairs={{1,0},{2,1},{3,2},{4,3},{5,4},{6,5},{7,6},{8,7},{9,8},{10,9},{11,1... | collective-permute-start | bytes 98312 | tf_op jit(solution)/shard_map/ppermute | solution.py:401

commit v4 on v3

--- a/solution.py
+++ b/solution.py
@@ -9,7 +9,7 @@
 WIDE = ("x", "z")
 NARROW = ("y", "c")
 EVERY = ("x", "z", "y", "c")
-VMEM_BYTES = 32 << 20
+VMEM_BYTES = 24 << 20
 
 
 def in_vmem(count):
@@ -118,63 +118,48 @@
 
 def expert_kernel(x_ref, *refs):
     sources, out_ref, held, sem = refs[:6], refs[6], refs[7:13], refs[13]
+    copies = [pltpu.make_async_copy(s, h, sem.at[i]) for i, (s, h) in enumerate(zip(sources, held))]
+    for i in (0, 1, 3, 4, 2, 5):
+        copies[i].start()
     chunks, _, width = x_ref.shape
-    units = held[0].shape[1]
-    parts = [slice(i * width, (i + 1) * width) for i in range(units // width)]
-    loads = {}
-    for pair in range(2):
-        for i, cols in enumerate(parts):
-            for which in (3 * pair, 3 * pair + 1):
-                at = sem.at[len(loads)]
-                loads[which, i] = pltpu.make_async_copy(
-                    sources[which].at[:, cols], held[which].at[:, cols], at
-                )
-    for which in (2, 5):
-        loads[which, 0] = pltpu.make_async_copy(sources[which], held[which], sem.at[len(loads)])
-    for copy in loads.values():
-        copy.start()
     x = jnp.concatenate([x_ref[q] for q in range(chunks)], axis=1)
     hidden = []
     for pair in range(2):
-        for i, cols in enumerate(parts):
-            loads[3 * pair, i].wait()
-            gate = mm(x, held[3 * pair][:, cols])
-            loads[3 * pair + 1, i].wait()
-            up = mm(x, held[3 * pair + 1][:, cols])
-            hidden.append((gate * jax.nn.sigmoid(gate) * up).astype(jnp.bfloat16))
-    hidden = jnp.concatenate(hidden, axis=1)
-    loads[2, 0].wait()
-    loads[5, 0].wait()
+        copies[3 * pair].wait()
+        gate = mm(x, held[3 * pair][...])
+        copies[3 * pair + 1].wait()
+        up = mm(x, held[3 * pair + 1][...])
+        hidden.append((gate * jax.nn.sigmoid(gate) * up).astype(jnp.bfloat16))
+    copies[2].wait()
+    copies[5].wait()
     for q in range(chunks):
         cols = slice(q * width, (q + 1) * width)
-        total = mm(hidden[:, :units], held[2][:, cols]) + mm(hidden[:, units:], held[5][:, cols])
-        out_ref[q] = total.astype(jnp.bfloat16)
-
-
-def gather(quarters, cores, first, last, sources, out_ref, sem):
+        out_ref[q] = (mm(hidden[0], held[2][:, cols]) + mm(hidden[1], held[5][:, cols])).astype(
+            jnp.bfloat16
+        )
+
+
+def blocks_of(quarters, cores, near):
     y, c = lax.axis_index("y"), lax.axis_index("c")
-    rows, cut = sources[0].shape[0], sources[3].shape[0]
-    copies, order = {}, []
-    for side in range(2):
-        core = c if side == 0 else cores - 1 - c
-        for i, (shift, start, stop) in enumerate(
-            ((0, 0, rows), (quarters - 1, 0, rows), (1, 0, rows), (2, 0, cut), (2, cut, rows))
-        ):
-            block = 4 * side + min(i, 3)
-            if block == len(order):
-                order.append(lax.rem(y + shift, quarters) * cores + core)
-                copies[block] = []
-            low, high = max(first, start), min(last, stop)
-            if low < high:
-                copies[block].append(
-                    pltpu.make_async_copy(
-                        sources[5 * side + i].at[low - start : high - start, :],
-                        out_ref.at[block, low - first : high - first, :],
-                        sem.at[5 * side + i],
-                    )
-                )
-                copies[block][-1].start()
-    return copies, order
+    index = [
+        lax.rem(y + (2 * side - 1) * step + quarters, quarters) * cores + side
+        for side in (c, cores - 1 - c)
+        for step in range(quarters)
+    ]
+    return [index[i] for i in order_of(len(index), near)]
+
+
+def order_of(count, near):
+    return [i for i in range(count) if i in near] + [i for i in range(count) if i not in near]
+
+
+def fetched_rows(near, first, last, refs, held_ref, sem):
+    views = [(ref.at[first:last, :], None) for ref in refs[: len(near)]]
+    for i, ref in enumerate(refs[len(near) :]):
+        copy = pltpu.make_async_copy(ref.at[first:last, :], held_ref.at[i], sem.at[i])
+        copy.start()
+        views.append((held_ref.at[i], copy))
+    return views
 
 
 def combine_kernel(table_ref, rows_ref, out_ref):
@@ -190,15 +175,16 @@
     out_ref[...] = total.astype(jnp.bfloat16)
 
 
-def norm_kernel(quarters, cores, frames_ref, *refs):
-    parts_ref, gain_ref, bias_ref, res_ref, lo_ref, hi_ref, taps_ref, own_ref, held_ref, sem = refs[10:]
+def norm_kernel(quarters, cores, near, frames_ref, *refs):
+    count = quarters * cores
+    parts_ref, gain_ref, bias_ref, res_ref, lo_ref, hi_ref, taps_ref, own_ref, held_ref, sem = refs[count:]
     own, width = own_ref.shape
     index = lax.axis_index("y") * cores + lax.axis_index("c")
     fetch = pltpu.make_async_copy(
-        frames_ref.at[pl.ds(pl.multiple_of(index * own, own), own), :], own_ref, sem.at[10]
+        frames_ref.at[pl.ds(pl.multiple_of(index * own, own), own), :], own_ref, sem.at[count]
     )
     fetch.start()
-    copies, order = gather(quarters, cores, 0, held_ref.shape[1], refs[:10], held_ref, sem)
+    views = fetched_rows(near, 0, held_ref.shape[1], refs[:count], held_ref, sem)
     moe = jnp.concatenate(
         [
             parts_ref[2 * q].astype(jnp.float32) + parts_ref[2 * q + 1].astype(jnp.float32)
@@ -214,31 +200,30 @@
     normed = (centered / jnp.sqrt(variance + 1e-05) * gain_ref[...] + bias_ref[...]).astype(
         jnp.bfloat16
     )
-    channels = held_ref.shape[2]
-    half = lo_ref.shape[0]
-    for block, index in enumerate(order):
-        for copy in copies[block]:
+    channels = width // count
+    half, taps = lo_ref.shape[0], taps_ref.shape[0]
+    for (ref, copy), index in zip(views, blocks_of(quarters, cores, near)):
+        if copy is not None:
             copy.wait()
-        both = jnp.concatenate(
-            [held_ref[block, :width, :], held_ref[block, width : 2 * width, :]], axis=1
-        )
+        both = jnp.concatenate([ref[:width, :], ref[width : 2 * width, :]], axis=1)
         projected = mm(normed, both)
         glu = projected[:, :channels] * jax.nn.sigmoid(projected[:, channels:])
         glu = glu.astype(jnp.bfloat16)
         cols = pl.ds(pl.multiple_of(index * channels, channels), channels)
         lo_ref[:, cols] = glu[:half]
         hi_ref[:, cols] = glu[half:]
-        taps_ref[:, cols] = held_ref[block, 2 * width :, :].astype(jnp.float32)
-
-
-def conv_kernel(quarters, cores, taps, *refs):
-    left_ref, lo_ref, hi_ref, right_ref, taps_ref, res_ref, out_ref, act_ref, held_ref, sem = refs[10:]
-    blocks, rows, channels = held_ref.shape
-    last = refs[0].shape[0]
-    copies, order = gather(quarters, cores, last - rows, last, refs[:10], held_ref, sem)
+        taps_ref[:, cols] = ref[2 * width : 2 * width + taps, :].astype(jnp.float32)
+
+
+def conv_kernel(quarters, cores, near, taps, *refs):
+    blocks = quarters * cores
+    left_ref, lo_ref, hi_ref, right_ref, taps_ref, res_ref, out_ref, act_ref, held_ref, sem = refs[blocks:]
     half, width = lo_ref.shape
     count = 2 * half
     reach = (taps - 1) // 2
+    channels = width // blocks
+    first = 2 * width + taps + 1
+    views = fetched_rows(near, first, first + width, refs[:blocks], held_ref, sem)
     for n in range(0, blocks, 2):
         cols = slice(n * channels, (n + 2) * channels)
         window = jnp.concatenate(
@@ -254,13 +239,13 @@
                     depth = term if depth is None else depth + term
         act_ref[:, cols] = (depth * jax.nn.sigmoid(depth)).astype(jnp.bfloat16)
     acts, points = [], []
-    for block, index in enumerate(order):
-        for copy in copies[block]:
+    for (ref, copy), index in zip(views, blocks_of(quarters, cores, near)):
+        if copy is not None:
             copy.wait()
         acts.append(act_ref[:, pl.ds(pl.multiple_of(index * channels, channels), channels)])
         points.append(
             jnp.concatenate(
-                [held_ref[block, b * channels : (b + 1) * channels, :] for b in range(blocks)],
+                [ref[b * channels : (b + 1) * channels, :] for b in range(blocks)],
                 axis=1,
             )
         )
@@ -296,10 +281,6 @@
     far = lambda array: pltpu.with_memory_space_constraint(array, pltpu.HBM)
     frames = far(frames)
 
-    mine = [w_gate[0], w_up[0], w_down[0]]
-    swap = [(i, cores - 1 - i) for i in range(cores)]
-    theirs = [lax.ppermute(w, "c", swap) for w in mine]
-
     rows = experts * slots
     packed_rows = 3 * width + taps + 1
     outgoing, table, packed = pl.pallas_call(
@@ -331,15 +312,27 @@
         far(gate_values.T),
     )
 
-    ahead = [(i, (i + 1) % quarters) for i in range(quarters)]
-    behind = [((i + 1) % quarters, i) for i in range(quarters)]
-    before = lax.ppermute(packed, "y", ahead)
-    after = lax.ppermute(packed, "y", behind)
+    ring = [
+        (y * cores + c, (y + 1 - 2 * c) % quarters * cores + c)
+        for y in range(quarters)
+        for c in range(cores)
+    ]
+    swap = [(i, cores - 1 - i) for i in range(cores)]
+    around = lambda cells: lax.ppermute(cells, NARROW, ring)
+    across = lambda cells: lax.ppermute(cells, "c", swap)
+    held = [packed]
+    for _ in range(quarters - 2):
+        held.append(around(held[-1]))
 
     def over(axis, cells):
         return lax.all_to_all(cells, axis, split_axis=0, concat_axis=0, tiled=True)
 
     arrived = over(WIDE, outgoing.reshape(experts, slots, share)).reshape(1, rows, share)
+    mine = [w_gate[0], w_up[0], w_down[0]]
+    theirs = [across(w) for w in mine]
+    arrived, *held = lax.optimization_barrier((arrived, *held))
+    swapped = [across(cells) for cells in held]
+    held.append(around(held[-1]))
     x = over("y", jnp.broadcast_to(arrived, (quarters, rows, share)))
     weights = mine + theirs
     partial = pl.pallas_call(
@@ -348,22 +341,15 @@
         out_specs=pl.BlockSpec(memory_space=pltpu.VMEM),
         out_shape=jax.ShapeDtypeStruct((quarters, rows, share), jnp.bfloat16),
         scratch_shapes=[pltpu.VMEM(w.shape, w.dtype) for w in weights]
-        + [pltpu.SemaphoreType.DMA((4 * w_gate.shape[2] // share + 2,))],
+        + [pltpu.SemaphoreType.DMA((6,))],
         compiler_params=params,
         name="experts",
     )(x, *[far(w) for w in weights])
     partial = over("y", partial)
     summed = jnp.sum(partial.astype(jnp.float32), axis=0).astype(jnp.bfloat16)
-    summed, packed, before, after = lax.optimization_barrier((summed, packed, before, after))
-    cut = packed_rows // 2
-    held = [
-        packed,
-        before,
-        after,
-        lax.ppermute(before[:cut], "y", ahead),
-        lax.ppermute(after[cut:], "y", behind),
-    ]
-    held = held + [lax.ppermute(cells, "c", swap) for cells in held]
+    summed, *held = lax.optimization_barrier((summed, *held, *swapped))
+    held, swapped = held[:quarters], held[quarters:]
+    swapped.append(across(held[-1]))
     returned = over(WIDE, summed.reshape(experts, slots, share)).reshape(rows, share)
     mixed = pl.pallas_call(
         combine_kernel,
@@ -373,13 +359,15 @@
         compiler_params=params,
         name="combine",
     )(table, returned)
-    held = [far(cells) for cells in held]
+    held = held + swapped
+    near = (0, 1, 2)
+    held = [held[i] if i in near else far(held[i]) for i in order_of(narrow, near)]
     parts = over(NARROW, mixed.reshape(narrow, own, share))
 
     half = own // 2
     residual, lo, hi, kernel = pl.pallas_call(
-        lambda *refs: norm_kernel(quarters, cores, *refs),
-        in_specs=in_hbm(11) + in_vmem(3),
+        lambda *refs: norm_kernel(quarters, cores, near, *refs),
+        in_specs=in_hbm(1) + in_vmem(3) + in_hbm(5) + in_vmem(3),
         out_specs=in_vmem(4),
         out_shape=[
             jax.ShapeDtypeStruct((own, width), jnp.float32),
@@ -389,8 +377,8 @@
         ],
         scratch_shapes=[
             pltpu.VMEM((own, width), jnp.bfloat16),
-            pltpu.VMEM((narrow, packed_rows - width, channels), jnp.bfloat16),
-            pltpu.SemaphoreType.DMA((11,)),
+            pltpu.VMEM((narrow - 3, packed_rows - width, channels), jnp.bfloat16),
+            pltpu.SemaphoreType.DMA((narrow + 1,)),
         ],
         compiler_params=params,
         name="norm_glu",
@@ -400,14 +388,14 @@
     left = lax.ppermute(hi, EVERY, [(i, i + 1) for i in range(ends)])
     right = lax.ppermute(lo, EVERY, [(i + 1, i) for i in range(ends)])
     return pl.pallas_call(
-        lambda *refs: conv_kernel(quarters, cores, taps, *refs),
-        in_specs=in_hbm(10) + in_vmem(6),
+        lambda *refs: conv_kernel(quarters, cores, near, taps, *refs),
+        in_specs=in_vmem(3) + in_hbm(5) + in_vmem(6),
         out_specs=pl.BlockSpec(memory_space=pltpu.VMEM),
         out_shape=jax.ShapeDtypeStruct((own, width), jnp.bfloat16),
         scratch_shapes=[
             pltpu.VMEM((own, width), jnp.bfloat16),
-            pltpu.VMEM((narrow, width, channels), jnp.bfloat16),
-            pltpu.SemaphoreType.DMA((10,)),
+            pltpu.VMEM((narrow - 3, width, channels), jnp.bfloat16),
+            pltpu.SemaphoreType.DMA((narrow,)),
         ],
         compiler_params=params,
         name="conv",

time: 146 us -> 143 us (0.979)
  waiting for transfers between devices: 34.3 us -> 40.9 us
  starting transfers between devices: 74.4 us -> 69.1 us
  Pallas kernels: 17.3 us -> 14 us
    all_to_all x4, waiting for transfers between devices: 32.4 us -> 39.3 us  [over(): return lax.all_to_all(cells, axis, split_axis=0, concat_axis=0, tiled=True)]
    ppermute x12 -> x10, starting transfers between devices: 29.7 us -> 25.3 us  [the longest x7 14.4 us: shards(): across = lambda cells: lax.ppermute(cells, 'c', swap)]
    pallas_call x1, Pallas kernels: 7.92 us -> 5.37 us  [shards(): pl.pallas_call(expert_kernel, in_specs=in_vmem(1) + in_hbm(6), out_specs=...]
  transfers between devices with their start and end apart: 18 -> 16, of which waited for: 6 -> 5; matrix products, arithmetic and copies ran while one was open for 1% -> 1% of each run, Pallas kernels for 6% -> 5%
where the time goes in v4:
time: 143 us; the launch traced here: 142 us
  starting transfers between devices  69.1 us (48%)
  waiting for transfers between devices  40.9 us (29%)
  blocking collectives  16 us (11%)
  Pallas kernels  14 us (10%)
    all_to_all x4, waiting for transfers between devices, over(): return lax.all_to_all(cells, axis, split_axis=0, concat_axis=0, tiled=True)  39.3 us
    all_to_all x4, starting transfers between devices, over(): return lax.all_to_all(cells, axis, split_axis=0, concat_axis=0, tiled=True)  34 us
    all_to_all x1, blocking collectives, over(): return lax.all_to_all(cells, axis, split_axis=0, concat_axis=0, tiled=True)  16 us
    ppermute x7, starting transfers between devices, shards(): across = lambda cells: lax.ppermute(cells, 'c', swap)  14.4 us
    ppermute x3, starting transfers between devices, shards(): around = lambda cells: lax.ppermute(cells, NARROW, ring)  10.8 us
    ppermute x1, starting transfers between devices, shards(): right = lax.ppermute(lo, EVERY, [(i + 1, i) for i in range(ends)])  7.86 us
    pallas_call x1, Pallas kernels, shards(): pl.pallas_call(expert_kernel, in_specs=in_vmem(1) + in_hbm(6), out_specs=...  5.37 us
    pallas_call x1, Pallas kernels, shards(): pl.pallas_call(lambda *refs: norm_kernel(quarters, cores, near, *refs), i...  2.87 us
  transfers between devices with their start and end apart: 16, of which 5 were waited for; matrix products, arithmetic and copies ran while one was open for 1% of the time, Pallas kernels for 5%

profile of v4, /device:TPU:6, one launch (start us, length us, event | category | flops | bytes accessed | tf_op | source)
XLA Modules:
  0.0 142.2 jit_solution(7431788638438930829)
XLA Ops:
  0.0 2.2 %prepare.1 = (bf16[512,256]{1,0:T(8,128)(2,1)}, f32[8,256]{1,0:T(8,128)S(1)}, bf16[3104,128]{1,0:T(8,128)(2,1)S(1)}) custom-call(s32[2,256]{1,0:T(2,128)} %bitcast.26, bf16[256,1024]{1,0:T(8,128)(2,1)} %refs_0_.1, bf16[2048,128]{1,0:T(8,128)(2,1)} %bitcast.25, bf16[31,128]{1,0:T(8,128)(2,1)} %refs_3_.1, bf16[128,1024]{1,0:T(8,128)(2,1)} %refs_4_.1, ...), custom_call_target="tpu_custom_call" | custom-call | tf_op jit(solution)/shard_map/prepare/pallas_call | solution.py:286
  2.2 3.5 %collective-permute-start = (bf16[3104,128]{1,0:T(8,128)(2,1)S(1)}, bf16[3104,128]{1,0:T(8,128)(2,1)S(1)}, u32[]{:S(2)}, u32[]{:S(2)}) collective-permute-start(bf16[3104,128]{1,0:T(8,128)(2,1)S(1)} %get-tuple-element.30.refs_1_.refs_0_), channel_id=1, source_target_pairs={{0,2},{1,7},{2,4},{3,1},{4,6},{5,3},{6,0},{7,5},{8,10},{9,15},{10,... | collective-permute-start | bytes 2383880 | tf_op jit(solution)/shard_map/ppermute | solution.py:321
  5.7 18.8 %all-to-all-start = ((bf16[64,8,256]{2,1,0:T(8,128)(2,1)}), bf16[64,8,256]{2,1,0:T(8,128)(2,1)S(1)}, u32[]{:S(2)}, u32[]{:S(2)}) async-start(bf16[64,8,256]{2,1,0:T(8,128)(2,1)} %bitcast.3), calls=%async_computation | async-start | bytes 524288 | tf_op jit(solution)/shard_map/all_to_all | solution.py:328
  24.5 0.0 collective-permute-done.refs_2_.refs_1_
  24.5 3.5 %collective-permute-start.1 = (bf16[3104,128]{1,0:T(8,128)(2,1)S(1)}, bf16[3104,128]{1,0:T(8,128)(2,1)S(1)}, u32[]{:S(2)}, u32[]{:S(2)}) collective-permute-start(bf16[3104,128]{1,0:T(8,128)(2,1)S(1)} %collective-permute-done.refs_2_.refs_1_), channel_id=1, source_target_pairs={{0,2},{1,7},{2,4},{3,1},{4,6},{5,3},{6,0},{7,5},{8,10},{9,15},{10,... | collective-permute-start | bytes 2383880 | tf_op jit(solution)/shard_map/ppermute | solution.py:321
  28.0 1.9 %collective-permute-start.2 = (bf16[1024,512]{1,0:T(8,128)(2,1)}, bf16[1024,512]{1,0:T(8,128)(2,1)}, u32[]{:S(2)}, u32[]{:S(2)}) collective-permute-start(bf16[1024,512]{1,0:T(8,128)(2,1)} %bitcast.19), channel_id=1, source_target_pairs={{0,1},{1,0},{2,3},{3,2},{4,5},{5,4},{6,7},{7,6},{8,9},{9,8},{10,11... | collective-permute-start | bytes 3145736 | tf_op jit(solution)/shard_map/ppermute | solution.py:322
  30.0 2.4 %collective-permute-start.3 = (bf16[1024,512]{1,0:T(8,128)(2,1)}, bf16[1024,512]{1,0:T(8,128)(2,1)}, u32[]{:S(2)}, u32[]{:S(2)}) collective-permute-start(bf16[1024,512]{1,0:T(8,128)(2,1)} %bitcast.21), channel_id=1, source_target_pairs={{0,1},{1,0},{2,3},{3,2},{4,5},{5,4},{6,7},{7,6},{8,9},{9,8},{10,11... | collective-permute-start | bytes 3145736 | tf_op jit(solution)/shard_map/ppermute | solution.py:322
  32.4 1.9 %collective-permute-start.4 = (bf16[512,1024]{1,0:T(8,128)(2,1)}, bf16[512,1024]{1,0:T(8,128)(2,1)}, u32[]{:S(2)}, u32[]{:S(2)}) collective-permute-start(bf16[512,1024]{1,0:T(8,128)(2,1)} %bitcast.23), channel_id=1, source_target_pairs={{0,1},{1,0},{2,3},{3,2},{4,5},{5,4},{6,7},{7,6},{8,9},{9,8},{10,11... | collective-permute-start | bytes 3145736 | tf_op jit(solution)/shard_map/ppermute | solution.py:322
  34.3 12.1 %all-to-all-done = bf16[64,8,256]{2,1,0:T(8,128)(2,1)S(1)} async-done(((bf16[64,8,256]{2,1,0:T(8,128)(2,1)}), bf16[64,8,256]{2,1,0:T(8,128)(2,1)S(1)}, u32[]{:S(2)}, u32[]{:S(2)}) %all-to-all-start) | async-done | bytes 262176 | tf_op jit(solution)/shard_map/all_to_all | solution.py:328
  46.4 0.0 collective-permute-done.1.refs_3_.refs_2_
  46.4 1.0 broadcast_in_dim.14
  47.5 3.5 %all-to-all-start.1 = ((bf16[4,512,256]{2,1,0:T(8,128)(2,1)}), bf16[4,512,256]{2,1,0:T(8,128)(2,1)S(1)}, u32[]{:S(2)}, u32[]{:S(2)}) async-start(bf16[4,512,256]{2,1,0:T(8,128)(2,1)} %broadcast_in_dim.14), calls=%async_computation.1 | async-start | bytes 2097152 | tf_op jit(solution)/shard_map/all_to_all | solution.py:328
  51.0 3.9 %collective-permute-start.5 = (bf16[3104,128]{1,0:T(8,128)(2,1)S(1)}, bf16[3104,128]{1,0:T(8,128)(2,1)}, u32[]{:S(2)}, u32[]{:S(2)}) collective-permute-start(bf16[3104,128]{1,0:T(8,128)(2,1)S(1)} %collective-permute-done.1.refs_3_.refs_2_), channel_id=1, source_target_pairs={{0,2},{1,7},{2,4},{3,1},{4,6},{5,3},{6,0},{7,5},{8,10},{9,15},{10,... | collective-permute-start | bytes 2383880 | tf_op jit(solution)/shard_map/ppermute | solution.py:321
  54.9 1.9 %collective-permute-start.8 = (bf16[3104,128]{1,0:T(8,128)(2,1)S(1)}, bf16[3104,128]{1,0:T(8,128)(2,1)}, u32[]{:S(2)}, u32[]{:S(2)}) collective-permute-start(bf16[3104,128]{1,0:T(8,128)(2,1)S(1)} %collective-permute-done.1.refs_3_.refs_2_), channel_id=1, source_target_pairs={{0,1},{1,0},{2,3},{3,2},{4,5},{5,4},{6,7},{7,6},{8,9},{9,8},{10,11... | collective-permute-start | bytes 2383880 | tf_op jit(solution)/shard_map/ppermute | solution.py:322
  56.8 0.0 collective-permute-done.2.refs_3_
  56.8 2.4 %collective-permute-start.6 = (bf16[3104,128]{1,0:T(8,128)(2,1)S(1)}, bf16[3104,128]{1,0:T(8,128)(2,1)}, u32[]{:S(2)}, u32[]{:S(2)}) collective-permute-start(bf16[3104,128]{1,0:T(8,128)(2,1)S(1)} %get-tuple-element.30.refs_1_.refs_0_), channel_id=1, source_target_pairs={{0,1},{1,0},{2,3},{3,2},{4,5},{5,4},{6,7},{7,6},{8,9},{9,8},{10,11... | collective-permute-start | bytes 2383880 | tf_op jit(solution)/shard_map/ppermute | solution.py:322
  59.2 0.0 collective-permute-done.3.refs_4_
  59.3 1.9 %collective-permute-start.7 = (bf16[3104,128]{1,0:T(8,128)(2,1)S(1)}, bf16[3104,128]{1,0:T(8,128)(2,1)}, u32[]{:S(2)}, u32[]{:S(2)}) collective-permute-start(bf16[3104,128]{1,0:T(8,128)(2,1)S(1)} %collective-permute-done.refs_2_.refs_1_), channel_id=1, source_target_pairs={{0,1},{1,0},{2,3},{3,2},{4,5},{5,4},{6,7},{7,6},{8,9},{9,8},{10,11... | collective-permute-start | bytes 2383880 | tf_op jit(solution)/shard_map/ppermute | solution.py:322
  61.2 0.0 collective-permute-done.4.refs_5_
  61.2 4.4 %all-to-all-done.1.x_ref = bf16[4,512,256]{2,1,0:T(8,128)(2,1)S(1)} async-done(((bf16[4,512,256]{2,1,0:T(8,128)(2,1)}), bf16[4,512,256]{2,1,0:T(8,128)(2,1)S(1)}, u32[]{:S(2)}, u32[]{:S(2)}) %all-to-all-start.1) | async-done | bytes 1048608 | tf_op jit(solution)/shard_map/all_to_all | solution.py:328
  65.6 5.4 %experts.1 = bf16[4,512,256]{2,1,0:T(8,128)(2,1)S(1)} custom-call(bf16[4,512,256]{2,1,0:T(8,128)(2,1)S(1)} %all-to-all-done.1.x_ref, bf16[1024,512]{1,0:T(8,128)(2,1)} %bitcast.20, bf16[1024,512]{1,0:T(8,128)(2,1)} %bitcast.22, bf16[512,1024]{1,0:T(8,128)(2,1)} %bitcast.24, bf16[1024,512]{1,0:T(8,128)(2,1)} %collective-permute-done.2.refs_3_, ...), custom_call_target="tpu_custom_call" | custom-call | tf_op jit(solution)/shard_map/experts/pallas_call | solution.py:338
  71.0 16.0 %all_to_all.25 = bf16[4,512,256]{2,1,0:T(8,128)(2,1)S(1)} all-to-all(bf16[4,512,256]{2,1,0:T(8,128)(2,1)S(1)} %experts.1), channel_id=1, replica_groups=mesh['x'=4,'z'=16,'y'=4,'c'=2] {'y'}, dimensions={0} | all-to-all | bytes 2097152 | tf_op jit(solution)/shard_map/all_to_all | solution.py:328
  87.0 0.9 reduce_sum.12
  87.9 0.0 collective-permute-done.5.refs_4_.refs_3_
  87.9 0.0 collective-permute-done.8.refs_7_.refs_6_
  87.9 0.0 collective-permute-done.6.refs_5_.refs_4_
  87.9 0.0 collective-permute-done.7.refs_6_.refs_5_
  87.9 8.2 %all-to-all-start.3 = ((bf16[64,8,256]{2,1,0:T(8,128)(2,1)}), bf16[64,8,256]{2,1,0:T(8,128)(2,1)S(1)}, u32[]{:S(2)}, u32[]{:S(2)}) async-start(bf16[64,8,256]{2,1,0:T(8,128)(2,1)} %bitcast.18), calls=%async_computation.3 | async-start | bytes 524288 | tf_op jit(solution)/shard_map/all_to_all | solution.py:328
  96.1 1.9 %collective-permute-start.9 = (bf16[3104,128]{1,0:T(8,128)(2,1)}, bf16[3104,128]{1,0:T(8,128)(2,1)S(1)}, u32[]{:S(2)}, u32[]{:S(2)}) collective-permute-start(bf16[3104,128]{1,0:T(8,128)(2,1)} %collective-permute-done.5.refs_4_.refs_3_), channel_id=1, source_target_pairs={{0,1},{1,0},{2,3},{3,2},{4,5},{5,4},{6,7},{7,6},{8,9},{9,8},{10,11... | collective-permute-start | bytes 2383880 | tf_op jit(solution)/shard_map/ppermute | solution.py:322
  98.1 16.7 %all-to-all-done.3 = bf16[64,8,256]{2,1,0:T(8,128)(2,1)S(1)} async-done(((bf16[64,8,256]{2,1,0:T(8,128)(2,1)}), bf16[64,8,256]{2,1,0:T(8,128)(2,1)S(1)}, u32[]{:S(2)}, u32[]{:S(2)}) %all-to-all-start.3) | async-done | bytes 262176 | tf_op jit(solution)/shard_map/all_to_all | solution.py:328
  114.8 1.1 combine.1
  115.9 0.0 copy-start
  115.9 0.0 copy-start.1
  115.9 3.5 %all-to-all-start.4 = ((bf16[8,32,256]{2,1,0:T(8,128)(2,1)}), bf16[8,32,256]{2,1,0:T(8,128)(2,1)S(1)}, u32[]{:S(2)}, u32[]{:S(2)}) async-start(bf16[8,32,256]{2,1,0:T(8,128)(2,1)} %bitcast.11), calls=%async_computation.4 | async-start | bytes 262144 | tf_op jit(solution)/shard_map/all_to_all | solution.py:328
  119.5 0.0 collective-permute-done.9.refs_8_.refs_7_
  119.5 0.0 copy-start.2
  119.5 6.0 %all-to-all-done.4.refs_9_ = bf16[8,32,256]{2,1,0:T(8,128)(2,1)S(1)} async-done(((bf16[8,32,256]{2,1,0:T(8,128)(2,1)}), bf16[8,32,256]{2,1,0:T(8,128)(2,1)S(1)}, u32[]{:S(2)}, u32[]{:S(2)}) %all-to-all-start.4) | async-done | bytes 131104 | tf_op jit(solution)/shard_map/all_to_all | solution.py:328
  125.5 0.0 copy-done.2
  125.5 0.0 copy-done
  125.5 0.0 copy-done.1
  125.5 2.9 %norm_glu.1 = (f32[32,1024]{1,0:T(8,128)S(1)}, bf16[16,1024]{1,0:T(8,128)(2,1)S(1)}, bf16[16,1024]{1,0:T(8,128)(2,1)S(1)}, f32[32,1024]{1,0:T(8,128)S(1)}) custom-call(bf16[256,1024]{1,0:T(8,128)(2,1)} %refs_0_.1, bf16[3104,128]{1,0:T(8,128)(2,1)S(1)} %get-tuple-element.30.refs_1_.refs_0_, bf16[3104,128]{1,0:T(8,128)(2,1)S(1)} %collective-permute-done.refs_2_.refs_1_, ...), custom_call_target="tpu_custom_call" | custom-call | tf_op jit(solution)/shard_map/norm_glu/pallas_call | solution.py:368
  128.4 1.9 %collective-permute-start.10 = (bf16[16,1024]{1,0:T(8,128)(2,1)S(1)}, bf16[16,1024]{1,0:T(8,128)(2,1)S(1)}, u32[]{:S(2)}, u32[]{:S(2)}) collective-permute-start(bf16[16,1024]{1,0:T(8,128)(2,1)S(1)} %get-tuple-element.39.refs_10_), channel_id=1, source_target_pairs={{0,1},{1,2},{2,3},{3,4},{4,5},{5,6},{6,7},{7,8},{8,9},{9,10},{10,1... | collective-permute-start | bytes 98312 | tf_op jit(solution)/shard_map/ppermute | solution.py:388
  130.3 7.9 %collective-permute-start.11 = (bf16[16,1024]{1,0:T(8,128)(2,1)S(1)}, bf16[16,1024]{1,0:T(8,128)(2,1)S(1)}, u32[]{:S(2)}, u32[]{:S(2)}) collective-permute-start(bf16[16,1024]{1,0:T(8,128)(2,1)S(1)} %get-tuple-element.40.refs_9_), channel_id=1, source_target_pairs={{1,0},{2,1},{3,2},{4,3},{5,4},{6,5},{7,6},{8,7},{9,8},{10,9},{11,1... | collective-permute-start | bytes 98312 | tf_op jit(solution)/shard_map/ppermute | solution.py:389
  138.2 0.0 collective-permute-done.10.refs_8_
  138.2 1.6 %collective-permute-done.11.refs_11_ = bf16[16,1024]{1,0:T(8,128)(2,1)S(1)} collective-permute-done((bf16[16,1024]{1,0:T(8,128)(2,1)S(1)}, bf16[16,1024]{1,0:T(8,128)(2,1)S(1)}, u32[]{:S(2)}, u32[]{:S(2)}) %collective-permute-start.11) | collective-permute-done | bytes 32800 | tf_op jit(solution)/shard_map/ppermute | solution.py:389
  139.8 2.4 %conv.1 = bf16[32,1024]{1,0:T(8,128)(2,1)} custom-call(bf16[3104,128]{1,0:T(8,128)(2,1)S(1)} %get-tuple-element.30.refs_1_.refs_0_, bf16[3104,128]{1,0:T(8,128)(2,1)S(1)} %collective-permute-done.refs_2_.refs_1_, bf16[3104,128]{1,0:T(8,128)(2,1)S(1)} %collective-permute-done.1.refs_3_.refs_2_, bf16[3104,128]{1,0:T(8,128)(2,1)} %collective-permute-done.5.refs_4_.refs_3_, ...), custom_call_target="tpu_custom_call" | custom-call | tf_op jit(solution)/shard_map/conv/pallas_call | solution.py:390
Async XLA Ops:
  2.2 22.3 %collective-permute-start = (bf16[3104,128]{1,0:T(8,128)(2,1)S(1)}, bf16[3104,128]{1,0:T(8,128)(2,1)S(1)}, u32[]{:S(2)}, u32[]{:S(2)}) collective-permute-start(bf16[3104,128]{1,0:T(8,128)(2,1)S(1)} %get-tuple-element.30.refs_1_.refs_0_), channel_id=1, source_target_pairs={{0,2},{1,7},{2,4},{3,1},{4,6},{5,3},{6,0},{7,5},{8,10},{9,15},{10,... | collective-permute-start | bytes 2383880 | tf_op jit(solution)/shard_map/ppermute | solution.py:321
  5.7 40.7 %all-to-all-start = ((bf16[64,8,256]{2,1,0:T(8,128)(2,1)}), bf16[64,8,256]{2,1,0:T(8,128)(2,1)S(1)}, u32[]{:S(2)}, u32[]{:S(2)}) async-start(bf16[64,8,256]{2,1,0:T(8,128)(2,1)} %bitcast.3), calls=%async_computation | async-start | bytes 524288 | tf_op jit(solution)/shard_map/all_to_all | solution.py:328
  24.5 21.9 %collective-permute-start.1 = (bf16[3104,128]{1,0:T(8,128)(2,1)S(1)}, bf16[3104,128]{1,0:T(8,128)(2,1)S(1)}, u32[]{:S(2)}, u32[]{:S(2)}) collective-permute-start(bf16[3104,128]{1,0:T(8,128)(2,1)S(1)} %collective-permute-done.refs_2_.refs_1_), channel_id=1, source_target_pairs={{0,2},{1,7},{2,4},{3,1},{4,6},{5,3},{6,0},{7,5},{8,10},{9,15},{10,... | collective-permute-start | bytes 2383880 | tf_op jit(solution)/shard_map/ppermute | solution.py:321
  28.0 28.8 %collective-permute-start.2 = (bf16[1024,512]{1,0:T(8,128)(2,1)}, bf16[1024,512]{1,0:T(8,128)(2,1)}, u32[]{:S(2)}, u32[]{:S(2)}) collective-permute-start(bf16[1024,512]{1,0:T(8,128)(2,1)} %bitcast.19), channel_id=1, source_target_pairs={{0,1},{1,0},{2,3},{3,2},{4,5},{5,4},{6,7},{7,6},{8,9},{9,8},{10,11... | collective-permute-start | bytes 3145736 | tf_op jit(solution)/shard_map/ppermute | solution.py:322
  30.0 29.3 %collective-permute-start.3 = (bf16[1024,512]{1,0:T(8,128)(2,1)}, bf16[1024,512]{1,0:T(8,128)(2,1)}, u32[]{:S(2)}, u32[]{:S(2)}) collective-permute-start(bf16[1024,512]{1,0:T(8,128)(2,1)} %bitcast.21), channel_id=1, source_target_pairs={{0,1},{1,0},{2,3},{3,2},{4,5},{5,4},{6,7},{7,6},{8,9},{9,8},{10,11... | collective-permute-start | bytes 3145736 | tf_op jit(solution)/shard_map/ppermute | solution.py:322
  32.4 28.8 %collective-permute-start.4 = (bf16[512,1024]{1,0:T(8,128)(2,1)}, bf16[512,1024]{1,0:T(8,128)(2,1)}, u32[]{:S(2)}, u32[]{:S(2)}) collective-permute-start(bf16[512,1024]{1,0:T(8,128)(2,1)} %bitcast.23), channel_id=1, source_target_pairs={{0,1},{1,0},{2,3},{3,2},{4,5},{5,4},{6,7},{7,6},{8,9},{9,8},{10,11... | collective-permute-start | bytes 3145736 | tf_op jit(solution)/shard_map/ppermute | solution.py:322
  47.5 18.2 %all-to-all-start.1 = ((bf16[4,512,256]{2,1,0:T(8,128)(2,1)}), bf16[4,512,256]{2,1,0:T(8,128)(2,1)S(1)}, u32[]{:S(2)}, u32[]{:S(2)}) async-start(bf16[4,512,256]{2,1,0:T(8,128)(2,1)} %broadcast_in_dim.14), calls=%async_computation.1 | async-start | bytes 2097152 | tf_op jit(solution)/shard_map/all_to_all | solution.py:328
  51.0 36.9 %collective-permute-start.5 = (bf16[3104,128]{1,0:T(8,128)(2,1)S(1)}, bf16[3104,128]{1,0:T(8,128)(2,1)}, u32[]{:S(2)}, u32[]{:S(2)}) collective-permute-start(bf16[3104,128]{1,0:T(8,128)(2,1)S(1)} %collective-permute-done.1.refs_3_.refs_2_), channel_id=1, source_target_pairs={{0,2},{1,7},{2,4},{3,1},{4,6},{5,3},{6,0},{7,5},{8,10},{9,15},{10,... | collective-permute-start | bytes 2383880 | tf_op jit(solution)/shard_map/ppermute | solution.py:321
  54.9 33.0 %collective-permute-start.8 = (bf16[3104,128]{1,0:T(8,128)(2,1)S(1)}, bf16[3104,128]{1,0:T(8,128)(2,1)}, u32[]{:S(2)}, u32[]{:S(2)}) collective-permute-start(bf16[3104,128]{1,0:T(8,128)(2,1)S(1)} %collective-permute-done.1.refs_3_.refs_2_), channel_id=1, source_target_pairs={{0,1},{1,0},{2,3},{3,2},{4,5},{5,4},{6,7},{7,6},{8,9},{9,8},{10,11... | collective-permute-start | bytes 2383880 | tf_op jit(solution)/shard_map/ppermute | solution.py:322
  56.8 31.1 %collective-permute-start.6 = (bf16[3104,128]{1,0:T(8,128)(2,1)S(1)}, bf16[3104,128]{1,0:T(8,128)(2,1)}, u32[]{:S(2)}, u32[]{:S(2)}) collective-permute-start(bf16[3104,128]{1,0:T(8,128)(2,1)S(1)} %get-tuple-element.30.refs_1_.refs_0_), channel_id=1, source_target_pairs={{0,1},{1,0},{2,3},{3,2},{4,5},{5,4},{6,7},{7,6},{8,9},{9,8},{10,11... | collective-permute-start | bytes 2383880 | tf_op jit(solution)/shard_map/ppermute | solution.py:322
  59.3 28.7 %collective-permute-start.7 = (bf16[3104,128]{1,0:T(8,128)(2,1)S(1)}, bf16[3104,128]{1,0:T(8,128)(2,1)}, u32[]{:S(2)}, u32[]{:S(2)}) collective-permute-start(bf16[3104,128]{1,0:T(8,128)(2,1)S(1)} %collective-permute-done.refs_2_.refs_1_), channel_id=1, source_target_pairs={{0,1},{1,0},{2,3},{3,2},{4,5},{5,4},{6,7},{7,6},{8,9},{9,8},{10,11... | collective-permute-start | bytes 2383880 | tf_op jit(solution)/shard_map/ppermute | solution.py:322
  87.9 26.9 %all-to-all-start.3 = ((bf16[64,8,256]{2,1,0:T(8,128)(2,1)}), bf16[64,8,256]{2,1,0:T(8,128)(2,1)S(1)}, u32[]{:S(2)}, u32[]{:S(2)}) async-start(bf16[64,8,256]{2,1,0:T(8,128)(2,1)} %bitcast.18), calls=%async_computation.3 | async-start | bytes 524288 | tf_op jit(solution)/shard_map/all_to_all | solution.py:328
  96.1 23.3 %collective-permute-start.9 = (bf16[3104,128]{1,0:T(8,128)(2,1)}, bf16[3104,128]{1,0:T(8,128)(2,1)S(1)}, u32[]{:S(2)}, u32[]{:S(2)}) collective-permute-start(bf16[3104,128]{1,0:T(8,128)(2,1)} %collective-permute-done.5.refs_4_.refs_3_), channel_id=1, source_target_pairs={{0,1},{1,0},{2,3},{3,2},{4,5},{5,4},{6,7},{7,6},{8,9},{9,8},{10,11... | collective-permute-start | bytes 2383880 | tf_op jit(solution)/shard_map/ppermute | solution.py:322
  115.9 9.6 %copy-start = (f32[1024]{0:T(1024)S(1)}, f32[1024]{0:T(1024)}, u32[]{:S(2)}) copy-start(f32[1024]{0:T(1024)} %param.17) | copy-start | bytes 12292
  115.9 9.6 %copy-start.1 = (f32[1024]{0:T(1024)S(1)}, f32[1024]{0:T(1024)}, u32[]{:S(2)}) copy-start(f32[1024]{0:T(1024)} %param.18) | copy-start | bytes 12292
  115.9 9.6 %all-to-all-start.4 = ((bf16[8,32,256]{2,1,0:T(8,128)(2,1)}), bf16[8,32,256]{2,1,0:T(8,128)(2,1)S(1)}, u32[]{:S(2)}, u32[]{:S(2)}) async-start(bf16[8,32,256]{2,1,0:T(8,128)(2,1)} %bitcast.11), calls=%async_computation.4 | async-start | bytes 262144 | tf_op jit(solution)/shard_map/all_to_all | solution.py:328
  119.5 6.0 %copy-start.2 = (bf16[3104,128]{1,0:T(8,128)(2,1)}, bf16[3104,128]{1,0:T(8,128)(2,1)S(1)}, u32[]{:S(2)}) copy-start(bf16[3104,128]{1,0:T(8,128)(2,1)S(1)} %collective-permute-done.9.refs_8_.refs_7_) | copy-start | bytes 2383876
  128.4 9.8 %collective-permute-start.10 = (bf16[16,1024]{1,0:T(8,128)(2,1)S(1)}, bf16[16,1024]{1,0:T(8,128)(2,1)S(1)}, u32[]{:S(2)}, u32[]{:S(2)}) collective-permute-start(bf16[16,1024]{1,0:T(8,128)(2,1)S(1)} %get-tuple-element.39.refs_10_), channel_id=1, source_target_pairs={{0,1},{1,2},{2,3},{3,4},{4,5},{5,6},{6,7},{7,8},{8,9},{9,10},{10,1... | collective-permute-start | bytes 98312 | tf_op jit(solution)/shard_map/ppermute | solution.py:388
  130.3 9.4 %collective-permute-start.11 = (bf16[16,1024]{1,0:T(8,128)(2,1)S(1)}, bf16[16,1024]{1,0:T(8,128)(2,1)S(1)}, u32[]{:S(2)}, u32[]{:S(2)}) collective-permute-start(bf16[16,1024]{1,0:T(8,128)(2,1)S(1)} %get-tuple-element.40.refs_9_), channel_id=1, source_target_pairs={{1,0},{2,1},{3,2},{4,3},{5,4},{6,5},{7,6},{8,7},{9,8},{10,9},{11,1... | collective-permute-start | bytes 98312 | tf_op jit(solution)/shard_map/ppermute | solution.py:389

commit v5 on v4

--- a/solution.py
+++ b/solution.py
@@ -320,9 +320,7 @@
     swap = [(i, cores - 1 - i) for i in range(cores)]
     around = lambda cells: lax.ppermute(cells, NARROW, ring)
     across = lambda cells: lax.ppermute(cells, "c", swap)
-    held = [packed]
-    for _ in range(quarters - 2):
-        held.append(around(held[-1]))
+    held = [packed, around(packed)]
 
     def over(axis, cells):
         return lax.all_to_all(cells, axis, split_axis=0, concat_axis=0, tiled=True)
@@ -348,8 +346,11 @@
     partial = over("y", partial)
     summed = jnp.sum(partial.astype(jnp.float32), axis=0).astype(jnp.bfloat16)
     summed, *held = lax.optimization_barrier((summed, *held, *swapped))
-    held, swapped = held[:quarters], held[quarters:]
+    held, swapped = held[: quarters - 1], held[quarters - 1 :]
     swapped.append(across(held[-1]))
+    back = [(b, a) for a, b in ring]
+    held.append(lax.ppermute(held[0], NARROW, back))
+    swapped.append(lax.ppermute(held[0], NARROW, [(a, b ^ 1) for a, b in back]))
     returned = over(WIDE, summed.reshape(experts, slots, share)).reshape(rows, share)
     mixed = pl.pallas_call(
         combine_kernel,

time: 143 us -> 137 us (0.958)
  waiting for transfers between devices: 40.9 us -> 32.2 us
  starting transfers between devices: 69.1 us -> 72.5 us
    all_to_all x4, waiting for transfers between devices: 39.3 us -> 22.4 us  [over(): return lax.all_to_all(cells, axis, split_axis=0, concat_axis=0, tiled=True)]
    ppermute x0 -> x2, starting transfers between devices: none -> 5.31 us  [the longest x1 3.18 us: shards(): swapped.append(lax.ppermute(held[0], NARROW, [(a, b ^ 1) for a, b in back]))]
    ppermute x3 -> x2, waiting for transfers between devices: 0.01 us -> 4.99 us  [shards(): around = lambda cells: lax.ppermute(cells, NARROW, ring)]
    ppermute x3 -> x2, starting transfers between devices: 10.8 us -> 7.42 us  [shards(): around = lambda cells: lax.ppermute(cells, NARROW, ring)]
    ppermute x0 -> x2, waiting for transfers between devices: none -> 3.29 us  [the longest x1 3.28 us: shards(): held.append(lax.ppermute(held[0], NARROW, back))]
    all_to_all x4, starting transfers between devices: 34 us -> 37 us  [over(): return lax.all_to_all(cells, axis, split_axis=0, concat_axis=0, tiled=True)]
    ppermute x7 -> x6, starting transfers between devices: 14.4 us -> 12.9 us  [shards(): across = lambda cells: lax.ppermute(cells, 'c', swap)]
  transfers between devices with their start and end apart: 16 -> 16, of which waited for: 5 -> 7; matrix products, arithmetic and copies ran while one was open for 1% -> 1% of each run, Pallas kernels for 5% -> 5%
where the time goes in v5:
time: 137 us; the launch traced here: 136 us
  starting transfers between devices  72.5 us (53%)
  waiting for transfers between devices  32.2 us (24%)
  blocking collectives  15.2 us (11%)
  Pallas kernels  14 us (10%)
    all_to_all x4, starting transfers between devices, over(): return lax.all_to_all(cells, axis, split_axis=0, concat_axis=0, tiled=True)  37 us
    all_to_all x4, waiting for transfers between devices, over(): return lax.all_to_all(cells, axis, split_axis=0, concat_axis=0, tiled=True)  22.4 us
    all_to_all x1, blocking collectives, over(): return lax.all_to_all(cells, axis, split_axis=0, concat_axis=0, tiled=True)  15.2 us
    ppermute x6, starting transfers between devices, shards(): across = lambda cells: lax.ppermute(cells, 'c', swap)  12.9 us
    ppermute x1, starting transfers between devices, shards(): right = lax.ppermute(lo, EVERY, [(i + 1, i) for i in range(ends)])  7.86 us
    ppermute x2, starting transfers between devices, shards(): around = lambda cells: lax.ppermute(cells, NARROW, ring)  7.42 us
    pallas_call x1, Pallas kernels, shards(): pl.pallas_call(expert_kernel, in_specs=in_vmem(1) + in_hbm(6), out_specs=...  5.37 us
    ppermute x2, waiting for transfers between devices, shards(): around = lambda cells: lax.ppermute(cells, NARROW, ring)  4.99 us
  transfers between devices with their start and end apart: 16, of which 7 were waited for; matrix products, arithmetic and copies ran while one was open for 1% of the time, Pallas kernels for 5%

profile of v5, /device:TPU:6, one launch (start us, length us, event | category | flops | bytes accessed | tf_op | source)
XLA Modules:
  0.0 136.1 jit_solution(4868007765853102111)
XLA Ops:
  0.0 2.2 %prepare.1 = (bf16[512,256]{1,0:T(8,128)(2,1)}, f32[8,256]{1,0:T(8,128)S(1)}, bf16[3104,128]{1,0:T(8,128)(2,1)S(1)}) custom-call(s32[2,256]{1,0:T(2,128)} %bitcast.20, bf16[256,1024]{1,0:T(8,128)(2,1)} %refs_0_.1, bf16[2048,128]{1,0:T(8,128)(2,1)} %bitcast.19, bf16[31,128]{1,0:T(8,128)(2,1)} %refs_3_.1, bf16[128,1024]{1,0:T(8,128)(2,1)} %refs_4_.1, ...), custom_call_target="tpu_custom_call" | custom-call | tf_op jit(solution)/shard_map/prepare/pallas_call | solution.py:286
  2.2 18.8 %all-to-all-start = ((bf16[64,8,256]{2,1,0:T(8,128)(2,1)}), bf16[64,8,256]{2,1,0:T(8,128)(2,1)S(1)}, u32[]{:S(2)}, u32[]{:S(2)}) async-start(bf16[64,8,256]{2,1,0:T(8,128)(2,1)} %bitcast.3), calls=%async_computation | async-start | bytes 524288 | tf_op jit(solution)/shard_map/all_to_all | solution.py:326
  21.0 3.5 %collective-permute-start = (bf16[3104,128]{1,0:T(8,128)(2,1)S(1)}, bf16[3104,128]{1,0:T(8,128)(2,1)S(1)}, u32[]{:S(2)}, u32[]{:S(2)}) collective-permute-start(bf16[3104,128]{1,0:T(8,128)(2,1)S(1)} %get-tuple-element.26.refs_1_.refs_0_), channel_id=1, source_target_pairs={{0,2},{1,7},{2,4},{3,1},{4,6},{5,3},{6,0},{7,5},{8,10},{9,15},{10,... | collective-permute-start | bytes 2383880 | tf_op jit(solution)/shard_map/ppermute | solution.py:321
  24.5 2.3 %collective-permute-start.1 = (bf16[1024,512]{1,0:T(8,128)(2,1)}, bf16[1024,512]{1,0:T(8,128)(2,1)}, u32[]{:S(2)}, u32[]{:S(2)}) collective-permute-start(bf16[1024,512]{1,0:T(8,128)(2,1)} %bitcast.6.refs_0_), channel_id=1, source_target_pairs={{0,1},{1,0},{2,3},{3,2},{4,5},{5,4},{6,7},{7,6},{8,9},{9,8},{10,11... | collective-permute-start | bytes 3145736 | tf_op jit(solution)/shard_map/ppermute | solution.py:322
  26.9 2.0 %collective-permute-start.2 = (bf16[1024,512]{1,0:T(8,128)(2,1)}, bf16[1024,512]{1,0:T(8,128)(2,1)}, u32[]{:S(2)}, u32[]{:S(2)}) collective-permute-start(bf16[1024,512]{1,0:T(8,128)(2,1)} %bitcast.7.refs_1_), channel_id=1, source_target_pairs={{0,1},{1,0},{2,3},{3,2},{4,5},{5,4},{6,7},{7,6},{8,9},{9,8},{10,11... | collective-permute-start | bytes 3145736 | tf_op jit(solution)/shard_map/ppermute | solution.py:322
  28.9 2.3 %collective-permute-start.3 = (bf16[512,1024]{1,0:T(8,128)(2,1)}, bf16[512,1024]{1,0:T(8,128)(2,1)}, u32[]{:S(2)}, u32[]{:S(2)}) collective-permute-start(bf16[512,1024]{1,0:T(8,128)(2,1)} %bitcast.8.refs_2_), channel_id=1, source_target_pairs={{0,1},{1,0},{2,3},{3,2},{4,5},{5,4},{6,7},{7,6},{8,9},{9,8},{10,11... | collective-permute-start | bytes 3145736 | tf_op jit(solution)/shard_map/ppermute | solution.py:322
  31.2 5.0 %collective-permute-done.refs_2_.refs_1_ = bf16[3104,128]{1,0:T(8,128)(2,1)S(1)} collective-permute-done((bf16[3104,128]{1,0:T(8,128)(2,1)S(1)}, bf16[3104,128]{1,0:T(8,128)(2,1)S(1)}, u32[]{:S(2)}, u32[]{:S(2)}) %collective-permute-start) | collective-permute-done | bytes 794656 | tf_op jit(solution)/shard_map/ppermute | solution.py:321
  36.2 5.6 %all-to-all-done = bf16[64,8,256]{2,1,0:T(8,128)(2,1)S(1)} async-done(((bf16[64,8,256]{2,1,0:T(8,128)(2,1)}), bf16[64,8,256]{2,1,0:T(8,128)(2,1)S(1)}, u32[]{:S(2)}, u32[]{:S(2)}) %all-to-all-start) | async-done | bytes 262176 | tf_op jit(solution)/shard_map/all_to_all | solution.py:326
  41.8 1.0 broadcast_in_dim.14
  42.9 4.5 %all-to-all-start.1 = ((bf16[4,512,256]{2,1,0:T(8,128)(2,1)}), bf16[4,512,256]{2,1,0:T(8,128)(2,1)S(1)}, u32[]{:S(2)}, u32[]{:S(2)}) async-start(bf16[4,512,256]{2,1,0:T(8,128)(2,1)} %broadcast_in_dim.14), calls=%async_computation.1 | async-start | bytes 2097152 | tf_op jit(solution)/shard_map/all_to_all | solution.py:326
  47.3 1.9 %collective-permute-start.5 = (bf16[3104,128]{1,0:T(8,128)(2,1)S(1)}, bf16[3104,128]{1,0:T(8,128)(2,1)}, u32[]{:S(2)}, u32[]{:S(2)}) collective-permute-start(bf16[3104,128]{1,0:T(8,128)(2,1)S(1)} %get-tuple-element.26.refs_1_.refs_0_), channel_id=1, source_target_pairs={{0,1},{1,0},{2,3},{3,2},{4,5},{5,4},{6,7},{7,6},{8,9},{9,8},{10,11... | collective-permute-start | bytes 2383880 | tf_op jit(solution)/shard_map/ppermute | solution.py:322
  49.3 2.4 %collective-permute-start.6 = (bf16[3104,128]{1,0:T(8,128)(2,1)S(1)}, bf16[3104,128]{1,0:T(8,128)(2,1)}, u32[]{:S(2)}, u32[]{:S(2)}) collective-permute-start(bf16[3104,128]{1,0:T(8,128)(2,1)S(1)} %collective-permute-done.refs_2_.refs_1_), channel_id=1, source_target_pairs={{0,1},{1,0},{2,3},{3,2},{4,5},{5,4},{6,7},{7,6},{8,9},{9,8},{10,11... | collective-permute-start | bytes 2383880 | tf_op jit(solution)/shard_map/ppermute | solution.py:322
  51.7 0.0 collective-permute-done.1.refs_3_
  51.7 3.9 %collective-permute-start.4 = (bf16[3104,128]{1,0:T(8,128)(2,1)S(1)}, bf16[3104,128]{1,0:T(8,128)(2,1)S(1)}, u32[]{:S(2)}, u32[]{:S(2)}) collective-permute-start(bf16[3104,128]{1,0:T(8,128)(2,1)S(1)} %collective-permute-done.refs_2_.refs_1_), channel_id=1, source_target_pairs={{0,2},{1,7},{2,4},{3,1},{4,6},{5,3},{6,0},{7,5},{8,10},{9,15},{10,... | collective-permute-start | bytes 2383880 | tf_op jit(solution)/shard_map/ppermute | solution.py:321
  55.6 0.0 collective-permute-done.2.refs_4_
  55.6 0.0 collective-permute-done.3.refs_5_
  55.6 4.6 %all-to-all-done.1.x_ref = bf16[4,512,256]{2,1,0:T(8,128)(2,1)S(1)} async-done(((bf16[4,512,256]{2,1,0:T(8,128)(2,1)}), bf16[4,512,256]{2,1,0:T(8,128)(2,1)S(1)}, u32[]{:S(2)}, u32[]{:S(2)}) %all-to-all-start.1) | async-done | bytes 1048608 | tf_op jit(solution)/shard_map/all_to_all | solution.py:326
  60.3 5.4 %experts.1 = bf16[4,512,256]{2,1,0:T(8,128)(2,1)S(1)} custom-call(bf16[4,512,256]{2,1,0:T(8,128)(2,1)S(1)} %all-to-all-done.1.x_ref, bf16[1024,512]{1,0:T(8,128)(2,1)} %bitcast.6.refs_0_, bf16[1024,512]{1,0:T(8,128)(2,1)} %bitcast.7.refs_1_, bf16[512,1024]{1,0:T(8,128)(2,1)} %bitcast.8.refs_2_, bf16[1024,512]{1,0:T(8,128)(2,1)} %collective-permute-done.1.refs_3_, ...), custom_call_target="tpu_custom_call" | custom-call | tf_op jit(solution)/shard_map/experts/pallas_call | solution.py:336
  65.6 15.2 %all_to_all.25 = bf16[4,512,256]{2,1,0:T(8,128)(2,1)S(1)} all-to-all(bf16[4,512,256]{2,1,0:T(8,128)(2,1)S(1)} %experts.1), channel_id=1, replica_groups=mesh['x'=4,'z'=16,'y'=4,'c'=2] {'y'}, dimensions={0} | all-to-all | bytes 2097152 | tf_op jit(solution)/shard_map/all_to_all | solution.py:326
  80.8 0.9 reduce_sum.12
  81.8 0.0 collective-permute-done.5.refs_5_.refs_4_
  81.8 0.0 collective-permute-done.6.refs_6_.refs_5_
  81.8 0.0 collective-permute-done.4.refs_3_.refs_2_
  81.8 10.3 %all-to-all-start.3 = ((bf16[64,8,256]{2,1,0:T(8,128)(2,1)}), bf16[64,8,256]{2,1,0:T(8,128)(2,1)S(1)}, u32[]{:S(2)}, u32[]{:S(2)}) async-start(bf16[64,8,256]{2,1,0:T(8,128)(2,1)} %bitcast.18), calls=%async_computation.3 | async-start | bytes 524288 | tf_op jit(solution)/shard_map/all_to_all | solution.py:326
  92.1 1.9 %collective-permute-start.8 = (bf16[3104,128]{1,0:T(8,128)(2,1)S(1)}, bf16[3104,128]{1,0:T(8,128)(2,1)S(1)}, u32[]{:S(2)}, u32[]{:S(2)}) collective-permute-start(bf16[3104,128]{1,0:T(8,128)(2,1)S(1)} %collective-permute-done.4.refs_3_.refs_2_), channel_id=1, source_target_pairs={{0,1},{1,0},{2,3},{3,2},{4,5},{5,4},{6,7},{7,6},{8,9},{9,8},{10,11... | collective-permute-start | bytes 2383880 | tf_op jit(solution)/shard_map/ppermute | solution.py:322
  94.0 3.2 %collective-permute-start.9 = (bf16[3104,128]{1,0:T(8,128)(2,1)S(1)}, bf16[3104,128]{1,0:T(8,128)(2,1)}, u32[]{:S(2)}, u32[]{:S(2)}) collective-permute-start(bf16[3104,128]{1,0:T(8,128)(2,1)S(1)} %get-tuple-element.26.refs_1_.refs_0_), channel_id=1, source_target_pairs={{2,1},{7,0},{4,3},{1,2},{6,5},{3,4},{0,7},{5,6},{10,9},{15,8},{12,... | collective-permute-start | bytes 2383880 | tf_op jit(solution)/shard_map/ppermute | solution.py:353
  97.2 2.1 %collective-permute-start.7 = (bf16[3104,128]{1,0:T(8,128)(2,1)S(1)}, bf16[3104,128]{1,0:T(8,128)(2,1)}, u32[]{:S(2)}, u32[]{:S(2)}) collective-permute-start(bf16[3104,128]{1,0:T(8,128)(2,1)S(1)} %get-tuple-element.26.refs_1_.refs_0_), channel_id=1, source_target_pairs={{2,0},{7,1},{4,2},{1,3},{6,4},{3,5},{0,6},{5,7},{10,8},{15,9},{12,... | collective-permute-start | bytes 2383880 | tf_op jit(solution)/shard_map/ppermute | solution.py:352
  99.3 9.4 %all-to-all-done.3 = bf16[64,8,256]{2,1,0:T(8,128)(2,1)S(1)} async-done(((bf16[64,8,256]{2,1,0:T(8,128)(2,1)}), bf16[64,8,256]{2,1,0:T(8,128)(2,1)S(1)}, u32[]{:S(2)}, u32[]{:S(2)}) %all-to-all-start.3) | async-done | bytes 262176 | tf_op jit(solution)/shard_map/all_to_all | solution.py:326
  108.7 1.2 combine.1
  109.9 0.0 copy-start
  109.9 0.0 copy-start.1
  109.9 3.5 %all-to-all-start.4 = ((bf16[8,32,256]{2,1,0:T(8,128)(2,1)}), bf16[8,32,256]{2,1,0:T(8,128)(2,1)S(1)}, u32[]{:S(2)}, u32[]{:S(2)}) async-start(bf16[8,32,256]{2,1,0:T(8,128)(2,1)} %bitcast.11), calls=%async_computation.4 | async-start | bytes 262144 | tf_op jit(solution)/shard_map/all_to_all | solution.py:326
  113.4 0.0 collective-permute-done.8.refs_7_.refs_6_
  113.4 0.0 copy-start.2
  113.4 0.0 collective-permute-done.9.refs_8_.refs_7_
  113.4 3.3 %collective-permute-done.7.refs_4_.refs_3_ = bf16[3104,128]{1,0:T(8,128)(2,1)} collective-permute-done((bf16[3104,128]{1,0:T(8,128)(2,1)S(1)}, bf16[3104,128]{1,0:T(8,128)(2,1)}, u32[]{:S(2)}, u32[]{:S(2)}) %collective-permute-start.7) | collective-permute-done | bytes 794656 | tf_op jit(solution)/shard_map/ppermute | solution.py:352
  116.7 2.7 %all-to-all-done.4.refs_9_ = bf16[8,32,256]{2,1,0:T(8,128)(2,1)S(1)} async-done(((bf16[8,32,256]{2,1,0:T(8,128)(2,1)}), bf16[8,32,256]{2,1,0:T(8,128)(2,1)S(1)}, u32[]{:S(2)}, u32[]{:S(2)}) %all-to-all-start.4) | async-done | bytes 131104 | tf_op jit(solution)/shard_map/all_to_all | solution.py:326
  119.4 0.0 copy-done.2
  119.4 0.0 copy-done
  119.4 0.0 copy-done.1
  119.4 2.9 %norm_glu.1 = (f32[32,1024]{1,0:T(8,128)S(1)}, bf16[16,1024]{1,0:T(8,128)(2,1)S(1)}, bf16[16,1024]{1,0:T(8,128)(2,1)S(1)}, f32[32,1024]{1,0:T(8,128)S(1)}) custom-call(bf16[256,1024]{1,0:T(8,128)(2,1)} %refs_0_.1, bf16[3104,128]{1,0:T(8,128)(2,1)S(1)} %get-tuple-element.26.refs_1_.refs_0_, bf16[3104,128]{1,0:T(8,128)(2,1)S(1)} %collective-permute-done.refs_2_.refs_1_, ...), custom_call_target="tpu_custom_call" | custom-call | tf_op jit(solution)/shard_map/norm_glu/pallas_call | solution.py:369
  122.3 1.9 %collective-permute-start.10 = (bf16[16,1024]{1,0:T(8,128)(2,1)S(1)}, bf16[16,1024]{1,0:T(8,128)(2,1)S(1)}, u32[]{:S(2)}, u32[]{:S(2)}) collective-permute-start(bf16[16,1024]{1,0:T(8,128)(2,1)S(1)} %get-tuple-element.33.refs_10_), channel_id=1, source_target_pairs={{0,1},{1,2},{2,3},{3,4},{4,5},{5,6},{6,7},{7,8},{8,9},{9,10},{10,1... | collective-permute-start | bytes 98312 | tf_op jit(solution)/shard_map/ppermute | solution.py:389
  124.2 7.9 %collective-permute-start.11 = (bf16[16,1024]{1,0:T(8,128)(2,1)S(1)}, bf16[16,1024]{1,0:T(8,128)(2,1)S(1)}, u32[]{:S(2)}, u32[]{:S(2)}) collective-permute-start(bf16[16,1024]{1,0:T(8,128)(2,1)S(1)} %get-tuple-element.34.refs_9_), channel_id=1, source_target_pairs={{1,0},{2,1},{3,2},{4,3},{5,4},{6,5},{7,6},{8,7},{9,8},{10,9},{11,1... | collective-permute-start | bytes 98312 | tf_op jit(solution)/shard_map/ppermute | solution.py:390
  132.1 0.0 collective-permute-done.10.refs_8_
  132.1 1.6 %collective-permute-done.11.refs_11_ = bf16[16,1024]{1,0:T(8,128)(2,1)S(1)} collective-permute-done((bf16[16,1024]{1,0:T(8,128)(2,1)S(1)}, bf16[16,1024]{1,0:T(8,128)(2,1)S(1)}, u32[]{:S(2)}, u32[]{:S(2)}) %collective-permute-start.11) | collective-permute-done | bytes 32800 | tf_op jit(solution)/shard_map/ppermute | solution.py:390
  133.7 2.4 %conv.1 = bf16[32,1024]{1,0:T(8,128)(2,1)} custom-call(bf16[3104,128]{1,0:T(8,128)(2,1)S(1)} %get-tuple-element.26.refs_1_.refs_0_, bf16[3104,128]{1,0:T(8,128)(2,1)S(1)} %collective-permute-done.refs_2_.refs_1_, bf16[3104,128]{1,0:T(8,128)(2,1)S(1)} %collective-permute-done.4.refs_3_.refs_2_, bf16[3104,128]{1,0:T(8,128)(2,1)} %collective-permute-done.7.refs_4_.refs_3_, ...), custom_call_target="tpu_custom_call" | custom-call | tf_op jit(solution)/shard_map/conv/pallas_call | solution.py:391
Async XLA Ops:
  2.2 39.6 %all-to-all-start = ((bf16[64,8,256]{2,1,0:T(8,128)(2,1)}), bf16[64,8,256]{2,1,0:T(8,128)(2,1)S(1)}, u32[]{:S(2)}, u32[]{:S(2)}) async-start(bf16[64,8,256]{2,1,0:T(8,128)(2,1)} %bitcast.3), calls=%async_computation | async-start | bytes 524288 | tf_op jit(solution)/shard_map/all_to_all | solution.py:326
  21.0 15.2 %collective-permute-start = (bf16[3104,128]{1,0:T(8,128)(2,1)S(1)}, bf16[3104,128]{1,0:T(8,128)(2,1)S(1)}, u32[]{:S(2)}, u32[]{:S(2)}) collective-permute-start(bf16[3104,128]{1,0:T(8,128)(2,1)S(1)} %get-tuple-element.26.refs_1_.refs_0_), channel_id=1, source_target_pairs={{0,2},{1,7},{2,4},{3,1},{4,6},{5,3},{6,0},{7,5},{8,10},{9,15},{10,... | collective-permute-start | bytes 2383880 | tf_op jit(solution)/shard_map/ppermute | solution.py:321
  24.5 27.2 %collective-permute-start.1 = (bf16[1024,512]{1,0:T(8,128)(2,1)}, bf16[1024,512]{1,0:T(8,128)(2,1)}, u32[]{:S(2)}, u32[]{:S(2)}) collective-permute-start(bf16[1024,512]{1,0:T(8,128)(2,1)} %bitcast.6.refs_0_), channel_id=1, source_target_pairs={{0,1},{1,0},{2,3},{3,2},{4,5},{5,4},{6,7},{7,6},{8,9},{9,8},{10,11... | collective-permute-start | bytes 3145736 | tf_op jit(solution)/shard_map/ppermute | solution.py:322
  26.9 28.8 %collective-permute-start.2 = (bf16[1024,512]{1,0:T(8,128)(2,1)}, bf16[1024,512]{1,0:T(8,128)(2,1)}, u32[]{:S(2)}, u32[]{:S(2)}) collective-permute-start(bf16[1024,512]{1,0:T(8,128)(2,1)} %bitcast.7.refs_1_), channel_id=1, source_target_pairs={{0,1},{1,0},{2,3},{3,2},{4,5},{5,4},{6,7},{7,6},{8,9},{9,8},{10,11... | collective-permute-start | bytes 3145736 | tf_op jit(solution)/shard_map/ppermute | solution.py:322
  28.9 26.8 %collective-permute-start.3 = (bf16[512,1024]{1,0:T(8,128)(2,1)}, bf16[512,1024]{1,0:T(8,128)(2,1)}, u32[]{:S(2)}, u32[]{:S(2)}) collective-permute-start(bf16[512,1024]{1,0:T(8,128)(2,1)} %bitcast.8.refs_2_), channel_id=1, source_target_pairs={{0,1},{1,0},{2,3},{3,2},{4,5},{5,4},{6,7},{7,6},{8,9},{9,8},{10,11... | collective-permute-start | bytes 3145736 | tf_op jit(solution)/shard_map/ppermute | solution.py:322
  42.9 17.4 %all-to-all-start.1 = ((bf16[4,512,256]{2,1,0:T(8,128)(2,1)}), bf16[4,512,256]{2,1,0:T(8,128)(2,1)S(1)}, u32[]{:S(2)}, u32[]{:S(2)}) async-start(bf16[4,512,256]{2,1,0:T(8,128)(2,1)} %broadcast_in_dim.14), calls=%async_computation.1 | async-start | bytes 2097152 | tf_op jit(solution)/shard_map/all_to_all | solution.py:326
  47.3 34.4 %collective-permute-start.5 = (bf16[3104,128]{1,0:T(8,128)(2,1)S(1)}, bf16[3104,128]{1,0:T(8,128)(2,1)}, u32[]{:S(2)}, u32[]{:S(2)}) collective-permute-start(bf16[3104,128]{1,0:T(8,128)(2,1)S(1)} %get-tuple-element.26.refs_1_.refs_0_), channel_id=1, source_target_pairs={{0,1},{1,0},{2,3},{3,2},{4,5},{5,4},{6,7},{7,6},{8,9},{9,8},{10,11... | collective-permute-start | bytes 2383880 | tf_op jit(solution)/shard_map/ppermute | solution.py:322
  49.3 32.5 %collective-permute-start.6 = (bf16[3104,128]{1,0:T(8,128)(2,1)S(1)}, bf16[3104,128]{1,0:T(8,128)(2,1)}, u32[]{:S(2)}, u32[]{:S(2)}) collective-permute-start(bf16[3104,128]{1,0:T(8,128)(2,1)S(1)} %collective-permute-done.refs_2_.refs_1_), channel_id=1, source_target_pairs={{0,1},{1,0},{2,3},{3,2},{4,5},{5,4},{6,7},{7,6},{8,9},{9,8},{10,11... | collective-permute-start | bytes 2383880 | tf_op jit(solution)/shard_map/ppermute | solution.py:322
  51.7 30.1 %collective-permute-start.4 = (bf16[3104,128]{1,0:T(8,128)(2,1)S(1)}, bf16[3104,128]{1,0:T(8,128)(2,1)S(1)}, u32[]{:S(2)}, u32[]{:S(2)}) collective-permute-start(bf16[3104,128]{1,0:T(8,128)(2,1)S(1)} %collective-permute-done.refs_2_.refs_1_), channel_id=1, source_target_pairs={{0,2},{1,7},{2,4},{3,1},{4,6},{5,3},{6,0},{7,5},{8,10},{9,15},{10,... | collective-permute-start | bytes 2383880 | tf_op jit(solution)/shard_map/ppermute | solution.py:321
  81.8 26.9 %all-to-all-start.3 = ((bf16[64,8,256]{2,1,0:T(8,128)(2,1)}), bf16[64,8,256]{2,1,0:T(8,128)(2,1)S(1)}, u32[]{:S(2)}, u32[]{:S(2)}) async-start(bf16[64,8,256]{2,1,0:T(8,128)(2,1)} %bitcast.18), calls=%async_computation.3 | async-start | bytes 524288 | tf_op jit(solution)/shard_map/all_to_all | solution.py:326
  92.1 21.3 %collective-permute-start.8 = (bf16[3104,128]{1,0:T(8,128)(2,1)S(1)}, bf16[3104,128]{1,0:T(8,128)(2,1)S(1)}, u32[]{:S(2)}, u32[]{:S(2)}) collective-permute-start(bf16[3104,128]{1,0:T(8,128)(2,1)S(1)} %collective-permute-done.4.refs_3_.refs_2_), channel_id=1, source_target_pairs={{0,1},{1,0},{2,3},{3,2},{4,5},{5,4},{6,7},{7,6},{8,9},{9,8},{10,11... | collective-permute-start | bytes 2383880 | tf_op jit(solution)/shard_map/ppermute | solution.py:322
  94.0 19.4 %collective-permute-start.9 = (bf16[3104,128]{1,0:T(8,128)(2,1)S(1)}, bf16[3104,128]{1,0:T(8,128)(2,1)}, u32[]{:S(2)}, u32[]{:S(2)}) collective-permute-start(bf16[3104,128]{1,0:T(8,128)(2,1)S(1)} %get-tuple-element.26.refs_1_.refs_0_), channel_id=1, source_target_pairs={{2,1},{7,0},{4,3},{1,2},{6,5},{3,4},{0,7},{5,6},{10,9},{15,8},{12,... | collective-permute-start | bytes 2383880 | tf_op jit(solution)/shard_map/ppermute | solution.py:353
  97.2 19.5 %collective-permute-start.7 = (bf16[3104,128]{1,0:T(8,128)(2,1)S(1)}, bf16[3104,128]{1,0:T(8,128)(2,1)}, u32[]{:S(2)}, u32[]{:S(2)}) collective-permute-start(bf16[3104,128]{1,0:T(8,128)(2,1)S(1)} %get-tuple-element.26.refs_1_.refs_0_), channel_id=1, source_target_pairs={{2,0},{7,1},{4,2},{1,3},{6,4},{3,5},{0,6},{5,7},{10,8},{15,9},{12,... | collective-permute-start | bytes 2383880 | tf_op jit(solution)/shard_map/ppermute | solution.py:352
  109.9 9.6 %copy-start = (f32[1024]{0:T(1024)S(1)}, f32[1024]{0:T(1024)}, u32[]{:S(2)}) copy-start(f32[1024]{0:T(1024)} %param.17) | copy-start | bytes 12292
  109.9 9.6 %copy-start.1 = (f32[1024]{0:T(1024)S(1)}, f32[1024]{0:T(1024)}, u32[]{:S(2)}) copy-start(f32[1024]{0:T(1024)} %param.18) | copy-start | bytes 12292
  109.9 9.6 %all-to-all-start.4 = ((bf16[8,32,256]{2,1,0:T(8,128)(2,1)}), bf16[8,32,256]{2,1,0:T(8,128)(2,1)S(1)}, u32[]{:S(2)}, u32[]{:S(2)}) async-start(bf16[8,32,256]{2,1,0:T(8,128)(2,1)} %bitcast.11), calls=%async_computation.4 | async-start | bytes 262144 | tf_op jit(solution)/shard_map/all_to_all | solution.py:326
  113.4 6.0 %copy-start.2 = (bf16[3104,128]{1,0:T(8,128)(2,1)}, bf16[3104,128]{1,0:T(8,128)(2,1)S(1)}, u32[]{:S(2)}) copy-start(bf16[3104,128]{1,0:T(8,128)(2,1)S(1)} %collective-permute-done.8.refs_7_.refs_6_) | copy-start | bytes 2383876
  122.3 9.8 %collective-permute-start.10 = (bf16[16,1024]{1,0:T(8,128)(2,1)S(1)}, bf16[16,1024]{1,0:T(8,128)(2,1)S(1)}, u32[]{:S(2)}, u32[]{:S(2)}) collective-permute-start(bf16[16,1024]{1,0:T(8,128)(2,1)S(1)} %get-tuple-element.33.refs_10_), channel_id=1, source_target_pairs={{0,1},{1,2},{2,3},{3,4},{4,5},{5,6},{6,7},{7,8},{8,9},{9,10},{10,1... | collective-permute-start | bytes 98312 | tf_op jit(solution)/shard_map/ppermute | solution.py:389
  124.2 9.4 %collective-permute-start.11 = (bf16[16,1024]{1,0:T(8,128)(2,1)S(1)}, bf16[16,1024]{1,0:T(8,128)(2,1)S(1)}, u32[]{:S(2)}, u32[]{:S(2)}) collective-permute-start(bf16[16,1024]{1,0:T(8,128)(2,1)S(1)} %get-tuple-element.34.refs_9_), channel_id=1, source_target_pairs={{1,0},{2,1},{3,2},{4,3},{5,4},{6,5},{7,6},{8,7},{9,8},{10,9},{11,1... | collective-permute-start | bytes 98312 | tf_op jit(solution)/shard_map/ppermute | solution.py:390

commit v6 on v5

--- a/solution.py
+++ b/solution.py
@@ -142,7 +142,7 @@
 def blocks_of(quarters, cores, near):
     y, c = lax.axis_index("y"), lax.axis_index("c")
     index = [
-        lax.rem(y + (2 * side - 1) * step + quarters, quarters) * cores + side
+        lax.rem(y + (1 - 2 * side) * step + quarters, quarters) * cores + side
         for side in (c, cores - 1 - c)
         for step in range(quarters)
     ]
@@ -313,7 +313,7 @@
     )
 
     ring = [
-        (y * cores + c, (y + 1 - 2 * c) % quarters * cores + c)
+        (y * cores + c, (y - 1 + 2 * c) % quarters * cores + c)
         for y in range(quarters)
         for c in range(cores)
     ]

time: 137 us -> 136 us (level)
  blocking collectives: 15.2 us -> 13.3 us
    ppermute x2, starting transfers between devices: 7.42 us -> 10.1 us  [shards(): around = lambda cells: lax.ppermute(cells, NARROW, ring)]
    all_to_all x1, blocking collectives: 15.2 us -> 13.3 us  [over(): return lax.all_to_all(cells, axis, split_axis=0, concat_axis=0, tiled=True)]
    ppermute x2, waiting for transfers between devices: 4.99 us -> 3.3 us  [shards(): around = lambda cells: lax.ppermute(cells, NARROW, ring)]
where the time goes in v6:
time: 136 us; the launch traced here: 135 us
  starting transfers between devices  73.3 us (54%)
  waiting for transfers between devices  31.8 us (23%)
  Pallas kernels  14 us (10%)
  blocking collectives  13.3 us (10%)
    all_to_all x4, starting transfers between devices, over(): return lax.all_to_all(cells, axis, split_axis=0, concat_axis=0, tiled=True)  36.3 us
    all_to_all x4, waiting for transfers between devices, over(): return lax.all_to_all(cells, axis, split_axis=0, concat_axis=0, tiled=True)  22.5 us
    all_to_all x1, blocking collectives, over(): return lax.all_to_all(cells, axis, split_axis=0, concat_axis=0, tiled=True)  13.3 us
    ppermute x6, starting transfers between devices, shards(): across = lambda cells: lax.ppermute(cells, 'c', swap)  12.5 us
    ppermute x2, starting transfers between devices, shards(): around = lambda cells: lax.ppermute(cells, NARROW, ring)  10.1 us
    ppermute x1, starting transfers between devices, shards(): right = lax.ppermute(lo, EVERY, [(i + 1, i) for i in range(ends)])  7.86 us
    pallas_call x1, Pallas kernels, shards(): pl.pallas_call(expert_kernel, in_specs=in_vmem(1) + in_hbm(6), out_specs=...  5.38 us
    ppermute x1, waiting for transfers between devices, shards(): held.append(lax.ppermute(held[0], NARROW, back))  4.48 us
  transfers between devices with their start and end apart: 16, of which 7 were waited for; matrix products, arithmetic and copies ran while one was open for 1% of the time, Pallas kernels for 5%

profile of v6, /device:TPU:6, one launch (start us, length us, event | category | flops | bytes accessed | tf_op | source)
XLA Modules:
  0.0 134.7 jit_solution(5218436207500539816)
XLA Ops:
  0.0 2.2 %prepare.1 = (bf16[512,256]{1,0:T(8,128)(2,1)}, f32[8,256]{1,0:T(8,128)S(1)}, bf16[3104,128]{1,0:T(8,128)(2,1)S(1)}) custom-call(s32[2,256]{1,0:T(2,128)} %bitcast.20, bf16[256,1024]{1,0:T(8,128)(2,1)} %refs_0_.1, bf16[2048,128]{1,0:T(8,128)(2,1)} %bitcast.19, bf16[31,128]{1,0:T(8,128)(2,1)} %refs_3_.1, bf16[128,1024]{1,0:T(8,128)(2,1)} %refs_4_.1, ...), custom_call_target="tpu_custom_call" | custom-call | tf_op jit(solution)/shard_map/prepare/pallas_call | solution.py:286
  2.2 18.8 %all-to-all-start = ((bf16[64,8,256]{2,1,0:T(8,128)(2,1)}), bf16[64,8,256]{2,1,0:T(8,128)(2,1)S(1)}, u32[]{:S(2)}, u32[]{:S(2)}) async-start(bf16[64,8,256]{2,1,0:T(8,128)(2,1)} %bitcast.3), calls=%async_computation | async-start | bytes 524288 | tf_op jit(solution)/shard_map/all_to_all | solution.py:326
  21.0 4.9 %collective-permute-start = (bf16[3104,128]{1,0:T(8,128)(2,1)S(1)}, bf16[3104,128]{1,0:T(8,128)(2,1)S(1)}, u32[]{:S(2)}, u32[]{:S(2)}) collective-permute-start(bf16[3104,128]{1,0:T(8,128)(2,1)S(1)} %get-tuple-element.26.refs_1_.refs_0_), channel_id=1, source_target_pairs={{0,6},{1,3},{2,0},{3,5},{4,2},{5,7},{6,4},{7,1},{8,14},{9,11},{10,... | collective-permute-start | bytes 2383880 | tf_op jit(solution)/shard_map/ppermute | solution.py:321
  26.0 1.9 %collective-permute-start.1 = (bf16[1024,512]{1,0:T(8,128)(2,1)}, bf16[1024,512]{1,0:T(8,128)(2,1)}, u32[]{:S(2)}, u32[]{:S(2)}) collective-permute-start(bf16[1024,512]{1,0:T(8,128)(2,1)} %bitcast.6.refs_0_), channel_id=1, source_target_pairs={{0,1},{1,0},{2,3},{3,2},{4,5},{5,4},{6,7},{7,6},{8,9},{9,8},{10,11... | collective-permute-start | bytes 3145736 | tf_op jit(solution)/shard_map/ppermute | solution.py:322
  27.9 2.4 %collective-permute-start.2 = (bf16[1024,512]{1,0:T(8,128)(2,1)}, bf16[1024,512]{1,0:T(8,128)(2,1)}, u32[]{:S(2)}, u32[]{:S(2)}) collective-permute-start(bf16[1024,512]{1,0:T(8,128)(2,1)} %bitcast.7.refs_1_), channel_id=1, source_target_pairs={{0,1},{1,0},{2,3},{3,2},{4,5},{5,4},{6,7},{7,6},{8,9},{9,8},{10,11... | collective-permute-start | bytes 3145736 | tf_op jit(solution)/shard_map/ppermute | solution.py:322
  30.3 1.9 %collective-permute-start.3 = (bf16[512,1024]{1,0:T(8,128)(2,1)}, bf16[512,1024]{1,0:T(8,128)(2,1)}, u32[]{:S(2)}, u32[]{:S(2)}) collective-permute-start(bf16[512,1024]{1,0:T(8,128)(2,1)} %bitcast.8.refs_2_), channel_id=1, source_target_pairs={{0,1},{1,0},{2,3},{3,2},{4,5},{5,4},{6,7},{7,6},{8,9},{9,8},{10,11... | collective-permute-start | bytes 3145736 | tf_op jit(solution)/shard_map/ppermute | solution.py:322
  32.2 3.3 %collective-permute-done.refs_2_.refs_1_ = bf16[3104,128]{1,0:T(8,128)(2,1)S(1)} collective-permute-done((bf16[3104,128]{1,0:T(8,128)(2,1)S(1)}, bf16[3104,128]{1,0:T(8,128)(2,1)S(1)}, u32[]{:S(2)}, u32[]{:S(2)}) %collective-permute-start) | collective-permute-done | bytes 794656 | tf_op jit(solution)/shard_map/ppermute | solution.py:321
  35.5 6.3 %all-to-all-done = bf16[64,8,256]{2,1,0:T(8,128)(2,1)S(1)} async-done(((bf16[64,8,256]{2,1,0:T(8,128)(2,1)}), bf16[64,8,256]{2,1,0:T(8,128)(2,1)S(1)}, u32[]{:S(2)}, u32[]{:S(2)}) %all-to-all-start) | async-done | bytes 262176 | tf_op jit(solution)/shard_map/all_to_all | solution.py:326
  41.8 1.0 broadcast_in_dim.14
  42.9 4.5 %all-to-all-start.1 = ((bf16[4,512,256]{2,1,0:T(8,128)(2,1)}), bf16[4,512,256]{2,1,0:T(8,128)(2,1)S(1)}, u32[]{:S(2)}, u32[]{:S(2)}) async-start(bf16[4,512,256]{2,1,0:T(8,128)(2,1)} %broadcast_in_dim.14), calls=%async_computation.1 | async-start | bytes 2097152 | tf_op jit(solution)/shard_map/all_to_all | solution.py:326
  47.3 1.9 %collective-permute-start.5 = (bf16[3104,128]{1,0:T(8,128)(2,1)S(1)}, bf16[3104,128]{1,0:T(8,128)(2,1)}, u32[]{:S(2)}, u32[]{:S(2)}) collective-permute-start(bf16[3104,128]{1,0:T(8,128)(2,1)S(1)} %get-tuple-element.26.refs_1_.refs_0_), channel_id=1, source_target_pairs={{0,1},{1,0},{2,3},{3,2},{4,5},{5,4},{6,7},{7,6},{8,9},{9,8},{10,11... | collective-permute-start | bytes 2383880 | tf_op jit(solution)/shard_map/ppermute | solution.py:322
  49.3 2.4 %collective-permute-start.6 = (bf16[3104,128]{1,0:T(8,128)(2,1)S(1)}, bf16[3104,128]{1,0:T(8,128)(2,1)}, u32[]{:S(2)}, u32[]{:S(2)}) collective-permute-start(bf16[3104,128]{1,0:T(8,128)(2,1)S(1)} %collective-permute-done.refs_2_.refs_1_), channel_id=1, source_target_pairs={{0,1},{1,0},{2,3},{3,2},{4,5},{5,4},{6,7},{7,6},{8,9},{9,8},{10,11... | collective-permute-start | bytes 2383880 | tf_op jit(solution)/shard_map/ppermute | solution.py:322
  51.7 0.0 collective-permute-done.1.refs_3_
  51.7 5.1 %collective-permute-start.4 = (bf16[3104,128]{1,0:T(8,128)(2,1)S(1)}, bf16[3104,128]{1,0:T(8,128)(2,1)S(1)}, u32[]{:S(2)}, u32[]{:S(2)}) collective-permute-start(bf16[3104,128]{1,0:T(8,128)(2,1)S(1)} %collective-permute-done.refs_2_.refs_1_), channel_id=1, source_target_pairs={{0,6},{1,3},{2,0},{3,5},{4,2},{5,7},{6,4},{7,1},{8,14},{9,11},{10,... | collective-permute-start | bytes 2383880 | tf_op jit(solution)/shard_map/ppermute | solution.py:321
  56.8 0.0 collective-permute-done.2.refs_4_
  56.9 0.0 collective-permute-done.3.refs_5_
  56.9 4.6 %all-to-all-done.1.x_ref = bf16[4,512,256]{2,1,0:T(8,128)(2,1)S(1)} async-done(((bf16[4,512,256]{2,1,0:T(8,128)(2,1)}), bf16[4,512,256]{2,1,0:T(8,128)(2,1)S(1)}, u32[]{:S(2)}, u32[]{:S(2)}) %all-to-all-start.1) | async-done | bytes 1048608 | tf_op jit(solution)/shard_map/all_to_all | solution.py:326
  61.5 5.4 %experts.1 = bf16[4,512,256]{2,1,0:T(8,128)(2,1)S(1)} custom-call(bf16[4,512,256]{2,1,0:T(8,128)(2,1)S(1)} %all-to-all-done.1.x_ref, bf16[1024,512]{1,0:T(8,128)(2,1)} %bitcast.6.refs_0_, bf16[1024,512]{1,0:T(8,128)(2,1)} %bitcast.7.refs_1_, bf16[512,1024]{1,0:T(8,128)(2,1)} %bitcast.8.refs_2_, bf16[1024,512]{1,0:T(8,128)(2,1)} %collective-permute-done.1.refs_3_, ...), custom_call_target="tpu_custom_call" | custom-call | tf_op jit(solution)/shard_map/experts/pallas_call | solution.py:336
  66.8 13.3 %all_to_all.25 = bf16[4,512,256]{2,1,0:T(8,128)(2,1)S(1)} all-to-all(bf16[4,512,256]{2,1,0:T(8,128)(2,1)S(1)} %experts.1), channel_id=1, replica_groups=mesh['x'=4,'z'=16,'y'=4,'c'=2] {'y'}, dimensions={0} | all-to-all | bytes 2097152 | tf_op jit(solution)/shard_map/all_to_all | solution.py:326
  80.2 0.9 reduce_sum.12
  81.1 0.0 collective-permute-done.5.refs_5_.refs_4_
  81.1 0.0 collective-permute-done.6.refs_6_.refs_5_
  81.1 0.0 collective-permute-done.4.refs_3_.refs_2_
  81.1 9.5 %all-to-all-start.3 = ((bf16[64,8,256]{2,1,0:T(8,128)(2,1)}), bf16[64,8,256]{2,1,0:T(8,128)(2,1)S(1)}, u32[]{:S(2)}, u32[]{:S(2)}) async-start(bf16[64,8,256]{2,1,0:T(8,128)(2,1)} %bitcast.18), calls=%async_computation.3 | async-start | bytes 524288 | tf_op jit(solution)/shard_map/all_to_all | solution.py:326
  90.6 1.9 %collective-permute-start.8 = (bf16[3104,128]{1,0:T(8,128)(2,1)S(1)}, bf16[3104,128]{1,0:T(8,128)(2,1)S(1)}, u32[]{:S(2)}, u32[]{:S(2)}) collective-permute-start(bf16[3104,128]{1,0:T(8,128)(2,1)S(1)} %collective-permute-done.4.refs_3_.refs_2_), channel_id=1, source_target_pairs={{0,1},{1,0},{2,3},{3,2},{4,5},{5,4},{6,7},{7,6},{8,9},{9,8},{10,11... | collective-permute-start | bytes 2383880 | tf_op jit(solution)/shard_map/ppermute | solution.py:322
  92.5 2.6 %collective-permute-start.9 = (bf16[3104,128]{1,0:T(8,128)(2,1)S(1)}, bf16[3104,128]{1,0:T(8,128)(2,1)}, u32[]{:S(2)}, u32[]{:S(2)}) collective-permute-start(bf16[3104,128]{1,0:T(8,128)(2,1)S(1)} %get-tuple-element.26.refs_1_.refs_0_), channel_id=1, source_target_pairs={{6,1},{3,0},{0,3},{5,2},{2,5},{7,4},{4,7},{1,6},{14,9},{11,8},{8,1... | collective-permute-start | bytes 2383880 | tf_op jit(solution)/shard_map/ppermute | solution.py:353
  95.1 2.1 %collective-permute-start.7 = (bf16[3104,128]{1,0:T(8,128)(2,1)S(1)}, bf16[3104,128]{1,0:T(8,128)(2,1)}, u32[]{:S(2)}, u32[]{:S(2)}) collective-permute-start(bf16[3104,128]{1,0:T(8,128)(2,1)S(1)} %get-tuple-element.26.refs_1_.refs_0_), channel_id=1, source_target_pairs={{6,0},{3,1},{0,2},{5,3},{2,4},{7,5},{4,6},{1,7},{14,8},{11,9},{8,1... | collective-permute-start | bytes 2383880 | tf_op jit(solution)/shard_map/ppermute | solution.py:352
  97.3 10.0 %all-to-all-done.3 = bf16[64,8,256]{2,1,0:T(8,128)(2,1)S(1)} async-done(((bf16[64,8,256]{2,1,0:T(8,128)(2,1)}), bf16[64,8,256]{2,1,0:T(8,128)(2,1)S(1)}, u32[]{:S(2)}, u32[]{:S(2)}) %all-to-all-start.3) | async-done | bytes 262176 | tf_op jit(solution)/shard_map/all_to_all | solution.py:326
  107.3 1.2 combine.1
  108.4 0.0 copy-start
  108.4 0.0 copy-start.1
  108.4 3.5 %all-to-all-start.4 = ((bf16[8,32,256]{2,1,0:T(8,128)(2,1)}), bf16[8,32,256]{2,1,0:T(8,128)(2,1)S(1)}, u32[]{:S(2)}, u32[]{:S(2)}) async-start(bf16[8,32,256]{2,1,0:T(8,128)(2,1)} %bitcast.11), calls=%async_computation.4 | async-start | bytes 262144 | tf_op jit(solution)/shard_map/all_to_all | solution.py:326
  111.9 0.0 collective-permute-done.8.refs_7_.refs_6_
  111.9 0.0 copy-start.2
  112.0 0.0 collective-permute-done.9.refs_8_.refs_7_
  112.0 4.5 %collective-permute-done.7.refs_4_.refs_3_ = bf16[3104,128]{1,0:T(8,128)(2,1)} collective-permute-done((bf16[3104,128]{1,0:T(8,128)(2,1)S(1)}, bf16[3104,128]{1,0:T(8,128)(2,1)}, u32[]{:S(2)}, u32[]{:S(2)}) %collective-permute-start.7) | collective-permute-done | bytes 794656 | tf_op jit(solution)/shard_map/ppermute | solution.py:352
  116.4 1.5 %all-to-all-done.4.refs_9_ = bf16[8,32,256]{2,1,0:T(8,128)(2,1)S(1)} async-done(((bf16[8,32,256]{2,1,0:T(8,128)(2,1)}), bf16[8,32,256]{2,1,0:T(8,128)(2,1)S(1)}, u32[]{:S(2)}, u32[]{:S(2)}) %all-to-all-start.4) | async-done | bytes 131104 | tf_op jit(solution)/shard_map/all_to_all | solution.py:326
  118.0 0.0 copy-done.2
  118.0 0.0 copy-done
  118.0 0.0 copy-done.1
  118.0 2.9 %norm_glu.1 = (f32[32,1024]{1,0:T(8,128)S(1)}, bf16[16,1024]{1,0:T(8,128)(2,1)S(1)}, bf16[16,1024]{1,0:T(8,128)(2,1)S(1)}, f32[32,1024]{1,0:T(8,128)S(1)}) custom-call(bf16[256,1024]{1,0:T(8,128)(2,1)} %refs_0_.1, bf16[3104,128]{1,0:T(8,128)(2,1)S(1)} %get-tuple-element.26.refs_1_.refs_0_, bf16[3104,128]{1,0:T(8,128)(2,1)S(1)} %collective-permute-done.refs_2_.refs_1_, ...), custom_call_target="tpu_custom_call" | custom-call | tf_op jit(solution)/shard_map/norm_glu/pallas_call | solution.py:369
  120.9 1.9 %collective-permute-start.10 = (bf16[16,1024]{1,0:T(8,128)(2,1)S(1)}, bf16[16,1024]{1,0:T(8,128)(2,1)S(1)}, u32[]{:S(2)}, u32[]{:S(2)}) collective-permute-start(bf16[16,1024]{1,0:T(8,128)(2,1)S(1)} %get-tuple-element.33.refs_10_), channel_id=1, source_target_pairs={{0,1},{1,2},{2,3},{3,4},{4,5},{5,6},{6,7},{7,8},{8,9},{9,10},{10,1... | collective-permute-start | bytes 98312 | tf_op jit(solution)/shard_map/ppermute | solution.py:389
  122.8 7.9 %collective-permute-start.11 = (bf16[16,1024]{1,0:T(8,128)(2,1)S(1)}, bf16[16,1024]{1,0:T(8,128)(2,1)S(1)}, u32[]{:S(2)}, u32[]{:S(2)}) collective-permute-start(bf16[16,1024]{1,0:T(8,128)(2,1)S(1)} %get-tuple-element.34.refs_9_), channel_id=1, source_target_pairs={{1,0},{2,1},{3,2},{4,3},{5,4},{6,5},{7,6},{8,7},{9,8},{10,9},{11,1... | collective-permute-start | bytes 98312 | tf_op jit(solution)/shard_map/ppermute | solution.py:390
  130.7 0.0 collective-permute-done.10.refs_8_
  130.7 1.6 %collective-permute-done.11.refs_11_ = bf16[16,1024]{1,0:T(8,128)(2,1)S(1)} collective-permute-done((bf16[16,1024]{1,0:T(8,128)(2,1)S(1)}, bf16[16,1024]{1,0:T(8,128)(2,1)S(1)}, u32[]{:S(2)}, u32[]{:S(2)}) %collective-permute-start.11) | collective-permute-done | bytes 32800 | tf_op jit(solution)/shard_map/ppermute | solution.py:390
  132.3 2.4 %conv.1 = bf16[32,1024]{1,0:T(8,128)(2,1)} custom-call(bf16[3104,128]{1,0:T(8,128)(2,1)S(1)} %get-tuple-element.26.refs_1_.refs_0_, bf16[3104,128]{1,0:T(8,128)(2,1)S(1)} %collective-permute-done.refs_2_.refs_1_, bf16[3104,128]{1,0:T(8,128)(2,1)S(1)} %collective-permute-done.4.refs_3_.refs_2_, bf16[3104,128]{1,0:T(8,128)(2,1)} %collective-permute-done.7.refs_4_.refs_3_, ...), custom_call_target="tpu_custom_call" | custom-call | tf_op jit(solution)/shard_map/conv/pallas_call | solution.py:391
Async XLA Ops:
  2.2 39.6 %all-to-all-start = ((bf16[64,8,256]{2,1,0:T(8,128)(2,1)}), bf16[64,8,256]{2,1,0:T(8,128)(2,1)S(1)}, u32[]{:S(2)}, u32[]{:S(2)}) async-start(bf16[64,8,256]{2,1,0:T(8,128)(2,1)} %bitcast.3), calls=%async_computation | async-start | bytes 524288 | tf_op jit(solution)/shard_map/all_to_all | solution.py:326
  21.0 14.5 %collective-permute-start = (bf16[3104,128]{1,0:T(8,128)(2,1)S(1)}, bf16[3104,128]{1,0:T(8,128)(2,1)S(1)}, u32[]{:S(2)}, u32[]{:S(2)}) collective-permute-start(bf16[3104,128]{1,0:T(8,128)(2,1)S(1)} %get-tuple-element.26.refs_1_.refs_0_), channel_id=1, source_target_pairs={{0,6},{1,3},{2,0},{3,5},{4,2},{5,7},{6,4},{7,1},{8,14},{9,11},{10,... | collective-permute-start | bytes 2383880 | tf_op jit(solution)/shard_map/ppermute | solution.py:321
  26.0 25.7 %collective-permute-start.1 = (bf16[1024,512]{1,0:T(8,128)(2,1)}, bf16[1024,512]{1,0:T(8,128)(2,1)}, u32[]{:S(2)}, u32[]{:S(2)}) collective-permute-start(bf16[1024,512]{1,0:T(8,128)(2,1)} %bitcast.6.refs_0_), channel_id=1, source_target_pairs={{0,1},{1,0},{2,3},{3,2},{4,5},{5,4},{6,7},{7,6},{8,9},{9,8},{10,11... | collective-permute-start | bytes 3145736 | tf_op jit(solution)/shard_map/ppermute | solution.py:322
  27.9 29.0 %collective-permute-start.2 = (bf16[1024,512]{1,0:T(8,128)(2,1)}, bf16[1024,512]{1,0:T(8,128)(2,1)}, u32[]{:S(2)}, u32[]{:S(2)}) collective-permute-start(bf16[1024,512]{1,0:T(8,128)(2,1)} %bitcast.7.refs_1_), channel_id=1, source_target_pairs={{0,1},{1,0},{2,3},{3,2},{4,5},{5,4},{6,7},{7,6},{8,9},{9,8},{10,11... | collective-permute-start | bytes 3145736 | tf_op jit(solution)/shard_map/ppermute | solution.py:322
  30.3 26.5 %collective-permute-start.3 = (bf16[512,1024]{1,0:T(8,128)(2,1)}, bf16[512,1024]{1,0:T(8,128)(2,1)}, u32[]{:S(2)}, u32[]{:S(2)}) collective-permute-start(bf16[512,1024]{1,0:T(8,128)(2,1)} %bitcast.8.refs_2_), channel_id=1, source_target_pairs={{0,1},{1,0},{2,3},{3,2},{4,5},{5,4},{6,7},{7,6},{8,9},{9,8},{10,11... | collective-permute-start | bytes 3145736 | tf_op jit(solution)/shard_map/ppermute | solution.py:322
  42.9 18.6 %all-to-all-start.1 = ((bf16[4,512,256]{2,1,0:T(8,128)(2,1)}), bf16[4,512,256]{2,1,0:T(8,128)(2,1)S(1)}, u32[]{:S(2)}, u32[]{:S(2)}) async-start(bf16[4,512,256]{2,1,0:T(8,128)(2,1)} %broadcast_in_dim.14), calls=%async_computation.1 | async-start | bytes 2097152 | tf_op jit(solution)/shard_map/all_to_all | solution.py:326
  47.3 33.7 %collective-permute-start.5 = (bf16[3104,128]{1,0:T(8,128)(2,1)S(1)}, bf16[3104,128]{1,0:T(8,128)(2,1)}, u32[]{:S(2)}, u32[]{:S(2)}) collective-permute-start(bf16[3104,128]{1,0:T(8,128)(2,1)S(1)} %get-tuple-element.26.refs_1_.refs_0_), channel_id=1, source_target_pairs={{0,1},{1,0},{2,3},{3,2},{4,5},{5,4},{6,7},{7,6},{8,9},{9,8},{10,11... | collective-permute-start | bytes 2383880 | tf_op jit(solution)/shard_map/ppermute | solution.py:322
  49.3 31.8 %collective-permute-start.6 = (bf16[3104,128]{1,0:T(8,128)(2,1)S(1)}, bf16[3104,128]{1,0:T(8,128)(2,1)}, u32[]{:S(2)}, u32[]{:S(2)}) collective-permute-start(bf16[3104,128]{1,0:T(8,128)(2,1)S(1)} %collective-permute-done.refs_2_.refs_1_), channel_id=1, source_target_pairs={{0,1},{1,0},{2,3},{3,2},{4,5},{5,4},{6,7},{7,6},{8,9},{9,8},{10,11... | collective-permute-start | bytes 2383880 | tf_op jit(solution)/shard_map/ppermute | solution.py:322
  51.7 29.4 %collective-permute-start.4 = (bf16[3104,128]{1,0:T(8,128)(2,1)S(1)}, bf16[3104,128]{1,0:T(8,128)(2,1)S(1)}, u32[]{:S(2)}, u32[]{:S(2)}) collective-permute-start(bf16[3104,128]{1,0:T(8,128)(2,1)S(1)} %collective-permute-done.refs_2_.refs_1_), channel_id=1, source_target_pairs={{0,6},{1,3},{2,0},{3,5},{4,2},{5,7},{6,4},{7,1},{8,14},{9,11},{10,... | collective-permute-start | bytes 2383880 | tf_op jit(solution)/shard_map/ppermute | solution.py:321
  81.1 26.2 %all-to-all-start.3 = ((bf16[64,8,256]{2,1,0:T(8,128)(2,1)}), bf16[64,8,256]{2,1,0:T(8,128)(2,1)S(1)}, u32[]{:S(2)}, u32[]{:S(2)}) async-start(bf16[64,8,256]{2,1,0:T(8,128)(2,1)} %bitcast.18), calls=%async_computation.3 | async-start | bytes 524288 | tf_op jit(solution)/shard_map/all_to_all | solution.py:326
  90.6 21.3 %collective-permute-start.8 = (bf16[3104,128]{1,0:T(8,128)(2,1)S(1)}, bf16[3104,128]{1,0:T(8,128)(2,1)S(1)}, u32[]{:S(2)}, u32[]{:S(2)}) collective-permute-start(bf16[3104,128]{1,0:T(8,128)(2,1)S(1)} %collective-permute-done.4.refs_3_.refs_2_), channel_id=1, source_target_pairs={{0,1},{1,0},{2,3},{3,2},{4,5},{5,4},{6,7},{7,6},{8,9},{9,8},{10,11... | collective-permute-start | bytes 2383880 | tf_op jit(solution)/shard_map/ppermute | solution.py:322
  92.5 19.4 %collective-permute-start.9 = (bf16[3104,128]{1,0:T(8,128)(2,1)S(1)}, bf16[3104,128]{1,0:T(8,128)(2,1)}, u32[]{:S(2)}, u32[]{:S(2)}) collective-permute-start(bf16[3104,128]{1,0:T(8,128)(2,1)S(1)} %get-tuple-element.26.refs_1_.refs_0_), channel_id=1, source_target_pairs={{6,1},{3,0},{0,3},{5,2},{2,5},{7,4},{4,7},{1,6},{14,9},{11,8},{8,1... | collective-permute-start | bytes 2383880 | tf_op jit(solution)/shard_map/ppermute | solution.py:353
  95.1 21.3 %collective-permute-start.7 = (bf16[3104,128]{1,0:T(8,128)(2,1)S(1)}, bf16[3104,128]{1,0:T(8,128)(2,1)}, u32[]{:S(2)}, u32[]{:S(2)}) collective-permute-start(bf16[3104,128]{1,0:T(8,128)(2,1)S(1)} %get-tuple-element.26.refs_1_.refs_0_), channel_id=1, source_target_pairs={{6,0},{3,1},{0,2},{5,3},{2,4},{7,5},{4,6},{1,7},{14,8},{11,9},{8,1... | collective-permute-start | bytes 2383880 | tf_op jit(solution)/shard_map/ppermute | solution.py:352
  108.4 9.6 %copy-start = (f32[1024]{0:T(1024)S(1)}, f32[1024]{0:T(1024)}, u32[]{:S(2)}) copy-start(f32[1024]{0:T(1024)} %param.17) | copy-start | bytes 12292
  108.4 9.6 %copy-start.1 = (f32[1024]{0:T(1024)S(1)}, f32[1024]{0:T(1024)}, u32[]{:S(2)}) copy-start(f32[1024]{0:T(1024)} %param.18) | copy-start | bytes 12292
  108.4 9.6 %all-to-all-start.4 = ((bf16[8,32,256]{2,1,0:T(8,128)(2,1)}), bf16[8,32,256]{2,1,0:T(8,128)(2,1)S(1)}, u32[]{:S(2)}, u32[]{:S(2)}) async-start(bf16[8,32,256]{2,1,0:T(8,128)(2,1)} %bitcast.11), calls=%async_computation.4 | async-start | bytes 262144 | tf_op jit(solution)/shard_map/all_to_all | solution.py:326
  111.9 6.0 %copy-start.2 = (bf16[3104,128]{1,0:T(8,128)(2,1)}, bf16[3104,128]{1,0:T(8,128)(2,1)S(1)}, u32[]{:S(2)}) copy-start(bf16[3104,128]{1,0:T(8,128)(2,1)S(1)} %collective-permute-done.8.refs_7_.refs_6_) | copy-start | bytes 2383876
  120.9 9.8 %collective-permute-start.10 = (bf16[16,1024]{1,0:T(8,128)(2,1)S(1)}, bf16[16,1024]{1,0:T(8,128)(2,1)S(1)}, u32[]{:S(2)}, u32[]{:S(2)}) collective-permute-start(bf16[16,1024]{1,0:T(8,128)(2,1)S(1)} %get-tuple-element.33.refs_10_), channel_id=1, source_target_pairs={{0,1},{1,2},{2,3},{3,4},{4,5},{5,6},{6,7},{7,8},{8,9},{9,10},{10,1... | collective-permute-start | bytes 98312 | tf_op jit(solution)/shard_map/ppermute | solution.py:389
  122.8 9.4 %collective-permute-start.11 = (bf16[16,1024]{1,0:T(8,128)(2,1)S(1)}, bf16[16,1024]{1,0:T(8,128)(2,1)S(1)}, u32[]{:S(2)}, u32[]{:S(2)}) collective-permute-start(bf16[16,1024]{1,0:T(8,128)(2,1)S(1)} %get-tuple-element.34.refs_9_), channel_id=1, source_target_pairs={{1,0},{2,1},{3,2},{4,3},{5,4},{6,5},{7,6},{8,7},{9,8},{10,9},{11,1... | collective-permute-start | bytes 98312 | tf_op jit(solution)/shard_map/ppermute | solution.py:390

commit v7 on v6

--- a/solution.py
+++ b/solution.py
@@ -116,6 +116,23 @@
         copy.wait()
 
 
+def repeat_kernel(cells_ref, out_ref, sem):
+    for copy in fetched(
+        [
+            pltpu.make_async_copy(cells_ref, out_ref.at[q], sem.at[q])
+            for q in range(out_ref.shape[0])
+        ]
+    ):
+        copy.wait()
+
+
+def sum_kernel(parts_ref, out_ref):
+    total = parts_ref[0].astype(jnp.float32)
+    for q in range(1, parts_ref.shape[0]):
+        total = total + parts_ref[q].astype(jnp.float32)
+    out_ref[...] = total.astype(jnp.bfloat16)
+
+
 def expert_kernel(x_ref, *refs):
     sources, out_ref, held, sem = refs[:6], refs[6], refs[7:13], refs[13]
     copies = [pltpu.make_async_copy(s, h, sem.at[i]) for i, (s, h) in enumerate(zip(sources, held))]
@@ -150,7 +167,7 @@
 
 
 def order_of(count, near):
-    return [i for i in range(count) if i in near] + [i for i in range(count) if i not in near]
+    return [i for i in range(count) if i in near] + [i for i in range(count)[::-1] if i not in near]
 
 
 def fetched_rows(near, first, last, refs, held_ref, sem):
@@ -331,7 +348,16 @@
     arrived, *held = lax.optimization_barrier((arrived, *held))
     swapped = [across(cells) for cells in held]
     held.append(around(held[-1]))
-    x = over("y", jnp.broadcast_to(arrived, (quarters, rows, share)))
+    repeated = pl.pallas_call(
+        repeat_kernel,
+        in_specs=in_vmem(1),
+        out_specs=pl.BlockSpec(memory_space=pltpu.HBM),
+        out_shape=jax.ShapeDtypeStruct((quarters, rows, share), jnp.bfloat16),
+        scratch_shapes=[pltpu.SemaphoreType.DMA((quarters,))],
+        compiler_params=params,
+        name="repeat",
+    )(arrived.reshape(rows, share))
+    x = over("y", repeated)
     weights = mine + theirs
     partial = pl.pallas_call(
         expert_kernel,
@@ -344,7 +370,14 @@
         name="experts",
     )(x, *[far(w) for w in weights])
     partial = over("y", partial)
-    summed = jnp.sum(partial.astype(jnp.float32), axis=0).astype(jnp.bfloat16)
+    summed = pl.pallas_call(
+        sum_kernel,
+        in_specs=in_vmem(1),
+        out_specs=pl.BlockSpec(memory_space=pltpu.VMEM),
+        out_shape=jax.ShapeDtypeStruct((rows, share), jnp.bfloat16),
+        compiler_params=params,
+        name="sum_parts",
+    )(partial)
     summed, *held = lax.optimization_barrier((summed, *held, *swapped))
     held, swapped = held[: quarters - 1], held[quarters - 1 :]
     swapped.append(across(held[-1]))

time: 136 us -> 135 us (level)
  Pallas kernels: 14 us -> 15.8 us
    ppermute x1, waiting for transfers between devices: 4.48 us -> 0.01 us  [shards(): held.append(lax.ppermute(held[0], NARROW, back))]
    ppermute x1, waiting for transfers between devices: 0.01 us -> 2.78 us  [shards(): swapped.append(lax.ppermute(held[0], NARROW, [(a, b ^ 1) for a, b in back]))]
    pallas_call x0 -> x2, Pallas kernels: none -> 1.82 us  [the longest x1 1 us: shards(): pl.pallas_call(repeat_kernel, in_specs=in_vmem(1), out_specs=pl.BlockSpec...]
  transfers between devices with their start and end apart: 16 -> 16, of which waited for: 7 -> 7; matrix products, arithmetic and copies ran while one was open for 1% -> 0% of each run, Pallas kernels for 5% -> 6%
where the time goes in v7:
time: 135 us; the launch traced here: 134 us
  starting transfers between devices  74.3 us (55%)
  waiting for transfers between devices  30.8 us (23%)
  Pallas kernels  15.8 us (12%)
  blocking collectives  13.3 us (10%)
    all_to_all x4, starting transfers between devices, over(): return lax.all_to_all(cells, axis, split_axis=0, concat_axis=0, tiled=True)  36.3 us
    all_to_all x4, waiting for transfers between devices, over(): return lax.all_to_all(cells, axis, split_axis=0, concat_axis=0, tiled=True)  23.1 us
    all_to_all x1, blocking collectives, over(): return lax.all_to_all(cells, axis, split_axis=0, concat_axis=0, tiled=True)  13.3 us
    ppermute x6, starting transfers between devices, shards(): across = lambda cells: lax.ppermute(cells, 'c', swap)  12.5 us
    ppermute x2, starting transfers between devices, shards(): around = lambda cells: lax.ppermute(cells, NARROW, ring)  10.1 us
    ppermute x1, starting transfers between devices, shards(): right = lax.ppermute(lo, EVERY, [(i + 1, i) for i in range(ends)])  7.86 us
    pallas_call x1, Pallas kernels, shards(): pl.pallas_call(expert_kernel, in_specs=in_vmem(1) + in_hbm(6), out_specs=...  5.37 us
    ppermute x2, waiting for transfers between devices, shards(): around = lambda cells: lax.ppermute(cells, NARROW, ring)  3.3 us
  transfers between devices with their start and end apart: 16, of which 7 were waited for; matrix products, arithmetic and copies ran while one was open for 0% of the time, Pallas kernels for 6%

profile of v7, /device:TPU:6, one launch (start us, length us, event | category | flops | bytes accessed | tf_op | source)
XLA Modules:
  0.0 134.5 jit_solution(17883253795950291836)
XLA Ops:
  0.0 2.2 %prepare.1 = (bf16[512,256]{1,0:T(8,128)(2,1)}, f32[8,256]{1,0:T(8,128)S(1)}, bf16[3104,128]{1,0:T(8,128)(2,1)S(1)}) custom-call(s32[2,256]{1,0:T(2,128)} %bitcast.19, bf16[256,1024]{1,0:T(8,128)(2,1)} %refs_0_.1, bf16[2048,128]{1,0:T(8,128)(2,1)} %bitcast.18, bf16[31,128]{1,0:T(8,128)(2,1)} %refs_3_.1, bf16[128,1024]{1,0:T(8,128)(2,1)} %refs_4_.1, ...), custom_call_target="tpu_custom_call" | custom-call | tf_op jit(solution)/shard_map/prepare/pallas_call | solution.py:303
  2.2 18.8 %all-to-all-start = ((bf16[64,8,256]{2,1,0:T(8,128)(2,1)}), bf16[64,8,256]{2,1,0:T(8,128)(2,1)S(1)}, u32[]{:S(2)}, u32[]{:S(2)}) async-start(bf16[64,8,256]{2,1,0:T(8,128)(2,1)} %bitcast.3), calls=%async_computation | async-start | bytes 524288 | tf_op jit(solution)/shard_map/all_to_all | solution.py:343
  21.0 4.9 %collective-permute-start = (bf16[3104,128]{1,0:T(8,128)(2,1)S(1)}, bf16[3104,128]{1,0:T(8,128)(2,1)S(1)}, u32[]{:S(2)}, u32[]{:S(2)}) collective-permute-start(bf16[3104,128]{1,0:T(8,128)(2,1)S(1)} %get-tuple-element.26.refs_1_.refs_0_), channel_id=1, source_target_pairs={{0,6},{1,3},{2,0},{3,5},{4,2},{5,7},{6,4},{7,1},{8,14},{9,11},{10,... | collective-permute-start | bytes 2383880 | tf_op jit(solution)/shard_map/ppermute | solution.py:338
  26.0 1.9 %collective-permute-start.1 = (bf16[1024,512]{1,0:T(8,128)(2,1)}, bf16[1024,512]{1,0:T(8,128)(2,1)}, u32[]{:S(2)}, u32[]{:S(2)}) collective-permute-start(bf16[1024,512]{1,0:T(8,128)(2,1)} %bitcast.6.refs_0_), channel_id=1, source_target_pairs={{0,1},{1,0},{2,3},{3,2},{4,5},{5,4},{6,7},{7,6},{8,9},{9,8},{10,11... | collective-permute-start | bytes 3145736 | tf_op jit(solution)/shard_map/ppermute | solution.py:339
  27.9 2.4 %collective-permute-start.2 = (bf16[1024,512]{1,0:T(8,128)(2,1)}, bf16[1024,512]{1,0:T(8,128)(2,1)}, u32[]{:S(2)}, u32[]{:S(2)}) collective-permute-start(bf16[1024,512]{1,0:T(8,128)(2,1)} %bitcast.7.refs_1_), channel_id=1, source_target_pairs={{0,1},{1,0},{2,3},{3,2},{4,5},{5,4},{6,7},{7,6},{8,9},{9,8},{10,11... | collective-permute-start | bytes 3145736 | tf_op jit(solution)/shard_map/ppermute | solution.py:339
  30.3 1.9 %collective-permute-start.3 = (bf16[512,1024]{1,0:T(8,128)(2,1)}, bf16[512,1024]{1,0:T(8,128)(2,1)}, u32[]{:S(2)}, u32[]{:S(2)}) collective-permute-start(bf16[512,1024]{1,0:T(8,128)(2,1)} %bitcast.8.refs_2_), channel_id=1, source_target_pairs={{0,1},{1,0},{2,3},{3,2},{4,5},{5,4},{6,7},{7,6},{8,9},{9,8},{10,11... | collective-permute-start | bytes 3145736 | tf_op jit(solution)/shard_map/ppermute | solution.py:339
  32.2 3.3 %collective-permute-done.refs_2_.refs_1_ = bf16[3104,128]{1,0:T(8,128)(2,1)S(1)} collective-permute-done((bf16[3104,128]{1,0:T(8,128)(2,1)S(1)}, bf16[3104,128]{1,0:T(8,128)(2,1)S(1)}, u32[]{:S(2)}, u32[]{:S(2)}) %collective-permute-start) | collective-permute-done | bytes 794656 | tf_op jit(solution)/shard_map/ppermute | solution.py:338
  35.5 6.3 %all-to-all-done = bf16[64,8,256]{2,1,0:T(8,128)(2,1)S(1)} async-done(((bf16[64,8,256]{2,1,0:T(8,128)(2,1)}), bf16[64,8,256]{2,1,0:T(8,128)(2,1)S(1)}, u32[]{:S(2)}, u32[]{:S(2)}) %all-to-all-start) | async-done | bytes 262176 | tf_op jit(solution)/shard_map/all_to_all | solution.py:343
  41.8 1.0 repeat.1
  42.8 4.5 %all-to-all-start.1 = ((bf16[4,512,256]{2,1,0:T(8,128)(2,1)}), bf16[4,512,256]{2,1,0:T(8,128)(2,1)S(1)}, u32[]{:S(2)}, u32[]{:S(2)}) async-start(bf16[4,512,256]{2,1,0:T(8,128)(2,1)} %repeat.1), calls=%async_computation.1 | async-start | bytes 2097152 | tf_op jit(solution)/shard_map/all_to_all | solution.py:343
  47.3 1.9 %collective-permute-start.5 = (bf16[3104,128]{1,0:T(8,128)(2,1)S(1)}, bf16[3104,128]{1,0:T(8,128)(2,1)}, u32[]{:S(2)}, u32[]{:S(2)}) collective-permute-start(bf16[3104,128]{1,0:T(8,128)(2,1)S(1)} %get-tuple-element.26.refs_1_.refs_0_), channel_id=1, source_target_pairs={{0,1},{1,0},{2,3},{3,2},{4,5},{5,4},{6,7},{7,6},{8,9},{9,8},{10,11... | collective-permute-start | bytes 2383880 | tf_op jit(solution)/shard_map/ppermute | solution.py:339
  49.2 2.4 %collective-permute-start.6 = (bf16[3104,128]{1,0:T(8,128)(2,1)S(1)}, bf16[3104,128]{1,0:T(8,128)(2,1)}, u32[]{:S(2)}, u32[]{:S(2)}) collective-permute-start(bf16[3104,128]{1,0:T(8,128)(2,1)S(1)} %collective-permute-done.refs_2_.refs_1_), channel_id=1, source_target_pairs={{0,1},{1,0},{2,3},{3,2},{4,5},{5,4},{6,7},{7,6},{8,9},{9,8},{10,11... | collective-permute-start | bytes 2383880 | tf_op jit(solution)/shard_map/ppermute | solution.py:339
  51.6 0.0 collective-permute-done.1.refs_3_
  51.7 5.1 %collective-permute-start.4 = (bf16[3104,128]{1,0:T(8,128)(2,1)S(1)}, bf16[3104,128]{1,0:T(8,128)(2,1)S(1)}, u32[]{:S(2)}, u32[]{:S(2)}) collective-permute-start(bf16[3104,128]{1,0:T(8,128)(2,1)S(1)} %collective-permute-done.refs_2_.refs_1_), channel_id=1, source_target_pairs={{0,6},{1,3},{2,0},{3,5},{4,2},{5,7},{6,4},{7,1},{8,14},{9,11},{10,... | collective-permute-start | bytes 2383880 | tf_op jit(solution)/shard_map/ppermute | solution.py:338
  56.8 0.0 collective-permute-done.2.refs_4_
  56.8 0.0 collective-permute-done.3.refs_5_
  56.8 4.6 %all-to-all-done.1.x_ref = bf16[4,512,256]{2,1,0:T(8,128)(2,1)S(1)} async-done(((bf16[4,512,256]{2,1,0:T(8,128)(2,1)}), bf16[4,512,256]{2,1,0:T(8,128)(2,1)S(1)}, u32[]{:S(2)}, u32[]{:S(2)}) %all-to-all-start.1) | async-done | bytes 1048608 | tf_op jit(solution)/shard_map/all_to_all | solution.py:343
  61.4 5.4 %experts.1 = bf16[4,512,256]{2,1,0:T(8,128)(2,1)S(1)} custom-call(bf16[4,512,256]{2,1,0:T(8,128)(2,1)S(1)} %all-to-all-done.1.x_ref, bf16[1024,512]{1,0:T(8,128)(2,1)} %bitcast.6.refs_0_, bf16[1024,512]{1,0:T(8,128)(2,1)} %bitcast.7.refs_1_, bf16[512,1024]{1,0:T(8,128)(2,1)} %bitcast.8.refs_2_, bf16[1024,512]{1,0:T(8,128)(2,1)} %collective-permute-done.1.refs_3_, ...), custom_call_target="tpu_custom_call" | custom-call | tf_op jit(solution)/shard_map/experts/pallas_call | solution.py:362
  66.8 13.3 %all_to_all.25.parts_ref = bf16[4,512,256]{2,1,0:T(8,128)(2,1)S(1)} all-to-all(bf16[4,512,256]{2,1,0:T(8,128)(2,1)S(1)} %experts.1), channel_id=1, replica_groups=mesh['x'=4,'z'=16,'y'=4,'c'=2] {'y'}, dimensions={0} | all-to-all | bytes 2097152 | tf_op jit(solution)/shard_map/all_to_all | solution.py:343
  80.1 0.8 sum_parts.1
  81.0 0.0 collective-permute-done.5.refs_7_.refs_6_
  81.0 0.0 collective-permute-done.6.refs_6_.refs_5_
  81.0 0.0 collective-permute-done.4.refs_3_.refs_2_
  81.0 9.5 %all-to-all-start.3 = ((bf16[64,8,256]{2,1,0:T(8,128)(2,1)}), bf16[64,8,256]{2,1,0:T(8,128)(2,1)S(1)}, u32[]{:S(2)}, u32[]{:S(2)}) async-start(bf16[64,8,256]{2,1,0:T(8,128)(2,1)} %bitcast.9), calls=%async_computation.3 | async-start | bytes 524288 | tf_op jit(solution)/shard_map/all_to_all | solution.py:343
  90.5 1.9 %collective-permute-start.8 = (bf16[3104,128]{1,0:T(8,128)(2,1)S(1)}, bf16[3104,128]{1,0:T(8,128)(2,1)}, u32[]{:S(2)}, u32[]{:S(2)}) collective-permute-start(bf16[3104,128]{1,0:T(8,128)(2,1)S(1)} %collective-permute-done.4.refs_3_.refs_2_), channel_id=1, source_target_pairs={{0,1},{1,0},{2,3},{3,2},{4,5},{5,4},{6,7},{7,6},{8,9},{9,8},{10,11... | collective-permute-start | bytes 2383880 | tf_op jit(solution)/shard_map/ppermute | solution.py:339
  92.4 2.5 %collective-permute-start.9 = (bf16[3104,128]{1,0:T(8,128)(2,1)S(1)}, bf16[3104,128]{1,0:T(8,128)(2,1)}, u32[]{:S(2)}, u32[]{:S(2)}) collective-permute-start(bf16[3104,128]{1,0:T(8,128)(2,1)S(1)} %get-tuple-element.26.refs_1_.refs_0_), channel_id=1, source_target_pairs={{6,0},{3,1},{0,2},{5,3},{2,4},{7,5},{4,6},{1,7},{14,8},{11,9},{8,1... | collective-permute-start | bytes 2383880 | tf_op jit(solution)/shard_map/ppermute | solution.py:385
  94.9 3.2 %collective-permute-start.7 = (bf16[3104,128]{1,0:T(8,128)(2,1)S(1)}, bf16[3104,128]{1,0:T(8,128)(2,1)}, u32[]{:S(2)}, u32[]{:S(2)}) collective-permute-start(bf16[3104,128]{1,0:T(8,128)(2,1)S(1)} %get-tuple-element.26.refs_1_.refs_0_), channel_id=1, source_target_pairs={{6,1},{3,0},{0,3},{5,2},{2,5},{7,4},{4,7},{1,6},{14,9},{11,8},{8,1... | collective-permute-start | bytes 2383880 | tf_op jit(solution)/shard_map/ppermute | solution.py:386
  98.1 9.0 %all-to-all-done.3 = bf16[64,8,256]{2,1,0:T(8,128)(2,1)S(1)} async-done(((bf16[64,8,256]{2,1,0:T(8,128)(2,1)}), bf16[64,8,256]{2,1,0:T(8,128)(2,1)S(1)}, u32[]{:S(2)}, u32[]{:S(2)}) %all-to-all-start.3) | async-done | bytes 262176 | tf_op jit(solution)/shard_map/all_to_all | solution.py:343
  107.1 1.1 combine.1
  108.2 0.0 copy-start
  108.2 0.0 copy-start.1
  108.2 3.5 %all-to-all-start.4 = ((bf16[8,32,256]{2,1,0:T(8,128)(2,1)}), bf16[8,32,256]{2,1,0:T(8,128)(2,1)S(1)}, u32[]{:S(2)}, u32[]{:S(2)}) async-start(bf16[8,32,256]{2,1,0:T(8,128)(2,1)} %bitcast.11), calls=%async_computation.4 | async-start | bytes 262144 | tf_op jit(solution)/shard_map/all_to_all | solution.py:343
  111.7 0.0 collective-permute-done.8.refs_5_.refs_4_
  111.8 0.0 collective-permute-done.9.refs_8_.refs_7_
  111.8 2.8 %collective-permute-done.7.refs_4_.refs_3_ = bf16[3104,128]{1,0:T(8,128)(2,1)} collective-permute-done((bf16[3104,128]{1,0:T(8,128)(2,1)S(1)}, bf16[3104,128]{1,0:T(8,128)(2,1)}, u32[]{:S(2)}, u32[]{:S(2)}) %collective-permute-start.7) | collective-permute-done | bytes 794656 | tf_op jit(solution)/shard_map/ppermute | solution.py:386
  114.5 3.3 %all-to-all-done.4.refs_9_ = bf16[8,32,256]{2,1,0:T(8,128)(2,1)S(1)} async-done(((bf16[8,32,256]{2,1,0:T(8,128)(2,1)}), bf16[8,32,256]{2,1,0:T(8,128)(2,1)S(1)}, u32[]{:S(2)}, u32[]{:S(2)}) %all-to-all-start.4) | async-done | bytes 131104 | tf_op jit(solution)/shard_map/all_to_all | solution.py:343
  117.8 0.0 copy-done
  117.8 0.0 copy-done.1
  117.8 2.9 %norm_glu.1 = (f32[32,1024]{1,0:T(8,128)S(1)}, bf16[16,1024]{1,0:T(8,128)(2,1)S(1)}, bf16[16,1024]{1,0:T(8,128)(2,1)S(1)}, f32[32,1024]{1,0:T(8,128)S(1)}) custom-call(bf16[256,1024]{1,0:T(8,128)(2,1)} %refs_0_.1, bf16[3104,128]{1,0:T(8,128)(2,1)S(1)} %get-tuple-element.26.refs_1_.refs_0_, bf16[3104,128]{1,0:T(8,128)(2,1)S(1)} %collective-permute-done.refs_2_.refs_1_, ...), custom_call_target="tpu_custom_call" | custom-call | tf_op jit(solution)/shard_map/norm_glu/pallas_call | solution.py:402
  120.7 1.9 %collective-permute-start.10 = (bf16[16,1024]{1,0:T(8,128)(2,1)S(1)}, bf16[16,1024]{1,0:T(8,128)(2,1)S(1)}, u32[]{:S(2)}, u32[]{:S(2)}) collective-permute-start(bf16[16,1024]{1,0:T(8,128)(2,1)S(1)} %get-tuple-element.33.refs_10_), channel_id=1, source_target_pairs={{0,1},{1,2},{2,3},{3,4},{4,5},{5,6},{6,7},{7,8},{8,9},{9,10},{10,1... | collective-permute-start | bytes 98312 | tf_op jit(solution)/shard_map/ppermute | solution.py:422
  122.6 7.9 %collective-permute-start.11 = (bf16[16,1024]{1,0:T(8,128)(2,1)S(1)}, bf16[16,1024]{1,0:T(8,128)(2,1)S(1)}, u32[]{:S(2)}, u32[]{:S(2)}) collective-permute-start(bf16[16,1024]{1,0:T(8,128)(2,1)S(1)} %get-tuple-element.34.refs_9_), channel_id=1, source_target_pairs={{1,0},{2,1},{3,2},{4,3},{5,4},{6,5},{7,6},{8,7},{9,8},{10,9},{11,1... | collective-permute-start | bytes 98312 | tf_op jit(solution)/shard_map/ppermute | solution.py:423
  130.5 0.0 collective-permute-done.10.refs_8_
  130.5 1.6 %collective-permute-done.11.refs_11_ = bf16[16,1024]{1,0:T(8,128)(2,1)S(1)} collective-permute-done((bf16[16,1024]{1,0:T(8,128)(2,1)S(1)}, bf16[16,1024]{1,0:T(8,128)(2,1)S(1)}, u32[]{:S(2)}, u32[]{:S(2)}) %collective-permute-start.11) | collective-permute-done | bytes 32800 | tf_op jit(solution)/shard_map/ppermute | solution.py:423
  132.1 2.4 %conv.1 = bf16[32,1024]{1,0:T(8,128)(2,1)} custom-call(bf16[3104,128]{1,0:T(8,128)(2,1)S(1)} %get-tuple-element.26.refs_1_.refs_0_, bf16[3104,128]{1,0:T(8,128)(2,1)S(1)} %collective-permute-done.refs_2_.refs_1_, bf16[3104,128]{1,0:T(8,128)(2,1)S(1)} %collective-permute-done.4.refs_3_.refs_2_, bf16[3104,128]{1,0:T(8,128)(2,1)} %collective-permute-done.7.refs_4_.refs_3_, ...), custom_call_target="tpu_custom_call" | custom-call | tf_op jit(solution)/shard_map/conv/pallas_call | solution.py:424
Async XLA Ops:
  2.2 39.6 %all-to-all-start = ((bf16[64,8,256]{2,1,0:T(8,128)(2,1)}), bf16[64,8,256]{2,1,0:T(8,128)(2,1)S(1)}, u32[]{:S(2)}, u32[]{:S(2)}) async-start(bf16[64,8,256]{2,1,0:T(8,128)(2,1)} %bitcast.3), calls=%async_computation | async-start | bytes 524288 | tf_op jit(solution)/shard_map/all_to_all | solution.py:343
  21.0 14.5 %collective-permute-start = (bf16[3104,128]{1,0:T(8,128)(2,1)S(1)}, bf16[3104,128]{1,0:T(8,128)(2,1)S(1)}, u32[]{:S(2)}, u32[]{:S(2)}) collective-permute-start(bf16[3104,128]{1,0:T(8,128)(2,1)S(1)} %get-tuple-element.26.refs_1_.refs_0_), channel_id=1, source_target_pairs={{0,6},{1,3},{2,0},{3,5},{4,2},{5,7},{6,4},{7,1},{8,14},{9,11},{10,... | collective-permute-start | bytes 2383880 | tf_op jit(solution)/shard_map/ppermute | solution.py:338
  26.0 25.7 %collective-permute-start.1 = (bf16[1024,512]{1,0:T(8,128)(2,1)}, bf16[1024,512]{1,0:T(8,128)(2,1)}, u32[]{:S(2)}, u32[]{:S(2)}) collective-permute-start(bf16[1024,512]{1,0:T(8,128)(2,1)} %bitcast.6.refs_0_), channel_id=1, source_target_pairs={{0,1},{1,0},{2,3},{3,2},{4,5},{5,4},{6,7},{7,6},{8,9},{9,8},{10,11... | collective-permute-start | bytes 3145736 | tf_op jit(solution)/shard_map/ppermute | solution.py:339
  27.9 28.9 %collective-permute-start.2 = (bf16[1024,512]{1,0:T(8,128)(2,1)}, bf16[1024,512]{1,0:T(8,128)(2,1)}, u32[]{:S(2)}, u32[]{:S(2)}) collective-permute-start(bf16[1024,512]{1,0:T(8,128)(2,1)} %bitcast.7.refs_1_), channel_id=1, source_target_pairs={{0,1},{1,0},{2,3},{3,2},{4,5},{5,4},{6,7},{7,6},{8,9},{9,8},{10,11... | collective-permute-start | bytes 3145736 | tf_op jit(solution)/shard_map/ppermute | solution.py:339
  30.3 26.5 %collective-permute-start.3 = (bf16[512,1024]{1,0:T(8,128)(2,1)}, bf16[512,1024]{1,0:T(8,128)(2,1)}, u32[]{:S(2)}, u32[]{:S(2)}) collective-permute-start(bf16[512,1024]{1,0:T(8,128)(2,1)} %bitcast.8.refs_2_), channel_id=1, source_target_pairs={{0,1},{1,0},{2,3},{3,2},{4,5},{5,4},{6,7},{7,6},{8,9},{9,8},{10,11... | collective-permute-start | bytes 3145736 | tf_op jit(solution)/shard_map/ppermute | solution.py:339
  42.8 18.6 %all-to-all-start.1 = ((bf16[4,512,256]{2,1,0:T(8,128)(2,1)}), bf16[4,512,256]{2,1,0:T(8,128)(2,1)S(1)}, u32[]{:S(2)}, u32[]{:S(2)}) async-start(bf16[4,512,256]{2,1,0:T(8,128)(2,1)} %repeat.1), calls=%async_computation.1 | async-start | bytes 2097152 | tf_op jit(solution)/shard_map/all_to_all | solution.py:343
  47.3 33.6 %collective-permute-start.5 = (bf16[3104,128]{1,0:T(8,128)(2,1)S(1)}, bf16[3104,128]{1,0:T(8,128)(2,1)}, u32[]{:S(2)}, u32[]{:S(2)}) collective-permute-start(bf16[3104,128]{1,0:T(8,128)(2,1)S(1)} %get-tuple-element.26.refs_1_.refs_0_), channel_id=1, source_target_pairs={{0,1},{1,0},{2,3},{3,2},{4,5},{5,4},{6,7},{7,6},{8,9},{9,8},{10,11... | collective-permute-start | bytes 2383880 | tf_op jit(solution)/shard_map/ppermute | solution.py:339
  49.2 31.7 %collective-permute-start.6 = (bf16[3104,128]{1,0:T(8,128)(2,1)S(1)}, bf16[3104,128]{1,0:T(8,128)(2,1)}, u32[]{:S(2)}, u32[]{:S(2)}) collective-permute-start(bf16[3104,128]{1,0:T(8,128)(2,1)S(1)} %collective-permute-done.refs_2_.refs_1_), channel_id=1, source_target_pairs={{0,1},{1,0},{2,3},{3,2},{4,5},{5,4},{6,7},{7,6},{8,9},{9,8},{10,11... | collective-permute-start | bytes 2383880 | tf_op jit(solution)/shard_map/ppermute | solution.py:339
  51.7 29.3 %collective-permute-start.4 = (bf16[3104,128]{1,0:T(8,128)(2,1)S(1)}, bf16[3104,128]{1,0:T(8,128)(2,1)S(1)}, u32[]{:S(2)}, u32[]{:S(2)}) collective-permute-start(bf16[3104,128]{1,0:T(8,128)(2,1)S(1)} %collective-permute-done.refs_2_.refs_1_), channel_id=1, source_target_pairs={{0,6},{1,3},{2,0},{3,5},{4,2},{5,7},{6,4},{7,1},{8,14},{9,11},{10,... | collective-permute-start | bytes 2383880 | tf_op jit(solution)/shard_map/ppermute | solution.py:338
  81.0 26.1 %all-to-all-start.3 = ((bf16[64,8,256]{2,1,0:T(8,128)(2,1)}), bf16[64,8,256]{2,1,0:T(8,128)(2,1)S(1)}, u32[]{:S(2)}, u32[]{:S(2)}) async-start(bf16[64,8,256]{2,1,0:T(8,128)(2,1)} %bitcast.9), calls=%async_computation.3 | async-start | bytes 524288 | tf_op jit(solution)/shard_map/all_to_all | solution.py:343
  90.5 21.3 %collective-permute-start.8 = (bf16[3104,128]{1,0:T(8,128)(2,1)S(1)}, bf16[3104,128]{1,0:T(8,128)(2,1)}, u32[]{:S(2)}, u32[]{:S(2)}) collective-permute-start(bf16[3104,128]{1,0:T(8,128)(2,1)S(1)} %collective-permute-done.4.refs_3_.refs_2_), channel_id=1, source_target_pairs={{0,1},{1,0},{2,3},{3,2},{4,5},{5,4},{6,7},{7,6},{8,9},{9,8},{10,11... | collective-permute-start | bytes 2383880 | tf_op jit(solution)/shard_map/ppermute | solution.py:339
  92.4 19.3 %collective-permute-start.9 = (bf16[3104,128]{1,0:T(8,128)(2,1)S(1)}, bf16[3104,128]{1,0:T(8,128)(2,1)}, u32[]{:S(2)}, u32[]{:S(2)}) collective-permute-start(bf16[3104,128]{1,0:T(8,128)(2,1)S(1)} %get-tuple-element.26.refs_1_.refs_0_), channel_id=1, source_target_pairs={{6,0},{3,1},{0,2},{5,3},{2,4},{7,5},{4,6},{1,7},{14,8},{11,9},{8,1... | collective-permute-start | bytes 2383880 | tf_op jit(solution)/shard_map/ppermute | solution.py:385
  94.9 19.6 %collective-permute-start.7 = (bf16[3104,128]{1,0:T(8,128)(2,1)S(1)}, bf16[3104,128]{1,0:T(8,128)(2,1)}, u32[]{:S(2)}, u32[]{:S(2)}) collective-permute-start(bf16[3104,128]{1,0:T(8,128)(2,1)S(1)} %get-tuple-element.26.refs_1_.refs_0_), channel_id=1, source_target_pairs={{6,1},{3,0},{0,3},{5,2},{2,5},{7,4},{4,7},{1,6},{14,9},{11,8},{8,1... | collective-permute-start | bytes 2383880 | tf_op jit(solution)/shard_map/ppermute | solution.py:386
  108.2 9.6 %copy-start = (f32[1024]{0:T(1024)S(1)}, f32[1024]{0:T(1024)}, u32[]{:S(2)}) copy-start(f32[1024]{0:T(1024)} %param.17) | copy-start | bytes 12292
  108.2 9.6 %copy-start.1 = (f32[1024]{0:T(1024)S(1)}, f32[1024]{0:T(1024)}, u32[]{:S(2)}) copy-start(f32[1024]{0:T(1024)} %param.18) | copy-start | bytes 12292
  108.2 9.6 %all-to-all-start.4 = ((bf16[8,32,256]{2,1,0:T(8,128)(2,1)}), bf16[8,32,256]{2,1,0:T(8,128)(2,1)S(1)}, u32[]{:S(2)}, u32[]{:S(2)}) async-start(bf16[8,32,256]{2,1,0:T(8,128)(2,1)} %bitcast.11), calls=%async_computation.4 | async-start | bytes 262144 | tf_op jit(solution)/shard_map/all_to_all | solution.py:343
  120.7 9.8 %collective-permute-start.10 = (bf16[16,1024]{1,0:T(8,128)(2,1)S(1)}, bf16[16,1024]{1,0:T(8,128)(2,1)S(1)}, u32[]{:S(2)}, u32[]{:S(2)}) collective-permute-start(bf16[16,1024]{1,0:T(8,128)(2,1)S(1)} %get-tuple-element.33.refs_10_), channel_id=1, source_target_pairs={{0,1},{1,2},{2,3},{3,4},{4,5},{5,6},{6,7},{7,8},{8,9},{9,10},{10,1... | collective-permute-start | bytes 98312 | tf_op jit(solution)/shard_map/ppermute | solution.py:422
  122.6 9.4 %collective-permute-start.11 = (bf16[16,1024]{1,0:T(8,128)(2,1)S(1)}, bf16[16,1024]{1,0:T(8,128)(2,1)S(1)}, u32[]{:S(2)}, u32[]{:S(2)}) collective-permute-start(bf16[16,1024]{1,0:T(8,128)(2,1)S(1)} %get-tuple-element.34.refs_9_), channel_id=1, source_target_pairs={{1,0},{2,1},{3,2},{4,3},{5,4},{6,5},{7,6},{8,7},{9,8},{10,9},{11,1... | collective-permute-start | bytes 98312 | tf_op jit(solution)/shard_map/ppermute | solution.py:423

commit v8 on v7

--- a/solution.py
+++ b/solution.py
@@ -183,12 +183,12 @@
     count = table_ref.shape[1]
     table = table_ref[...].T
     slot = lax.broadcasted_iota(jnp.int32, (count, rows_ref.shape[0]), 1)
-    total = None
-    for k in range(2):
-        hit = slot == table[:, k : k + 1].astype(jnp.int32)
-        picked = mm(jnp.where(hit, 1.0, 0.0).astype(jnp.bfloat16), rows_ref[...])
-        picked = picked * table[:, 2 + k : 3 + k]
-        total = picked if total is None else total + picked
+    hits = [
+        jnp.where(slot == table[:, k : k + 1].astype(jnp.int32), 1.0, 0.0).astype(jnp.bfloat16)
+        for k in range(2)
+    ]
+    picked = mm(jnp.concatenate(hits, axis=0), rows_ref[...])
+    total = picked[:count] * table[:, 2:3] + picked[count:] * table[:, 3:4]
     out_ref[...] = total.astype(jnp.bfloat16)
 
 

time: 135 us -> 135 us (level)
  no operation moved by 1% of the time
where the time goes in v8:
time: 135 us; the launch traced here: 134 us
  starting transfers between devices  74.3 us (55%)
  waiting for transfers between devices  30.8 us (23%)
  Pallas kernels  15.8 us (12%)
  blocking collectives  13.3 us (10%)
    all_to_all x4, starting transfers between devices, over(): return lax.all_to_all(cells, axis, split_axis=0, concat_axis=0, tiled=True)  36.3 us
    all_to_all x4, waiting for transfers between devices, over(): return lax.all_to_all(cells, axis, split_axis=0, concat_axis=0, tiled=True)  23.1 us
    all_to_all x1, blocking collectives, over(): return lax.all_to_all(cells, axis, split_axis=0, concat_axis=0, tiled=True)  13.3 us
    ppermute x6, starting transfers between devices, shards(): across = lambda cells: lax.ppermute(cells, 'c', swap)  12.5 us
    ppermute x2, starting transfers between devices, shards(): around = lambda cells: lax.ppermute(cells, NARROW, ring)  10.1 us
    ppermute x1, starting transfers between devices, shards(): right = lax.ppermute(lo, EVERY, [(i + 1, i) for i in range(ends)])  7.86 us
    pallas_call x1, Pallas kernels, shards(): pl.pallas_call(expert_kernel, in_specs=in_vmem(1) + in_hbm(6), out_specs=...  5.37 us
    ppermute x2, waiting for transfers between devices, shards(): around = lambda cells: lax.ppermute(cells, NARROW, ring)  3.3 us
  transfers between devices with their start and end apart: 16, of which 7 were waited for; matrix products, arithmetic and copies ran while one was open for 0% of the time, Pallas kernels for 6%

profile of v8, /device:TPU:6, one launch (start us, length us, event | category | flops | bytes accessed | tf_op | source)
XLA Modules:
  0.0 134.4 jit_solution(11666349661589599573)
XLA Ops:
  0.0 2.2 %prepare.1 = (bf16[512,256]{1,0:T(8,128)(2,1)}, f32[8,256]{1,0:T(8,128)S(1)}, bf16[3104,128]{1,0:T(8,128)(2,1)S(1)}) custom-call(s32[2,256]{1,0:T(2,128)} %bitcast.19, bf16[256,1024]{1,0:T(8,128)(2,1)} %refs_0_.1, bf16[2048,128]{1,0:T(8,128)(2,1)} %bitcast.18, bf16[31,128]{1,0:T(8,128)(2,1)} %refs_3_.1, bf16[128,1024]{1,0:T(8,128)(2,1)} %refs_4_.1, ...), custom_call_target="tpu_custom_call" | custom-call | tf_op jit(solution)/shard_map/prepare/pallas_call | solution.py:303
  2.2 18.8 %all-to-all-start = ((bf16[64,8,256]{2,1,0:T(8,128)(2,1)}), bf16[64,8,256]{2,1,0:T(8,128)(2,1)S(1)}, u32[]{:S(2)}, u32[]{:S(2)}) async-start(bf16[64,8,256]{2,1,0:T(8,128)(2,1)} %bitcast.3), calls=%async_computation | async-start | bytes 524288 | tf_op jit(solution)/shard_map/all_to_all | solution.py:343
  21.0 4.9 %collective-permute-start = (bf16[3104,128]{1,0:T(8,128)(2,1)S(1)}, bf16[3104,128]{1,0:T(8,128)(2,1)S(1)}, u32[]{:S(2)}, u32[]{:S(2)}) collective-permute-start(bf16[3104,128]{1,0:T(8,128)(2,1)S(1)} %get-tuple-element.26.refs_1_.refs_0_), channel_id=1, source_target_pairs={{0,6},{1,3},{2,0},{3,5},{4,2},{5,7},{6,4},{7,1},{8,14},{9,11},{10,... | collective-permute-start | bytes 2383880 | tf_op jit(solution)/shard_map/ppermute | solution.py:338
  26.0 1.9 %collective-permute-start.1 = (bf16[1024,512]{1,0:T(8,128)(2,1)}, bf16[1024,512]{1,0:T(8,128)(2,1)}, u32[]{:S(2)}, u32[]{:S(2)}) collective-permute-start(bf16[1024,512]{1,0:T(8,128)(2,1)} %bitcast.6.refs_0_), channel_id=1, source_target_pairs={{0,1},{1,0},{2,3},{3,2},{4,5},{5,4},{6,7},{7,6},{8,9},{9,8},{10,11... | collective-permute-start | bytes 3145736 | tf_op jit(solution)/shard_map/ppermute | solution.py:339
  27.9 2.4 %collective-permute-start.2 = (bf16[1024,512]{1,0:T(8,128)(2,1)}, bf16[1024,512]{1,0:T(8,128)(2,1)}, u32[]{:S(2)}, u32[]{:S(2)}) collective-permute-start(bf16[1024,512]{1,0:T(8,128)(2,1)} %bitcast.7.refs_1_), channel_id=1, source_target_pairs={{0,1},{1,0},{2,3},{3,2},{4,5},{5,4},{6,7},{7,6},{8,9},{9,8},{10,11... | collective-permute-start | bytes 3145736 | tf_op jit(solution)/shard_map/ppermute | solution.py:339
  30.3 1.9 %collective-permute-start.3 = (bf16[512,1024]{1,0:T(8,128)(2,1)}, bf16[512,1024]{1,0:T(8,128)(2,1)}, u32[]{:S(2)}, u32[]{:S(2)}) collective-permute-start(bf16[512,1024]{1,0:T(8,128)(2,1)} %bitcast.8.refs_2_), channel_id=1, source_target_pairs={{0,1},{1,0},{2,3},{3,2},{4,5},{5,4},{6,7},{7,6},{8,9},{9,8},{10,11... | collective-permute-start | bytes 3145736 | tf_op jit(solution)/shard_map/ppermute | solution.py:339
  32.2 3.3 %collective-permute-done.refs_2_.refs_1_ = bf16[3104,128]{1,0:T(8,128)(2,1)S(1)} collective-permute-done((bf16[3104,128]{1,0:T(8,128)(2,1)S(1)}, bf16[3104,128]{1,0:T(8,128)(2,1)S(1)}, u32[]{:S(2)}, u32[]{:S(2)}) %collective-permute-start) | collective-permute-done | bytes 794656 | tf_op jit(solution)/shard_map/ppermute | solution.py:338
  35.5 6.3 %all-to-all-done = bf16[64,8,256]{2,1,0:T(8,128)(2,1)S(1)} async-done(((bf16[64,8,256]{2,1,0:T(8,128)(2,1)}), bf16[64,8,256]{2,1,0:T(8,128)(2,1)S(1)}, u32[]{:S(2)}, u32[]{:S(2)}) %all-to-all-start) | async-done | bytes 262176 | tf_op jit(solution)/shard_map/all_to_all | solution.py:343
  41.8 1.0 repeat.1
  42.8 4.5 %all-to-all-start.1 = ((bf16[4,512,256]{2,1,0:T(8,128)(2,1)}), bf16[4,512,256]{2,1,0:T(8,128)(2,1)S(1)}, u32[]{:S(2)}, u32[]{:S(2)}) async-start(bf16[4,512,256]{2,1,0:T(8,128)(2,1)} %repeat.1), calls=%async_computation.1 | async-start | bytes 2097152 | tf_op jit(solution)/shard_map/all_to_all | solution.py:343
  47.3 1.9 %collective-permute-start.5 = (bf16[3104,128]{1,0:T(8,128)(2,1)S(1)}, bf16[3104,128]{1,0:T(8,128)(2,1)}, u32[]{:S(2)}, u32[]{:S(2)}) collective-permute-start(bf16[3104,128]{1,0:T(8,128)(2,1)S(1)} %get-tuple-element.26.refs_1_.refs_0_), channel_id=1, source_target_pairs={{0,1},{1,0},{2,3},{3,2},{4,5},{5,4},{6,7},{7,6},{8,9},{9,8},{10,11... | collective-permute-start | bytes 2383880 | tf_op jit(solution)/shard_map/ppermute | solution.py:339
  49.2 2.4 %collective-permute-start.6 = (bf16[3104,128]{1,0:T(8,128)(2,1)S(1)}, bf16[3104,128]{1,0:T(8,128)(2,1)}, u32[]{:S(2)}, u32[]{:S(2)}) collective-permute-start(bf16[3104,128]{1,0:T(8,128)(2,1)S(1)} %collective-permute-done.refs_2_.refs_1_), channel_id=1, source_target_pairs={{0,1},{1,0},{2,3},{3,2},{4,5},{5,4},{6,7},{7,6},{8,9},{9,8},{10,11... | collective-permute-start | bytes 2383880 | tf_op jit(solution)/shard_map/ppermute | solution.py:339
  51.6 0.0 collective-permute-done.1.refs_3_
  51.7 5.1 %collective-permute-start.4 = (bf16[3104,128]{1,0:T(8,128)(2,1)S(1)}, bf16[3104,128]{1,0:T(8,128)(2,1)S(1)}, u32[]{:S(2)}, u32[]{:S(2)}) collective-permute-start(bf16[3104,128]{1,0:T(8,128)(2,1)S(1)} %collective-permute-done.refs_2_.refs_1_), channel_id=1, source_target_pairs={{0,6},{1,3},{2,0},{3,5},{4,2},{5,7},{6,4},{7,1},{8,14},{9,11},{10,... | collective-permute-start | bytes 2383880 | tf_op jit(solution)/shard_map/ppermute | solution.py:338
  56.8 0.0 collective-permute-done.2.refs_4_
  56.8 0.0 collective-permute-done.3.refs_5_
  56.8 4.6 %all-to-all-done.1.x_ref = bf16[4,512,256]{2,1,0:T(8,128)(2,1)S(1)} async-done(((bf16[4,512,256]{2,1,0:T(8,128)(2,1)}), bf16[4,512,256]{2,1,0:T(8,128)(2,1)S(1)}, u32[]{:S(2)}, u32[]{:S(2)}) %all-to-all-start.1) | async-done | bytes 1048608 | tf_op jit(solution)/shard_map/all_to_all | solution.py:343
  61.4 5.4 %experts.1 = bf16[4,512,256]{2,1,0:T(8,128)(2,1)S(1)} custom-call(bf16[4,512,256]{2,1,0:T(8,128)(2,1)S(1)} %all-to-all-done.1.x_ref, bf16[1024,512]{1,0:T(8,128)(2,1)} %bitcast.6.refs_0_, bf16[1024,512]{1,0:T(8,128)(2,1)} %bitcast.7.refs_1_, bf16[512,1024]{1,0:T(8,128)(2,1)} %bitcast.8.refs_2_, bf16[1024,512]{1,0:T(8,128)(2,1)} %collective-permute-done.1.refs_3_, ...), custom_call_target="tpu_custom_call" | custom-call | tf_op jit(solution)/shard_map/experts/pallas_call | solution.py:362
  66.8 13.3 %all_to_all.25.parts_ref = bf16[4,512,256]{2,1,0:T(8,128)(2,1)S(1)} all-to-all(bf16[4,512,256]{2,1,0:T(8,128)(2,1)S(1)} %experts.1), channel_id=1, replica_groups=mesh['x'=4,'z'=16,'y'=4,'c'=2] {'y'}, dimensions={0} | all-to-all | bytes 2097152 | tf_op jit(solution)/shard_map/all_to_all | solution.py:343
  80.1 0.8 sum_parts.1
  81.0 0.0 collective-permute-done.5.refs_7_.refs_6_
  81.0 0.0 collective-permute-done.6.refs_6_.refs_5_
  81.0 0.0 collective-permute-done.4.refs_3_.refs_2_
  81.0 9.5 %all-to-all-start.3 = ((bf16[64,8,256]{2,1,0:T(8,128)(2,1)}), bf16[64,8,256]{2,1,0:T(8,128)(2,1)S(1)}, u32[]{:S(2)}, u32[]{:S(2)}) async-start(bf16[64,8,256]{2,1,0:T(8,128)(2,1)} %bitcast.9), calls=%async_computation.3 | async-start | bytes 524288 | tf_op jit(solution)/shard_map/all_to_all | solution.py:343
  90.5 1.9 %collective-permute-start.8 = (bf16[3104,128]{1,0:T(8,128)(2,1)S(1)}, bf16[3104,128]{1,0:T(8,128)(2,1)}, u32[]{:S(2)}, u32[]{:S(2)}) collective-permute-start(bf16[3104,128]{1,0:T(8,128)(2,1)S(1)} %collective-permute-done.4.refs_3_.refs_2_), channel_id=1, source_target_pairs={{0,1},{1,0},{2,3},{3,2},{4,5},{5,4},{6,7},{7,6},{8,9},{9,8},{10,11... | collective-permute-start | bytes 2383880 | tf_op jit(solution)/shard_map/ppermute | solution.py:339
  92.4 2.5 %collective-permute-start.9 = (bf16[3104,128]{1,0:T(8,128)(2,1)S(1)}, bf16[3104,128]{1,0:T(8,128)(2,1)}, u32[]{:S(2)}, u32[]{:S(2)}) collective-permute-start(bf16[3104,128]{1,0:T(8,128)(2,1)S(1)} %get-tuple-element.26.refs_1_.refs_0_), channel_id=1, source_target_pairs={{6,0},{3,1},{0,2},{5,3},{2,4},{7,5},{4,6},{1,7},{14,8},{11,9},{8,1... | collective-permute-start | bytes 2383880 | tf_op jit(solution)/shard_map/ppermute | solution.py:385
  94.9 3.2 %collective-permute-start.7 = (bf16[3104,128]{1,0:T(8,128)(2,1)S(1)}, bf16[3104,128]{1,0:T(8,128)(2,1)}, u32[]{:S(2)}, u32[]{:S(2)}) collective-permute-start(bf16[3104,128]{1,0:T(8,128)(2,1)S(1)} %get-tuple-element.26.refs_1_.refs_0_), channel_id=1, source_target_pairs={{6,1},{3,0},{0,3},{5,2},{2,5},{7,4},{4,7},{1,6},{14,9},{11,8},{8,1... | collective-permute-start | bytes 2383880 | tf_op jit(solution)/shard_map/ppermute | solution.py:386
  98.1 9.0 %all-to-all-done.3 = bf16[64,8,256]{2,1,0:T(8,128)(2,1)S(1)} async-done(((bf16[64,8,256]{2,1,0:T(8,128)(2,1)}), bf16[64,8,256]{2,1,0:T(8,128)(2,1)S(1)}, u32[]{:S(2)}, u32[]{:S(2)}) %all-to-all-start.3) | async-done | bytes 262176 | tf_op jit(solution)/shard_map/all_to_all | solution.py:343
  107.1 1.1 combine.1
  108.2 0.0 copy-start
  108.2 0.0 copy-start.1
  108.2 3.5 %all-to-all-start.4 = ((bf16[8,32,256]{2,1,0:T(8,128)(2,1)}), bf16[8,32,256]{2,1,0:T(8,128)(2,1)S(1)}, u32[]{:S(2)}, u32[]{:S(2)}) async-start(bf16[8,32,256]{2,1,0:T(8,128)(2,1)} %bitcast.11), calls=%async_computation.4 | async-start | bytes 262144 | tf_op jit(solution)/shard_map/all_to_all | solution.py:343
  111.7 0.0 collective-permute-done.8.refs_5_.refs_4_
  111.7 0.0 collective-permute-done.9.refs_8_.refs_7_
  111.7 2.8 %collective-permute-done.7.refs_4_.refs_3_ = bf16[3104,128]{1,0:T(8,128)(2,1)} collective-permute-done((bf16[3104,128]{1,0:T(8,128)(2,1)S(1)}, bf16[3104,128]{1,0:T(8,128)(2,1)}, u32[]{:S(2)}, u32[]{:S(2)}) %collective-permute-start.7) | collective-permute-done | bytes 794656 | tf_op jit(solution)/shard_map/ppermute | solution.py:386
  114.5 3.2 %all-to-all-done.4.refs_9_ = bf16[8,32,256]{2,1,0:T(8,128)(2,1)S(1)} async-done(((bf16[8,32,256]{2,1,0:T(8,128)(2,1)}), bf16[8,32,256]{2,1,0:T(8,128)(2,1)S(1)}, u32[]{:S(2)}, u32[]{:S(2)}) %all-to-all-start.4) | async-done | bytes 131104 | tf_op jit(solution)/shard_map/all_to_all | solution.py:343
  117.7 0.0 copy-done
  117.7 0.0 copy-done.1
  117.8 2.9 %norm_glu.1 = (f32[32,1024]{1,0:T(8,128)S(1)}, bf16[16,1024]{1,0:T(8,128)(2,1)S(1)}, bf16[16,1024]{1,0:T(8,128)(2,1)S(1)}, f32[32,1024]{1,0:T(8,128)S(1)}) custom-call(bf16[256,1024]{1,0:T(8,128)(2,1)} %refs_0_.1, bf16[3104,128]{1,0:T(8,128)(2,1)S(1)} %get-tuple-element.26.refs_1_.refs_0_, bf16[3104,128]{1,0:T(8,128)(2,1)S(1)} %collective-permute-done.refs_2_.refs_1_, ...), custom_call_target="tpu_custom_call" | custom-call | tf_op jit(solution)/shard_map/norm_glu/pallas_call | solution.py:402
  120.6 1.9 %collective-permute-start.10 = (bf16[16,1024]{1,0:T(8,128)(2,1)S(1)}, bf16[16,1024]{1,0:T(8,128)(2,1)S(1)}, u32[]{:S(2)}, u32[]{:S(2)}) collective-permute-start(bf16[16,1024]{1,0:T(8,128)(2,1)S(1)} %get-tuple-element.33.refs_10_), channel_id=1, source_target_pairs={{0,1},{1,2},{2,3},{3,4},{4,5},{5,6},{6,7},{7,8},{8,9},{9,10},{10,1... | collective-permute-start | bytes 98312 | tf_op jit(solution)/shard_map/ppermute | solution.py:422
  122.6 7.9 %collective-permute-start.11 = (bf16[16,1024]{1,0:T(8,128)(2,1)S(1)}, bf16[16,1024]{1,0:T(8,128)(2,1)S(1)}, u32[]{:S(2)}, u32[]{:S(2)}) collective-permute-start(bf16[16,1024]{1,0:T(8,128)(2,1)S(1)} %get-tuple-element.34.refs_9_), channel_id=1, source_target_pairs={{1,0},{2,1},{3,2},{4,3},{5,4},{6,5},{7,6},{8,7},{9,8},{10,9},{11,1... | collective-permute-start | bytes 98312 | tf_op jit(solution)/shard_map/ppermute | solution.py:423
  130.4 0.0 collective-permute-done.10.refs_8_
  130.4 1.6 %collective-permute-done.11.refs_11_ = bf16[16,1024]{1,0:T(8,128)(2,1)S(1)} collective-permute-done((bf16[16,1024]{1,0:T(8,128)(2,1)S(1)}, bf16[16,1024]{1,0:T(8,128)(2,1)S(1)}, u32[]{:S(2)}, u32[]{:S(2)}) %collective-permute-start.11) | collective-permute-done | bytes 32800 | tf_op jit(solution)/shard_map/ppermute | solution.py:423
  132.0 2.4 %conv.1 = bf16[32,1024]{1,0:T(8,128)(2,1)} custom-call(bf16[3104,128]{1,0:T(8,128)(2,1)S(1)} %get-tuple-element.26.refs_1_.refs_0_, bf16[3104,128]{1,0:T(8,128)(2,1)S(1)} %collective-permute-done.refs_2_.refs_1_, bf16[3104,128]{1,0:T(8,128)(2,1)S(1)} %collective-permute-done.4.refs_3_.refs_2_, bf16[3104,128]{1,0:T(8,128)(2,1)} %collective-permute-done.7.refs_4_.refs_3_, ...), custom_call_target="tpu_custom_call" | custom-call | tf_op jit(solution)/shard_map/conv/pallas_call | solution.py:424
Async XLA Ops:
  2.2 39.6 %all-to-all-start = ((bf16[64,8,256]{2,1,0:T(8,128)(2,1)}), bf16[64,8,256]{2,1,0:T(8,128)(2,1)S(1)}, u32[]{:S(2)}, u32[]{:S(2)}) async-start(bf16[64,8,256]{2,1,0:T(8,128)(2,1)} %bitcast.3), calls=%async_computation | async-start | bytes 524288 | tf_op jit(solution)/shard_map/all_to_all | solution.py:343
  21.0 14.5 %collective-permute-start = (bf16[3104,128]{1,0:T(8,128)(2,1)S(1)}, bf16[3104,128]{1,0:T(8,128)(2,1)S(1)}, u32[]{:S(2)}, u32[]{:S(2)}) collective-permute-start(bf16[3104,128]{1,0:T(8,128)(2,1)S(1)} %get-tuple-element.26.refs_1_.refs_0_), channel_id=1, source_target_pairs={{0,6},{1,3},{2,0},{3,5},{4,2},{5,7},{6,4},{7,1},{8,14},{9,11},{10,... | collective-permute-start | bytes 2383880 | tf_op jit(solution)/shard_map/ppermute | solution.py:338
  26.0 25.7 %collective-permute-start.1 = (bf16[1024,512]{1,0:T(8,128)(2,1)}, bf16[1024,512]{1,0:T(8,128)(2,1)}, u32[]{:S(2)}, u32[]{:S(2)}) collective-permute-start(bf16[1024,512]{1,0:T(8,128)(2,1)} %bitcast.6.refs_0_), channel_id=1, source_target_pairs={{0,1},{1,0},{2,3},{3,2},{4,5},{5,4},{6,7},{7,6},{8,9},{9,8},{10,11... | collective-permute-start | bytes 3145736 | tf_op jit(solution)/shard_map/ppermute | solution.py:339
  27.9 28.9 %collective-permute-start.2 = (bf16[1024,512]{1,0:T(8,128)(2,1)}, bf16[1024,512]{1,0:T(8,128)(2,1)}, u32[]{:S(2)}, u32[]{:S(2)}) collective-permute-start(bf16[1024,512]{1,0:T(8,128)(2,1)} %bitcast.7.refs_1_), channel_id=1, source_target_pairs={{0,1},{1,0},{2,3},{3,2},{4,5},{5,4},{6,7},{7,6},{8,9},{9,8},{10,11... | collective-permute-start | bytes 3145736 | tf_op jit(solution)/shard_map/ppermute | solution.py:339
  30.3 26.5 %collective-permute-start.3 = (bf16[512,1024]{1,0:T(8,128)(2,1)}, bf16[512,1024]{1,0:T(8,128)(2,1)}, u32[]{:S(2)}, u32[]{:S(2)}) collective-permute-start(bf16[512,1024]{1,0:T(8,128)(2,1)} %bitcast.8.refs_2_), channel_id=1, source_target_pairs={{0,1},{1,0},{2,3},{3,2},{4,5},{5,4},{6,7},{7,6},{8,9},{9,8},{10,11... | collective-permute-start | bytes 3145736 | tf_op jit(solution)/shard_map/ppermute | solution.py:339
  42.8 18.6 %all-to-all-start.1 = ((bf16[4,512,256]{2,1,0:T(8,128)(2,1)}), bf16[4,512,256]{2,1,0:T(8,128)(2,1)S(1)}, u32[]{:S(2)}, u32[]{:S(2)}) async-start(bf16[4,512,256]{2,1,0:T(8,128)(2,1)} %repeat.1), calls=%async_computation.1 | async-start | bytes 2097152 | tf_op jit(solution)/shard_map/all_to_all | solution.py:343
  47.3 33.6 %collective-permute-start.5 = (bf16[3104,128]{1,0:T(8,128)(2,1)S(1)}, bf16[3104,128]{1,0:T(8,128)(2,1)}, u32[]{:S(2)}, u32[]{:S(2)}) collective-permute-start(bf16[3104,128]{1,0:T(8,128)(2,1)S(1)} %get-tuple-element.26.refs_1_.refs_0_), channel_id=1, source_target_pairs={{0,1},{1,0},{2,3},{3,2},{4,5},{5,4},{6,7},{7,6},{8,9},{9,8},{10,11... | collective-permute-start | bytes 2383880 | tf_op jit(solution)/shard_map/ppermute | solution.py:339
  49.2 31.7 %collective-permute-start.6 = (bf16[3104,128]{1,0:T(8,128)(2,1)S(1)}, bf16[3104,128]{1,0:T(8,128)(2,1)}, u32[]{:S(2)}, u32[]{:S(2)}) collective-permute-start(bf16[3104,128]{1,0:T(8,128)(2,1)S(1)} %collective-permute-done.refs_2_.refs_1_), channel_id=1, source_target_pairs={{0,1},{1,0},{2,3},{3,2},{4,5},{5,4},{6,7},{7,6},{8,9},{9,8},{10,11... | collective-permute-start | bytes 2383880 | tf_op jit(solution)/shard_map/ppermute | solution.py:339
  51.7 29.3 %collective-permute-start.4 = (bf16[3104,128]{1,0:T(8,128)(2,1)S(1)}, bf16[3104,128]{1,0:T(8,128)(2,1)S(1)}, u32[]{:S(2)}, u32[]{:S(2)}) collective-permute-start(bf16[3104,128]{1,0:T(8,128)(2,1)S(1)} %collective-permute-done.refs_2_.refs_1_), channel_id=1, source_target_pairs={{0,6},{1,3},{2,0},{3,5},{4,2},{5,7},{6,4},{7,1},{8,14},{9,11},{10,... | collective-permute-start | bytes 2383880 | tf_op jit(solution)/shard_map/ppermute | solution.py:338
  81.0 26.1 %all-to-all-start.3 = ((bf16[64,8,256]{2,1,0:T(8,128)(2,1)}), bf16[64,8,256]{2,1,0:T(8,128)(2,1)S(1)}, u32[]{:S(2)}, u32[]{:S(2)}) async-start(bf16[64,8,256]{2,1,0:T(8,128)(2,1)} %bitcast.9), calls=%async_computation.3 | async-start | bytes 524288 | tf_op jit(solution)/shard_map/all_to_all | solution.py:343
  90.5 21.2 %collective-permute-start.8 = (bf16[3104,128]{1,0:T(8,128)(2,1)S(1)}, bf16[3104,128]{1,0:T(8,128)(2,1)}, u32[]{:S(2)}, u32[]{:S(2)}) collective-permute-start(bf16[3104,128]{1,0:T(8,128)(2,1)S(1)} %collective-permute-done.4.refs_3_.refs_2_), channel_id=1, source_target_pairs={{0,1},{1,0},{2,3},{3,2},{4,5},{5,4},{6,7},{7,6},{8,9},{9,8},{10,11... | collective-permute-start | bytes 2383880 | tf_op jit(solution)/shard_map/ppermute | solution.py:339
  92.4 19.3 %collective-permute-start.9 = (bf16[3104,128]{1,0:T(8,128)(2,1)S(1)}, bf16[3104,128]{1,0:T(8,128)(2,1)}, u32[]{:S(2)}, u32[]{:S(2)}) collective-permute-start(bf16[3104,128]{1,0:T(8,128)(2,1)S(1)} %get-tuple-element.26.refs_1_.refs_0_), channel_id=1, source_target_pairs={{6,0},{3,1},{0,2},{5,3},{2,4},{7,5},{4,6},{1,7},{14,8},{11,9},{8,1... | collective-permute-start | bytes 2383880 | tf_op jit(solution)/shard_map/ppermute | solution.py:385
  94.9 19.6 %collective-permute-start.7 = (bf16[3104,128]{1,0:T(8,128)(2,1)S(1)}, bf16[3104,128]{1,0:T(8,128)(2,1)}, u32[]{:S(2)}, u32[]{:S(2)}) collective-permute-start(bf16[3104,128]{1,0:T(8,128)(2,1)S(1)} %get-tuple-element.26.refs_1_.refs_0_), channel_id=1, source_target_pairs={{6,1},{3,0},{0,3},{5,2},{2,5},{7,4},{4,7},{1,6},{14,9},{11,8},{8,1... | collective-permute-start | bytes 2383880 | tf_op jit(solution)/shard_map/ppermute | solution.py:386
  108.2 9.6 %copy-start = (f32[1024]{0:T(1024)S(1)}, f32[1024]{0:T(1024)}, u32[]{:S(2)}) copy-start(f32[1024]{0:T(1024)} %param.17) | copy-start | bytes 12292
  108.2 9.6 %copy-start.1 = (f32[1024]{0:T(1024)S(1)}, f32[1024]{0:T(1024)}, u32[]{:S(2)}) copy-start(f32[1024]{0:T(1024)} %param.18) | copy-start | bytes 12292
  108.2 9.6 %all-to-all-start.4 = ((bf16[8,32,256]{2,1,0:T(8,128)(2,1)}), bf16[8,32,256]{2,1,0:T(8,128)(2,1)S(1)}, u32[]{:S(2)}, u32[]{:S(2)}) async-start(bf16[8,32,256]{2,1,0:T(8,128)(2,1)} %bitcast.11), calls=%async_computation.4 | async-start | bytes 262144 | tf_op jit(solution)/shard_map/all_to_all | solution.py:343
  120.6 9.8 %collective-permute-start.10 = (bf16[16,1024]{1,0:T(8,128)(2,1)S(1)}, bf16[16,1024]{1,0:T(8,128)(2,1)S(1)}, u32[]{:S(2)}, u32[]{:S(2)}) collective-permute-start(bf16[16,1024]{1,0:T(8,128)(2,1)S(1)} %get-tuple-element.33.refs_10_), channel_id=1, source_target_pairs={{0,1},{1,2},{2,3},{3,4},{4,5},{5,6},{6,7},{7,8},{8,9},{9,10},{10,1... | collective-permute-start | bytes 98312 | tf_op jit(solution)/shard_map/ppermute | solution.py:422
  122.6 9.4 %collective-permute-start.11 = (bf16[16,1024]{1,0:T(8,128)(2,1)S(1)}, bf16[16,1024]{1,0:T(8,128)(2,1)S(1)}, u32[]{:S(2)}, u32[]{:S(2)}) collective-permute-start(bf16[16,1024]{1,0:T(8,128)(2,1)S(1)} %get-tuple-element.34.refs_9_), channel_id=1, source_target_pairs={{1,0},{2,1},{3,2},{4,3},{5,4},{6,5},{7,6},{8,7},{9,8},{10,9},{11,1... | collective-permute-start | bytes 98312 | tf_op jit(solution)/shard_map/ppermute | solution.py:423
